TPU v7x, 32 devices: a whole 2x2x4 slice. The times are simulated.
32 devices in a mesh: dp: 8 (over z, y), mp: 4 (over x, core).
Axes of the slice: x: 2, y: 2, z: 4, core: 2. Of those that a mesh axis runs over, the one named last changes fastest.
Arguments:
- tokens: bfloat16 [16384, 768], P(('dp', 'mp')), may hold values from -6 to 6
- w_query: bfloat16 [768, 768], P('dp', 'mp'), may hold values from -0.109375 to 0.109375
- w_key: bfloat16 [768, 768], P('dp', 'mp'), may hold values from -0.109375 to 0.109375
- w_value: bfloat16 [768, 768], P('dp', 'mp'), may hold values from -0.21875 to 0.21875
- w_out: bfloat16 [768, 768], P('dp', 'mp'), may hold values from -0.625 to 0.625
- w_gate: bfloat16 [768, 2048], P('dp', 'mp'), may hold values from -0.21875 to 0.21875
- w_up: bfloat16 [768, 2048], P('dp', 'mp'), may hold values from -0.21875 to 0.21875
- w_down: bfloat16 [768, 2048], P('dp', 'mp'), may hold values from -0.125 to 0.125
- norm_attn: float32 [768], replicated, may hold values from 0.5 to 1.5
- norm_mlp: float32 [768], replicated, may hold values from 0.5 to 1.5
- valid_counts: int32 [8], P('dp'), may hold values from 512 to 2048
- group_ids: int32 [8, 2048], P('dp'), may hold values from 0 to 3, never falling along the last dimension, each value on 1 to 1024 neighbouring positions
- cotangent: bfloat16 [16384, 768], P(('dp', 'mp')), may hold values from -6 to 6
Outputs:
- output: bfloat16 [16384, 768], P(('dp', 'mp'))
- grad_tokens: bfloat16 [16384, 768], P(('dp', 'mp'))
- grad_query: float32 [768, 768], P('dp', 'mp')
- grad_key: float32 [768, 768], P('dp', 'mp')
- grad_value: float32 [768, 768], P('dp', 'mp')
- grad_out: float32 [768, 768], P('dp', 'mp')
- grad_gate: float32 [768, 2048], P('dp', 'mp')
- grad_up: float32 [768, 2048], P('dp', 'mp')
- grad_down: float32 [768, 2048], P('dp', 'mp')
- grad_norm_attn: float32 [768], replicated
- grad_norm_mlp: float32 [768], replicated
Inputs may be any that keep to these rules, and one draw needn't show every extreme that they name: `group_ids`: in each image the ids never fall, start at 0 and reach 3; each group has 1 to 1024 patches.
All inputs are finite; a program needn't handle non-finite values.
Results may differ from a plain program's by a relative error of at most 0.02.
Values may be sent and summed in bfloat16 or wider, within the bound.
No kernel may reach another device: no remote copies, remote signals or barrier semaphores. Data moves between devices by JAX's collectives and lax.ppermute only.
A program may use at most 128 MiB of HBM per device.

v0:
```python
import functools

import jax
import jax.numpy as jnp
from jax import lax
from jax.experimental import pallas as pl
from jax.experimental.pallas import tpu as pltpu
from jax.sharding import PartitionSpec as P

HEAD = 64
BLK = 256
DIRECT = 8
FOLD = 32
EXTRA = 8
ROOT = 0.7978845608028654
eps_norm = 1e-06
neg_large = -1e30
F32 = jnp.float32
BF16 = jnp.bfloat16


def nn(a, b):
    return lax.dot_general(a, b, (((1,), (0,)), ((), ())), preferred_element_type=F32)


def nt(a, b):
    return lax.dot_general(a, b, (((1,), (1,)), ((), ())), preferred_element_type=F32)


def tn(a, b):
    return lax.dot_general(a, b, (((0,), (0,)), ((), ())), preferred_element_type=F32)


def shape(dims, kind):
    return jax.ShapeDtypeStruct(dims, kind)


def whole(dims):
    return pl.BlockSpec(dims, lambda *_: (0,) * len(dims))


SMEM = pl.BlockSpec(memory_space=pltpu.SMEM)
VMEM = pl.BlockSpec(memory_space=pltpu.VMEM)
HBM = pl.BlockSpec(memory_space=pltpu.HBM)
ANY = pl.BlockSpec(memory_space=pl.ANY)


def room(mib):
    return pltpu.CompilerParams(vmem_limit_bytes=mib << 20)


def qkv_kernel(pieces, sc, t0, t1, t2, t3, gain, *rest):
    w_refs, (n1_o, qkvt_o, kn_o, vn_o, wt_o, wo_o, xs, ws) = rest[:pieces], rest[pieces:]
    step = pl.program_id(0)
    cols = kn_o.shape[1]

    @pl.when(step == 0)
    def _():
        if pieces == 1:
            ws[...] = w_refs[0][...]
        else:
            depth = w_refs[0].shape[0]
            for j in range(pieces):
                at = pl.multiple_of((sc[1] ^ j) * depth, 16)
                ws[pl.ds(at, depth), :] = w_refs[j][...]
        turned = ws[...].T
        wt_o[...] = turned[: 3 * cols, :]
        wo_o[...] = turned[3 * cols :, :]

    for j, ref in enumerate((t0, t1, t2, t3)):

        @pl.when(step == j)
        def _(ref=ref):
            xs[...] = ref[...]

    x = xs[...].astype(F32)
    scale = lax.rsqrt(jnp.mean(x * x, axis=-1, keepdims=True) + eps_norm)
    n1 = (x * scale * gain[...]).astype(BF16)
    n1_o[...] = n1
    qkvt_o[...] = nt(wt_o[...], n1).astype(BF16)
    kn_o[...] = nn(n1, ws[:, 0:cols]).astype(BF16)
    vn_o[...] = nn(n1, ws[:, 2 * cols : 3 * cols]).astype(BF16)


def qkv(sc, shards, gain, pieces, cols):
    rows, width = shards[0].shape
    total = rows * len(shards)
    return pl.pallas_call(
        functools.partial(qkv_kernel, len(pieces)),
        grid=(len(shards),),
        in_specs=[SMEM]
        + [whole((rows, width))] * 4
        + [whole((1, width))]
        + [whole(p.shape) for p in pieces],
        out_specs=[
            pl.BlockSpec((rows, width), lambda i: (i, 0)),
            pl.BlockSpec((3 * cols, rows), lambda i: (0, i)),
            pl.BlockSpec((rows, cols), lambda i: (i, 0)),
            pl.BlockSpec((rows, cols), lambda i: (i, 0)),
            whole((3 * cols, width)),
            whole((cols, width)),
        ],
        out_shape=[
            shape((total, width), BF16),
            shape((3 * cols, total), BF16),
            shape((total, cols), BF16),
            shape((total, cols), BF16),
            shape((3 * cols, width), BF16),
            shape((cols, width), BF16),
        ],
        scratch_shapes=[pltpu.VMEM((rows, width), BF16), pltpu.VMEM((width, 4 * cols), BF16)],
        name="qkv",
        cost_estimate=cost(0.01),
    )(sc, *shards, gain, *pieces)


def spread(rows, z_ref):
    heads = rows.shape[0] // HEAD
    z_ref[...] = jnp.zeros(z_ref.shape, z_ref.dtype)
    for h in range(heads):
        z_ref[h, h * HEAD : (h + 1) * HEAD, :] = rows[h * HEAD : (h + 1) * HEAD, :]


def cost(us):
    return pl.CostEstimate(flops=int(us * 1e9), transcendentals=0, bytes_accessed=1024)


def span(sc, half, per, blocks):
    me = sc[0]
    stored = half * blocks + pl.program_id(0)
    shard = (stored // per) ^ me
    place = shard * per + lax.rem(stored, per)
    low, high = sc[8 + place] // per, (sc[16 + place] + per - 1) // per
    has_own = jnp.logical_and(low <= shard, shard < high)
    count = jnp.maximum(high - low, 0) - has_own.astype(jnp.int32)

    def at(t):
        other = low + t - 1
        other = jnp.where(t == 0, shard, other + (other >= shard).astype(jnp.int32))
        return other, other ^ me

    return place, count + 1, at


def allowed(gkv, queries, place, shard, size, own=True):
    keys = gkv[pl.ds(pl.multiple_of(shard * size, size), size), :]
    mask = jnp.concatenate([keys] * (BLK // 128), axis=1) == queries
    if not own:
        return mask
    key_at = lax.broadcasted_iota(jnp.int32, mask.shape, 0)
    query_at = lax.broadcasted_iota(jnp.int32, mask.shape, 1) + (place * BLK - shard * size)
    return mask | (key_at == query_at)


def forward_kernel(half, per, sc, qt, kn, vt, gq, gkv, ot, lse, zq):
    heads = qt.shape[0] // HEAD
    size = per * BLK
    place, count, at = span(sc, half, per, pl.num_programs(0))
    spread(qt, zq)
    queries = gq[:, pl.ds(pl.multiple_of(place * BLK, BLK), BLK)]

    def scores(t, own):
        shard, stored = at(t)
        mask = allowed(gkv, queries, place, shard, size, own)
        where = pl.ds(pl.multiple_of(stored * size, size), size)
        keys = kn[where, :]
        return where, [jnp.where(mask, nn(keys, zq[h]), neg_large) for h in range(heads)]

    def mixed(h, where, p):
        return nn(vt[h * HEAD : (h + 1) * HEAD, where], p.astype(BF16))

    carry = []
    where, first = scores(0, True)
    for h, s in enumerate(first):
        top = jnp.max(s, axis=0, keepdims=True)
        p = jnp.exp(s - top)
        carry.append((top, jnp.sum(p, axis=0, keepdims=True), mixed(h, where, p)))

    def body(t, carry):
        where, more = scores(t, False)
        out = []
        for h, s in enumerate(more):
            top, total, acc = carry[h]
            higher = jnp.maximum(top, jnp.max(s, axis=0, keepdims=True))
            p = jnp.exp(s - higher)
            fade = jnp.exp(top - higher)
            out.append(
                (
                    higher,
                    fade * total + jnp.sum(p, axis=0, keepdims=True),
                    fade * acc + mixed(h, where, p),
                )
            )
        return tuple(out)

    carry = lax.fori_loop(1, count, body, tuple(carry))
    for h, (top, total, acc) in enumerate(carry):
        ot[h * HEAD : (h + 1) * HEAD, :] = (acc / total).astype(BF16)
        lse[h : h + 1, :] = top + jnp.log(total)


def attention(half, sc, qkvt, kn, gq, gkv):
    cols3, total = qkvt.shape
    cols = cols3 // 3
    blocks = total // BLK // 2
    per = total // 4 // BLK
    return pl.pallas_call(
        functools.partial(forward_kernel, half, per),
        grid=(blocks,),
        in_specs=[
            SMEM,
            pl.BlockSpec((cols, BLK), lambda i: (1, half * blocks + i)),
            whole((total, cols)),
            pl.BlockSpec((cols, total), lambda i: (2, 0)),
            whole((1, total)),
            whole((total, 128)),
        ],
        out_specs=[
            pl.BlockSpec((cols, BLK), lambda i: (0, i)),
            pl.BlockSpec((8, BLK), lambda i: (0, i)),
        ],
        out_shape=[shape((cols, blocks * BLK), BF16), shape((8, blocks * BLK), F32)],
        scratch_shapes=[pltpu.VMEM((cols // HEAD, cols, BLK), BF16)],
        compiler_params=room(32),
        name="attention",
        cost_estimate=cost(12),
    )(sc, qkvt, kn, qkvt, gq, gkv)


def backward_block(
    half, per, sc, qt, kn, kt, vn, dot_, ot, lse, gq, gkv, dk, dv, zq, zd
):
    heads = qt.shape[0] // HEAD
    size = per * BLK
    place, count, at = span(sc, half, per, pl.num_programs(0))
    queries = gq[:, pl.ds(pl.multiple_of(place * BLK, BLK), BLK)]
    spread(qt, zq)
    spread(dot_, zd)
    deltas = []
    for h in range(heads):
        part = slice(h * HEAD, (h + 1) * HEAD)
        deltas.append(
            jnp.sum(dot_[part, :].astype(F32) * ot[part, :].astype(F32), axis=0, keepdims=True)
        )

    def body(t, carry):
        shard, stored = at(t)
        mask = allowed(gkv, queries, place, shard, size)
        at_keys = pl.ds(pl.multiple_of(stored * size, size), size)
        keys, values = kn[at_keys, :], vn[at_keys, :]
        out = []
        for h in range(heads):
            part = slice(h * HEAD, (h + 1) * HEAD)
            s = jnp.where(mask, nn(keys, zq[h]), neg_large)
            p = jnp.exp(s - lse[h : h + 1, :])
            ds = (p * (nn(values, zd[h]) - deltas[h])).astype(BF16)
            dv[part, at_keys] += nt(dot_[part, :], p.astype(BF16))
            dk[part, at_keys] += nt(qt[part, :], ds)
            out.append(carry[h] + nn(kt[part, at_keys], ds))
        return tuple(out)

    zero = jnp.zeros((HEAD, BLK), F32)
    return lax.fori_loop(0, count, body, (zero,) * heads)


def first_back_kernel(per, sc, qt, kn, kt, vn, dot_, ot, lse, gq, gkv, dqt, dk_o, dv_o, dk, dv, zq, zd):
    step = pl.program_id(0)

    @pl.when(step == 0)
    def _():
        dk[...] = jnp.zeros(dk.shape, F32)
        dv[...] = jnp.zeros(dv.shape, F32)

    dq = backward_block(0, per, sc, qt, kn, kt, vn, dot_, ot, lse, gq, gkv, dk, dv, zq, zd)
    for h, part in enumerate(dq):
        dqt[h * HEAD : (h + 1) * HEAD, :] = part.astype(BF16)

    @pl.when(step == pl.num_programs(0) - 1)
    def _():
        dk_o[...] = dk[...]
        dv_o[...] = dv[...]


def folded(v):
    return sum(v[at : at + FOLD, :] for at in range(0, v.shape[0], FOLD))


def halves(row):
    high = row.astype(BF16)
    return [high, (row - high.astype(F32)).astype(BF16)]


def second_back_kernel(
    per, pieces, sc, qt, kn, kt, vn, dot_, ot, lse, gq, gkv,
    dk_i, dv_i, dqa, go, gox, gain, gain_m, n1_h, wt_h, *rest
):
    r2, r3, dk_o, dv_o = rest[:4]
    outs = rest[4 : 4 + pieces]
    dk, dv, dqb, zq, zd, n1, wt, gs, sems = rest[4 + pieces :]
    step = pl.program_id(0)
    cols = dk.shape[0]
    copies = [
        pltpu.make_async_copy(n1_h, n1, sems.at[0]),
        pltpu.make_async_copy(wt_h, wt, sems.at[1]),
    ]

    @pl.when(step == 0)
    def _():
        for copy in copies:
            copy.start()
        dk[...] = dk_i[...]
        dv[...] = dv_i[...]

    dq = backward_block(1, per, sc, qt, kn, kt, vn, dot_, ot, lse, gq, gkv, dk, dv, zq, zd)
    at = pl.multiple_of(step * BLK, BLK)
    for h, part in enumerate(dq):
        dqb[h * HEAD : (h + 1) * HEAD, pl.ds(at, BLK)] = part.astype(BF16)

    @pl.when(step == pl.num_programs(0) - 1)
    def _():
        for copy in copies:
            copy.wait()
        both = dqb.shape[1]
        dkb, dvb = dk[...].astype(BF16), dv[...].astype(BF16)
        dk_o[...] = dkb[:, :both]
        dv_o[...] = dvb[:, :both]
        grads = jnp.concatenate([dkb[:, both:], dqb[...], dvb[:, both:]], axis=0)
        part = nn(grads.T, wt[0 : 3 * cols, :]).astype(BF16)
        r2[...] = part[: both // 2]
        r3[...] = part[both // 2 :]
        gt = [
            nn(dkb, n1[...]),
            nn(dqa[...], n1[:both, :]) + nn(dqb[...], n1[both:, :]),
            nn(dvb, n1[...]),
        ]
        total = jnp.zeros((FOLD, gain.shape[1]), F32)
        for j in range(3):
            total += folded(gt[j] * wt[j * cols : (j + 1) * cols, :].astype(F32))
        gain_a = jnp.sum(total, axis=0, keepdims=True) / gain[...]
        gt.append(go[...] + gox[...].astype(F32))
        gs[...] = jnp.concatenate(gt, axis=0).T.astype(BF16)
        depth = gs.shape[0] // pieces
        extra = halves(gain_a) + halves(jnp.sum(gain_m[...], axis=0, keepdims=True))
        extra.append(jnp.zeros((EXTRA - len(extra), gain.shape[1]), BF16))
        extra = jnp.concatenate(extra, axis=0)
        for j, out in enumerate(outs):
            start = pl.multiple_of((sc[1] ^ j) * depth, 16) if pieces > 1 else 0
            out[0:depth, :] = gs[pl.ds(start, depth), :]
            out[depth : depth + EXTRA, :] = extra


def back_specs(half, total, cols):
    blocks = total // BLK // 2
    return [
        SMEM,
        pl.BlockSpec((cols, BLK), lambda i: (1, half * blocks + i)),
        whole((total, cols)),
        pl.BlockSpec((cols, total), lambda i: (0, 0)),
        whole((total, cols)),
        pl.BlockSpec((cols, BLK), lambda i: (0, i)),
        pl.BlockSpec((cols, BLK), lambda i: (0, i)),
        pl.BlockSpec((8, BLK), lambda i: (0, i)),
        whole((1, total)),
        whole((total, 128)),
    ]


def spread_scratch(cols):
    return [pltpu.VMEM((cols // HEAD, cols, BLK), BF16)] * 2


def first_back(sc, qkvt, kn, vn, dout, out, lse, gq, gkv):
    total, cols = kn.shape
    blocks = total // BLK // 2
    return pl.pallas_call(
        functools.partial(first_back_kernel, total // 4 // BLK),
        grid=(blocks,),
        in_specs=back_specs(0, total, cols),
        out_specs=[
            pl.BlockSpec((cols, BLK), lambda i: (0, i)),
            whole((cols, total)),
            whole((cols, total)),
        ],
        out_shape=[
            shape((cols, blocks * BLK), BF16),
            shape((cols, total), F32),
            shape((cols, total), F32),
        ],
        scratch_shapes=[pltpu.VMEM((cols, total), F32)] * 2 + spread_scratch(cols),
        name="attention_back",
        cost_estimate=cost(20),
    )(sc, qkvt, kn, qkvt, vn, dout, out, lse, gq, gkv)


def second_back(pieces, sc, qkvt, kn, vn, dout, out, lse, gq, gkv, dk, dv, dqa, go, gox, gain, gain_m, n1, wt):
    total, cols = kn.shape
    blocks = total // BLK // 2
    both = blocks * BLK
    width = n1.shape[1]
    piece = (width // pieces + EXTRA, 4 * cols)
    return pl.pallas_call(
        functools.partial(second_back_kernel, total // 4 // BLK, pieces),
        grid=(blocks,),
        in_specs=back_specs(1, total, cols)
        + [whole((cols, total))] * 2
        + [whole((cols, both))]
        + [whole((cols, width))] * 2
        + [whole((1, width)), whole(gain_m.shape)]
        + [HBM] * 2,
        out_specs=[whole((both // 2, width))] * 2
        + [whole((cols, both))] * 2
        + [whole(piece)] * pieces,
        out_shape=[shape((both // 2, width), BF16)] * 2
        + [shape((cols, both), BF16)] * 2
        + [shape(piece, BF16)] * pieces,
        scratch_shapes=[pltpu.VMEM((cols, total), F32)] * 2
        + [pltpu.VMEM((cols, both), BF16)]
        + spread_scratch(cols)
        + [
            pltpu.VMEM(n1.shape, BF16),
            pltpu.VMEM(wt.shape, BF16),
            pltpu.VMEM((width, 4 * cols), BF16),
            pltpu.SemaphoreType.DMA((2,)),
        ],
        compiler_params=room(48),
        name="attention_back_end",
        cost_estimate=cost(0.01),
    )(sc, qkvt, kn, qkvt, vn, dout, out, lse, gq, gkv, dk, dv, dqa, go, gox, gain, gain_m, n1, wt)


def rows_kernel(fn, counts, n_const, n_out, chunks, split, *refs):
    ins = []
    for count in counts:
        ins.append(refs[:count])
        refs = refs[count:]
    n_in = len(ins)
    consts, refs = refs[:n_const], refs[n_const:]
    outs, refs = refs[:n_out], refs[n_out:]
    pieces, refs = refs[:split], refs[split:]
    sums, refs = refs[: len(refs) - n_in - n_out - 2], refs[len(refs) - n_in - n_out - 2 :]
    held, made, (in_sem, out_sem) = refs[:n_in], refs[n_in:-2], refs[-2:]
    size = held[0].shape[0] // chunks

    def part(c):
        return pl.ds(pl.multiple_of(c * size, size), size)

    def arrival(i, c):
        src = ins[i][c] if len(ins[i]) > 1 else ins[i][0].at[part(c)]
        return pltpu.make_async_copy(src, held[i].at[part(c)], in_sem.at[i, c])

    def departure(i, c):
        return pltpu.make_async_copy(made[i].at[part(c)], outs[i].at[part(c)], out_sem.at[i, c])

    def apart(c):
        return pltpu.make_async_copy(made[-1].at[part(c)], pieces[c], out_sem.at[n_out, c])

    for c in range(chunks):
        for i in range(n_in):
            arrival(i, c).start()
    def each(c, of_chunk, many):
        if not many:
            of_chunk(c)
            return
        for known in range(chunks):

            @pl.when(c == known)
            def _(known=known):
                of_chunk(known)

    def body(c, totals):
        for i in range(n_in):
            each(c, lambda c, i=i: arrival(i, c).wait(), len(ins[i]) > 1)
        where = pl.ds(pl.multiple_of(c * size, size), size)
        results, adds = fn([r[where, :] for r in held], [r[...] for r in consts])
        for i, value in enumerate(results):
            made[i][where, :] = value
        if split:
            each(c, lambda c: apart(c).start(), True)
        for i in range(n_out):
            departure(i, c).start()
        return tuple(t + a for t, a in zip(totals, adds))

    totals = lax.fori_loop(0, chunks, body, tuple(jnp.zeros(r.shape, F32) for r in sums))
    for ref, t in zip(sums, totals):
        ref[...] = t
    for c in range(chunks):
        if split:
            apart(c).wait()
        for i in range(n_out):
            departure(i, c).wait()


def by_rows(name, fn, ins, arrived, consts, kinds, sums=(), chunks=2, split=0):
    near = len(ins)
    ins = (*ins, *arrived)
    dims = ins[0].shape
    flat = [v if isinstance(v, tuple) else (v,) for v in ins]
    return pl.pallas_call(
        functools.partial(
            rows_kernel, fn, [len(v) for v in flat], len(consts), len(kinds), chunks, split
        ),
        in_specs=[HBM] * near
        + [ANY] * sum(len(v) for v in flat[near:])
        + [VMEM] * len(consts),
        out_specs=[HBM] * (len(kinds) + split) + [VMEM] * len(sums),
        out_shape=[shape(dims, k) for k in kinds]
        + [shape((dims[0] // chunks, dims[1]), kinds[-1])] * split
        + [shape(d, F32) for d in sums],
        scratch_shapes=[pltpu.VMEM(dims, v[0].dtype) for v in flat]
        + [pltpu.VMEM(dims, k) for k in kinds]
        + [
            pltpu.SemaphoreType.DMA((len(ins), chunks)),
            pltpu.SemaphoreType.DMA((len(kinds) + 1, chunks)),
        ],
        compiler_params=room(24),
        name=name,
        cost_estimate=cost(0.01),
    )(*[part for v in flat for part in v], *consts)


def out_kernel(om, ox, wm, wx, own, other, omv, oxv, wmv, wxv, ownv, otherv, sems):
    rows = own.shape[0]
    copies = [
        pltpu.make_async_copy(src, dst, sems.at[i])
        for i, (src, dst) in enumerate(((om, omv), (ox, oxv), (wm, wmv), (wx, wxv)))
    ]
    for copy in copies:
        copy.start()
    for copy in copies:
        copy.wait()
    leave = [
        pltpu.make_async_copy(made, out, sems.at[4 + i])
        for i, (made, out) in enumerate(((otherv, other), (ownv, own)))
    ]

    def body(i, carry):
        where = pl.ds(pl.multiple_of((1 - i) * rows, rows), rows)
        part = (nn(omv[:, where].T, wmv[...]) + nn(oxv[:, where].T, wxv[...])).astype(BF16)
        for c, (made, copy) in enumerate(zip((otherv, ownv), leave)):

            @pl.when(i == c)
            def _(made=made, copy=copy):
                made[...] = part
                copy.start()

        return carry

    lax.fori_loop(0, 2, body, 0)
    for copy in leave:
        copy.wait()


def out_projection(om, ox, wm, wx):
    cols, both = om.shape
    width = wm.shape[1]
    made = (both // 2, width)
    return pl.pallas_call(
        out_kernel,
        in_specs=[HBM, ANY, HBM, ANY],
        out_specs=[HBM] * 2,
        out_shape=[shape(made, BF16)] * 2,
        scratch_shapes=[pltpu.VMEM(v.shape, BF16) for v in (om, ox, wm, wx)]
        + [pltpu.VMEM(made, BF16)] * 2
        + [pltpu.SemaphoreType.DMA((6,))],
        compiler_params=room(24),
        name="out_projection",
        cost_estimate=cost(0.01),
    )(om, ox, wm, wx)


def middle_rows(held, consts):
    tokens, own, got = (v.astype(F32) for v in held)
    h1 = tokens + (own + got)
    scale = lax.rsqrt(jnp.mean(h1 * h1, axis=-1, keepdims=True) + eps_norm)
    return (h1, (h1 * scale * consts[0]).astype(BF16)), ()


def middle(tokens, own, got, gain):
    return by_rows("middle", middle_rows, (tokens, own), (got,), (gain,), (F32, BF16), split=2)


def mlp_kernel(at, aliased, na, nb, ya, yb, w, *refs):
    ma, mb, da, db, hid_o, dgu_o, nv, yv, wv, mv, dv, hv, gv, in_sem, w_sem, out_sem = refs[aliased:]
    rows, units = na.shape[0], hv.shape[1]
    arrivals, departures = [], []
    for c, (n, y, m, d) in enumerate(((na, ya, ma, da), (nb, yb, mb, db))):
        part, place = pl.ds(c * rows, rows), pl.ds(at, rows)
        arrivals += [
            pltpu.make_async_copy(n, nv.at[part], in_sem.at[0, c]),
            pltpu.make_async_copy(y.at[place], yv.at[part], in_sem.at[1, c]),
        ]
        departures.append(
            [
                pltpu.make_async_copy(dv.at[part], d, out_sem.at[0, c]),
                pltpu.make_async_copy(mv.at[part], m.at[place], out_sem.at[1, c]),
                pltpu.make_async_copy(hv.at[part], hid_o.at[part], out_sem.at[2, c]),
                pltpu.make_async_copy(gv.at[part], dgu_o.at[part], out_sem.at[3, c]),
            ]
        )
    weights = [
        pltpu.make_async_copy(
            w.at[:, pl.ds(j * units, units)], wv.at[:, pl.ds(j * units, units)], w_sem.at[j]
        )
        for j in range(3)
    ]
    for copy in weights + arrivals:
        copy.start()
    for copy in weights + arrivals:
        copy.wait()
    wg, wu, wd = (wv.at[:, pl.ds(j * units, units)] for j in range(3))
    tile = rows if rows < 512 else 512

    def body(i, carry):
        part = pl.ds(pl.multiple_of(i * tile, tile), tile)
        n2 = nv[part, :]
        gate, up = nn(n2, wg[...]), nn(n2, wu[...])
        dhid = nn(yv[part, :], wd[...])
        square = gate * gate
        share = 0.5 * jnp.tanh(gate * (ROOT + ROOT * 0.044715 * square)) + 0.5
        value = gate * share
        slope = share + value * (1.0 - share) * (2.0 * ROOT + 6.0 * ROOT * 0.044715 * square)
        dgate = (dhid * up * slope).astype(BF16)
        dup = (dhid * value).astype(BF16)
        hidden = (value * up).astype(BF16)
        dv[part, :] = (nt(dgate, wg[...]) + nt(dup, wu[...])).astype(BF16)
        hv[part, :] = hidden
        gv[part, 0:units] = dgate
        gv[part, units : 2 * units] = dup
        mv[part, :] = nt(hidden, wd[...]).astype(BF16)
        for c, copies in enumerate(departures):

            @pl.when(i == c * rows // tile)
            def _(copies=copies):
                for copy in copies:
                    copy.start()

        return carry

    lax.fori_loop(0, 2 * rows // tile, body, 0)
    for copies in departures:
        for copy in copies:
            copy.wait()


def mlp_both(na, nb, ya, yb, weights, at=0, into=(), mib=32):
    rows, width = na.shape
    units = weights.shape[1] // 3
    both = 2 * rows
    return pl.pallas_call(
        functools.partial(mlp_kernel, at, len(into)),
        in_specs=[ANY] * 4 + [HBM] * (1 + len(into)),
        out_specs=[HBM] * 6,
        out_shape=[shape(ya.shape, BF16)] * 2
        + [shape((rows, width), BF16)] * 2
        + [shape((both, units), BF16), shape((both, 2 * units), BF16)],
        scratch_shapes=[
            pltpu.VMEM((both, width), BF16),
            pltpu.VMEM((both, width), BF16),
            pltpu.VMEM(weights.shape, BF16),
            pltpu.VMEM((both, width), BF16),
            pltpu.VMEM((both, width), BF16),
            pltpu.VMEM((both, units), BF16),
            pltpu.VMEM((both, 2 * units), BF16),
            pltpu.SemaphoreType.DMA((2, 2)),
            pltpu.SemaphoreType.DMA((3,)),
            pltpu.SemaphoreType.DMA((4, 2)),
        ],
        input_output_aliases={5 + i: i for i in range(len(into))},
        compiler_params=room(mib),
        name="mlp",
        cost_estimate=cost(8),
    )(na, nb, ya, yb, weights, *into)


def mlp_weights_kernel(order, n_in, *refs):
    ins, (out, *held, total, made, sems, sem) = refs[:n_in], refs[n_in:]
    copies = []
    for group, moves in enumerate(order):
        for which, start, rows, at in moves:
            copy = pltpu.make_async_copy(
                ins[which].at[pl.ds(start, rows)], held[group].at[pl.ds(at, rows)], sems.at[len(copies)]
            )
            copies.append((at + rows, copy))
    size = held[0].shape[0] // 2
    copies.sort(key=lambda v: v[0])
    for _, copy in copies:
        copy.start()
    wide = held[2].shape[1]

    def body(i, carry):
        for c in range(2):

            @pl.when(i == c)
            def _(c=c):
                for end, copy in copies:
                    if c * size < end <= (c + 1) * size:
                        copy.wait()

        rows = pl.ds(pl.multiple_of(i * size, size), size)
        n2, dy, dgu, hidden = (r[rows, :] for r in held)
        for at, left, right in ((0, n2, dgu), (wide, dy, hidden)):
            cols = pl.ds(at, right.shape[1])
            new = nn(left.T, right) + total[:, cols]
            total[:, cols] = new
            made[:, cols] = new.astype(BF16)
        return carry

    total[...] = jnp.zeros(total.shape, F32)
    lax.fori_loop(0, 2, body, 0)
    leave = pltpu.make_async_copy(made, out, sem)
    leave.start()
    leave.wait()


def mlp_weights(n2, dy, dgu, hidden):
    ins = (*n2, *dy, *dgu, *hidden)
    rows = n2[0].shape[0]
    half = rows // 2
    first = [(0, 0, rows, 0), (1, 0, rows, rows)]
    order = [
        first + [(2, 0, half, 2 * rows), (4, 0, half, 2 * rows + half), (3, 0, half, 3 * rows), (5, 0, half, 3 * rows + half)],
        [(6 + j, 0, rows, j * rows) for j in range(4)],
    ]
    for base in (10, 13):
        order.append(
            [
                (base, 0, 2 * rows, 0),
                (base + 1, 0, half, 2 * rows),
                (base + 2, 0, half, 2 * rows + half),
                (base + 1, half, half, 3 * rows),
                (base + 2, half, half, 3 * rows + half),
            ]
        )
    width = n2[0].shape[1]
    dims = (width, dgu[0].shape[1] + hidden[0].shape[1])
    return pl.pallas_call(
        functools.partial(mlp_weights_kernel, order, len(ins)),
        in_specs=[HBM] * len(ins),
        out_specs=HBM,
        out_shape=shape(dims, BF16),
        scratch_shapes=[
            pltpu.VMEM((4 * rows, v.shape[1]), BF16) for v in (n2[0], dy[0], dgu[0], hidden[0])
        ]
        + [
            pltpu.VMEM(dims, F32),
            pltpu.VMEM(dims, BF16),
            pltpu.SemaphoreType.DMA((sum(len(v) for v in order),)),
            pltpu.SemaphoreType.DMA,
        ],
        compiler_params=room(48),
        name="mlp_weights",
        cost_estimate=cost(10),
    )(*ins)


def middle_back_rows(held, consts):
    dy, h1, *shares = (v.astype(F32) for v in held)
    dn2 = sum(shares[1:], shares[0])
    scale = lax.rsqrt(jnp.mean(h1 * h1, axis=-1, keepdims=True) + eps_norm)
    hat = dn2 * consts[0]
    dh1 = (
        dy
        + scale * hat
        - h1 * (scale * scale * scale) * jnp.mean(hat * h1, axis=-1, keepdims=True)
    )
    return (dh1, dh1.astype(BF16)), (folded(dn2 * h1 * scale),)


def middle_back(dy, h1, a, b, c, gain):
    return by_rows(
        "middle_back",
        middle_back_rows,
        (dy, h1, a),
        (b, c),
        (gain,),
        (F32, BF16),
        sums=((FOLD, dy.shape[1]),),
    )


def out_back_kernel(own, other, wm, wx, om, ox, dm_o, dx_o, gm_o, gx_o, *scratch):
    refs = (own, other, wm, wx, om, ox)
    held, made, sems = scratch[:6], scratch[6:10], scratch[10]
    copies = [pltpu.make_async_copy(src, dst, sems.at[i]) for i, (src, dst) in enumerate(zip(refs, held))]
    for copy in copies:
        copy.start()
    ownv, otherv, wmv, wxv, omv, oxv = held
    dm, dx, gm, gx = made
    rows = own.shape[0]
    for copy in copies:
        copy.wait()
    leave = [
        pltpu.make_async_copy(src, dst, sems.at[6 + i])
        for i, (src, dst) in enumerate(((dx, dx_o), (dm, dm_o), (gx, gx_o), (gm, gm_o)))
    ]
    for i, (w, out) in enumerate(((wxv, dx), (wmv, dm))):
        for at, ref in ((0, ownv), (rows, otherv)):
            out[:, at : at + rows] = nt(w[...], ref[...]).astype(BF16)
        leave[i].start()
    gx[...] = (nn(oxv[:, :rows], ownv[...]) + nn(oxv[:, rows:], otherv[...])).astype(BF16)
    leave[2].start()
    gm[...] = nn(omv[:, :rows], ownv[...]) + nn(omv[:, rows:], otherv[...])
    leave[3].start()
    for copy in leave:
        copy.wait()


def out_back(own, other, wm, wx, om, ox):
    cols, both = om.shape
    width = own.shape[1]
    ins = (own, other, wm, wx, om, ox)
    outs = [
        ((cols, both), BF16),
        ((cols, both), BF16),
        ((cols, width), F32),
        ((cols, width), BF16),
    ]
    return pl.pallas_call(
        out_back_kernel,
        in_specs=[HBM, ANY, HBM, ANY, HBM, ANY],
        out_specs=[HBM] * 4,
        out_shape=[shape(*v) for v in outs],
        scratch_shapes=[pltpu.VMEM(v.shape, BF16) for v in ins]
        + [pltpu.VMEM(*v) for v in outs]
        + [pltpu.SemaphoreType.DMA((10,))],
        compiler_params=room(24),
        name="out_back",
        cost_estimate=cost(0.01),
    )(*ins)


def rows_back_kernel(dk, dq, dv, wt, a_o, b_o):
    rows = a_o.shape[0]

    def body(i, carry):
        where = pl.ds(pl.multiple_of(i * rows, rows), rows)
        grads = jnp.concatenate([dk[:, where], dq[:, where], dv[:, where]], axis=0)
        part = nn(grads.T, wt[...]).astype(BF16)
        for c, ref in enumerate((a_o, b_o)):

            @pl.when(i == c)
            def _(ref=ref):
                ref[...] = part

        return carry

    lax.fori_loop(0, 2, body, 0)


def rows_back(dk, dq, dv, wt):
    cols, both = dq.shape
    width = wt.shape[1]
    return pl.pallas_call(
        rows_back_kernel,
        out_shape=[shape((both // 2, width), BF16)] * 2,
        compiler_params=room(24),
        name="rows_back",
        cost_estimate=cost(0.01),
    )(dk, dq, dv, wt)


def last_rows(held, consts):
    x, dh1, *shares = (v.astype(F32) for v in held)
    dn1 = sum(shares[1:], shares[0])
    scale = lax.rsqrt(jnp.mean(x * x, axis=-1, keepdims=True) + eps_norm)
    hat = dn1 * consts[0]
    out = (
        dh1
        + scale * hat
        - x * (scale * scale * scale) * jnp.mean(hat * x, axis=-1, keepdims=True)
    )
    return (out.astype(BF16),), ()


def last(tokens, dh1, a, b, c, gain):
    return by_rows("last", last_rows, (tokens, dh1, a), (b, c), (gain,), (BF16,))[0]


def grads_sum_kernel(count, *refs):
    ins, outs, gains_o = refs[:count], refs[count:-1], refs[-1]
    rows, cols = outs[0].shape
    total = ins[0][0:rows, :].astype(F32)
    for ref in ins[1:]:
        total = total + ref[0:rows, :].astype(F32)
    for j, ref in enumerate(outs):
        ref[...] = total[:, j * cols : (j + 1) * cols]
    tail = [ref[rows : rows + EXTRA, :].astype(F32) for ref in ins]
    gains = tail[0]
    for part in tail[1:]:
        gains = gains + part
    gains = gains[0:4, :] + gains[4:8, :]
    gains_o[...] = jnp.concatenate(
        [gains[0:1, :] + gains[1:2, :], gains[2:3, :] + gains[3:4, :]], axis=0
    )


def grads_sum(parts):
    rows, width = parts[0].shape
    rows -= EXTRA
    return pl.pallas_call(
        functools.partial(grads_sum_kernel, len(parts)),
        out_shape=[shape((rows, width // 4), F32)] * 4 + [shape((2, width), F32)],
        compiler_params=room(16),
        name="grads_sum",
        cost_estimate=cost(0.01),
    )(*parts)


def local(
    dp,
    mp,
    tokens,
    w_query,
    w_key,
    w_value,
    w_out,
    w_gate,
    w_up,
    w_down,
    norm_attn,
    norm_mlp,
    valid_counts,
    group_ids,
    cotangent,
):
    me, row = lax.axis_index("mp"), lax.axis_index("dp")
    cols = w_query.shape[1]
    length = group_ids.shape[1]

    def core(v):
        return lax.ppermute(v, "mp", [(i, i ^ 1) for i in range(mp)])

    def across(v):
        return lax.ppermute(v, "mp", [(i, i ^ 2) for i in range(mp)])

    def far(v, k):
        return lax.ppermute(v, "dp", [(i, i ^ k) for i in range(dp)])

    def after(v, *others):
        return lax.optimization_barrier((v, *others))[0]

    def summed(a, b):
        return (a.astype(F32) + b.astype(F32)).astype(BF16)

    direct = dp <= DIRECT
    gain_a, gain_m = norm_attn[None], norm_mlp[None]

    gq = group_ids
    flat = group_ids[0]
    valid = valid_counts[0]
    tiles = flat.reshape(length // BLK, BLK)
    low = jnp.sum(flat[None, :] < tiles[:, :1], axis=1) // BLK
    high = jnp.minimum(jnp.sum(flat[None, :] <= tiles[:, -1:], axis=1), valid)
    high = (high + BLK - 1) // BLK
    head = jnp.stack([me, row, valid, valid, valid, valid, valid, valid])
    sc = jnp.concatenate([head, low, high]).astype(jnp.int32)
    keyed = jnp.where(jnp.arange(length, dtype=jnp.int32) < valid, flat, -1)
    gkv = jnp.broadcast_to(keyed[:, None], (length, 128))

    tok2 = across(tokens)
    w_attn = jnp.concatenate([w_key, w_query, w_value, w_out], axis=1)
    w_mlp = jnp.concatenate([w_gate, w_up, w_down], axis=1)
    if direct:
        near = [w_attn] + [far(w_attn, k) for k in range(2, dp, 2)]
        near[1] = after(near[1], sc, gkv, w_mlp)
        w_pieces = [p for v in near for p in (v, far(v, 1))]
        tok1 = core(after(tokens, w_pieces[1]))
    else:
        w_pieces = [lax.all_gather(w_attn, "dp", axis=0, tiled=True)]
        tok1 = core(tokens)
    w_mlp = lax.all_gather(w_mlp, "dp", axis=0, tiled=True)
    tok3 = core(after(tok2, *w_pieces[1::2]))

    n1, qkvt, kn, vn, wt, wo = qkv(sc, (tokens, tok1, tok2, tok3), gain_a, w_pieces, cols)
    wo_x = across(wo)
    dy0 = cotangent
    dy2 = across(after(cotangent, tok2))
    dy1 = core(after(cotangent, tok3))

    o_far, lse_far = attention(1, sc, qkvt, kn, gq, gkv)
    o_x = across(after(o_far, dy2, wo_x))
    dy3 = core(after(dy2, o_far))
    o_own, lse_own = attention(0, after(sc, o_far), qkvt, kn, gq, gkv)
    p_own, p_other = out_projection(o_own, o_x, wo, wo_x)
    h1, n2, n2_a, n2_b = middle(tokens, p_own, core(p_other), gain_m)

    half = n2.shape[0] // 2
    n2_1 = core(n2)
    far_a = across(n2_a)
    far_b = across(n2_b)
    m0, m1, d0, d1, hid_o, dgu_o = mlp_both(n2, n2_1, dy0, dy1, w_mlp, mib=60)
    side_a = core(after(far_a, d0))
    m2, m3, d2a, d3a, hid_a, dgu_a = mlp_both(far_a, side_a, dy2, dy3, w_mlp)
    dsum_a = summed(d2a, core(d3a))
    dx_a = across(dsum_a)
    side_b = core(after(far_b, d2a))
    far_b = after(far_b, dsum_a)
    m2, m3, d2b, d3b, hid_b, dgu_b = mlp_both(far_b, side_b, dy2, dy3, w_mlp, half, (m2, m3))

    d_sum = summed(d2b, core(after(d3b, dx_a)))
    dx_b = across(d_sum)
    mlp_all = mlp_weights(
        (n2, n2_1, far_a, side_a, far_b, side_b),
        (dy0, dy1, dy2, dy3),
        (dgu_o, dgu_a, dgu_b),
        (after(hid_o, d_sum), hid_a, hid_b),
    )
    mlp_grads = lax.psum_scatter(mlp_all, "dp", scatter_dimension=0, tiled=True)
    m_sum, m_core = summed(after(m2, d_sum), core(m3)), core(after(m1, d_sum))
    dh1, da, gain_m_part = middle_back(
        dy0,
        h1,
        d0,
        core(after(d1, d_sum)),
        (dx_a, after(dx_b, mlp_all, m_sum, m_core)),
        gain_m,
    )

    do_own, do_send, go, go_send = out_back(da, core(da), wo, wo_x, o_own, o_x)
    do_far = across(do_send)
    go_x = across(go_send)
    m_x = across(after(m_sum, do_send))
    dq_own, dk, dv = first_back(sc, qkvt, kn, vn, do_own, o_own, lse_own, gq, gkv)
    r2, r3, dk_own, dv_own, *grads = second_back(
        dp if direct else 1,
        sc, qkvt, kn, vn, do_far, o_far, lse_far, gq, gkv,
        dk, dv, dq_own, go, go_x, gain_a, gain_m_part, n1, wt,
    )
    r_sum = summed(r2, core(after(r3, m_x)))
    r_x = across(r_sum)
    depth = w_query.shape[0]
    parts = []
    if direct:
        others = {}
        for k in range(dp - 2, -1, -2):
            sent = grads[k + 1]
            others[k] = far(after(sent, others[k + dp // 2]) if k + dp // 2 in others else sent, 1)
        for k in range(0, dp, 2):
            near, other = grads[k], after(others[k], r_sum)
            both = summed(near[:depth], other[:depth])
            part = jnp.concatenate([both, near[depth : depth + 4], other[depth : depth + 4]], axis=0)
            parts.append(part if k == 0 else far(part, k))
    r0, r1 = rows_back(after(dk_own, r_sum), dq_own, dv_own, wt)
    grad_tokens = last(tokens, dh1, r0, core(r1), r_x, gain_a)
    output = (
        h1 + (m0.astype(F32) + m_core.astype(F32) + after(m_x, r_sum).astype(F32))
    ).astype(BF16)
    units = w_gate.shape[1]
    grad_gate, grad_up, grad_down = (
        mlp_grads[:, j * units : (j + 1) * units].astype(F32) for j in range(3)
    )
    if direct:
        parts[0] = after(parts[0], grad_tokens, output, grad_gate)
        grad_k, grad_q, grad_v, grad_o, gains = grads_sum(parts)
        gains = gains + core(gains)
        gains = gains + across(gains)
    else:
        width = tokens.shape[1]
        attn_grads = lax.psum_scatter(
            grads[0][:width], "dp", scatter_dimension=0, tiled=True
        ).astype(F32)
        grad_k, grad_q, grad_v, grad_o = jnp.split(attn_grads, 4, axis=1)
        extra = grads[0][width : width + 4].astype(F32)
        gains = lax.psum(extra[0::2] + extra[1::2], ("dp", "mp"))

    return (
        output,
        grad_tokens,
        grad_q,
        grad_k,
        grad_v,
        grad_o,
        grad_gate,
        grad_up,
        grad_down,
        gains[0],
        gains[1],
    )


def solution(mesh):
    rows, weight = P(("dp", "mp"), None), P("dp", "mp")
    return jax.shard_map(
        functools.partial(local, mesh.shape["dp"], mesh.shape["mp"]),
        mesh=mesh,
        in_specs=(rows,) + (weight,) * 7 + (P(), P(), P("dp"), P("dp", None), rows),
        out_specs=(rows, rows) + (weight,) * 7 + (P(), P()),
        check_vma=False,
    )
```

profile of v0, /device:TPU:0, one launch (start us, length us, event | category | flops | bytes accessed | tf_op | source)
XLA Modules:
  0.0 247.6 jit_solution(17997583010579313100)
XLA Ops:
  8.3 5.1 %collective-permute-start.7 = (bf16[96,768]{1,0:T(8,128)(2,1)S(1)}, bf16[96,768]{1,0:T(8,128)(2,1)S(1)}, u32[]{:S(2)}, u32[]{:S(2)}) collective-permute-start(bf16[96,768]{1,0:T(8,128)(2,1)S(1)} %pad_maximum_fusion.4.rest_0_), channel_id=1, source_target_pairs={{0,24},{4,28},{8,16},{12,20},{16,8},{20,12},{24,0},{28,4},{1,25},{... | collective-permute-start | bytes 442376 | tf_op jit(solution)/shard_map/ppermute | solution.py:937
  28.0 4.2 %collective-permute-done.8.rest_7_ = bf16[96,768]{1,0:T(8,128)(2,1)S(1)} collective-permute-done((bf16[96,768]{1,0:T(8,128)(2,1)S(1)}, bf16[96,768]{1,0:T(8,128)(2,1)S(1)}, u32[]{:S(2)}, u32[]{:S(2)}) %collective-permute-start.8) | collective-permute-done | bytes 147488 | tf_op jit(solution)/shard_map/ppermute | solution.py:937
  32.2 2.3 collective-permute-done.6.rest_5_
  38.7 9.5 %qkv.1 = (bf16[2048,768]{1,0:T(8,128)(2,1)}, bf16[576,2048]{1,0:T(8,128)(2,1)}, bf16[2048,192]{1,0:T(8,128)(2,1)}, bf16[2048,192]{1,0:T(8,128)(2,1)}, bf16[576,7...) custom-call(s32[24]{0:T(128)} %concatenate.21.sc, bf16[512,768]{1,0:T(8,128)(2,1)} %refs_0_.5, ...), custom_call_target="tpu_custom_call" | custom-call | flops 10000000 | bytes 1024 | tf_op jit(solution)/shard_map/qkv/pallas_call | solution.py:88
  52.1 4.4 %attention.2 = (bf16[192,1024]{1,0:T(8,128)(2,1)S(1)}, f32[8,1024]{1,0:T(8,128)S(1)}) custom-call(s32[24]{0:T(128)S(1)} %copy-done.30, bf16[576,2048]{1,0:T(8,128)(2,1)S(1)} %copy-done, bf16[2048,192]{1,0:T(8,128)(2,1)S(1)} %copy-done.16, bf16[576,2048]{1,0:T(8,128)(2,1)S(1)} %copy-done, s32[1,2048]{1,0:T(1,128)S(1)} %copy-done.23, ...), custom_call_target="tpu_custom_call" | custom-call | flops 12000000000 | bytes 1024 | tf_op jit(solution)/shard_map/attention/pallas_call | solution.py:207
  57.9 5.3 %collective-permute-done.11.wx = bf16[192,768]{1,0:T(8,128)(2,1)S(1)} collective-permute-done((bf16[192,768]{1,0:T(8,128)(2,1)}, bf16[192,768]{1,0:T(8,128)(2,1)S(1)}, u32[]{:S(2)}, u32[]{:S(2)}) %collective-permute-start.11) | collective-permute-done | bytes 294944 | tf_op jit(solution)/shard_map/ppermute | solution.py:934
  64.3 6.1 %attention.3 = (bf16[192,1024]{1,0:T(8,128)(2,1)S(1)}, f32[8,1024]{1,0:T(8,128)S(1)}) custom-call(s32[24]{0:T(128)S(1)} %copy-done.30, bf16[576,2048]{1,0:T(8,128)(2,1)S(1)} %copy-done, bf16[2048,192]{1,0:T(8,128)(2,1)S(1)} %copy-done.16, bf16[576,2048]{1,0:T(8,128)(2,1)S(1)} %copy-done, s32[1,2048]{1,0:T(1,128)S(1)} %copy-done.23, ...), custom_call_target="tpu_custom_call" | custom-call | flops 12000000000 | bytes 1024 | tf_op jit(solution)/shard_map/attention/pallas_call | solution.py:207
  70.4 3.0 %collective-permute-done.12.ox = bf16[192,1024]{1,0:T(8,128)(2,1)S(1)} collective-permute-done((bf16[192,1024]{1,0:T(8,128)(2,1)S(1)}, bf16[192,1024]{1,0:T(8,128)(2,1)S(1)}, u32[]{:S(2)}, u32[]{:S(2)}) %collective-permute-start.12) | collective-permute-done | bytes 393248 | tf_op jit(solution)/shard_map/ppermute | solution.py:934
  73.4 2.1 out_projection.1
  78.0 2.4 middle.1
  84.5 3.5 %all-gather.2.cloned.1.call-done.w = bf16[768,1536]{1,0:T(8,128)(2,1)} async-done(((bf16[96,1536]{1,0:T(8,128)(2,1)}), bf16[768,1536]{1,0:T(8,128)(2,1)}) %all-gather.2.cloned.1.call-update) | async-done | bytes 2359312 | tf_op jit(solution)/shard_map/all_gather | solution.py:971
  88.0 10.1 %mlp.3 = (bf16[512,768]{1,0:T(8,128)(2,1)}, bf16[512,768]{1,0:T(8,128)(2,1)}, bf16[512,768]{1,0:T(8,128)(2,1)}, bf16[512,768]{1,0:T(8,128)(2,1)}, bf16[1024,512]{1,0:T(8,128)(2,1)}, /*index=5*/bf16[1024,1024]{1,0:T(8,128)(2,1)}) custom-call(bf16[512,768]{1,0:T(8,128)(2,1)} %copy-done.34, bf16[512,768]{1,0:T(8,128)(2,1)} %collective-permute-done.14.nb.refs_1_, ...), custom_call_target="tpu_custom_call" | custom-call | flops 8000000000 | bytes 1024 | tf_op jit(solution)/shard_map/mlp/pallas_call | solution.py:649
  101.6 6.3 %mlp.4 = (bf16[512,768]{1,0:T(8,128)(2,1)S(1)}, bf16[512,768]{1,0:T(8,128)(2,1)}, bf16[256,768]{1,0:T(8,128)(2,1)S(1)}, bf16[256,768]{1,0:T(8,128)(2,1)S(1)}, bf...) custom-call(bf16[256,768]{1,0:T(8,128)(2,1)S(1)} %collective-permute-done.17.na.refs_2_, ...), custom_call_target="tpu_custom_call" | custom-call | flops 8000000000 | bytes 1024 | tf_op jit(solution)/shard_map/mlp/pallas_call | solution.py:649
  111.5 6.3 %mlp.5 = (bf16[512,768]{1,0:T(8,128)(2,1)S(1)}, bf16[512,768]{1,0:T(8,128)(2,1)}, bf16[256,768]{1,0:T(8,128)(2,1)S(1)}, bf16[256,768]{1,0:T(8,128)(2,1)S(1)}, bf...) custom-call(bf16[256,768]{1,0:T(8,128)(2,1)S(1)} %collective-permute-done., ...), custom_call_target="tpu_custom_call", output_to_operand_aliasing={{0}: (5, {}), {1}: (6, {})} | custom-call | flops 8000000000 | bytes 1024 | tf_op jit(solution)/shard_map/mlp/pallas_call | solution.py:649
  118.7 2.8 %collective-permute-done.22.refs_4_ = bf16[256,768]{1,0:T(8,128)(2,1)S(1)} collective-permute-done((bf16[256,768]{1,0:T(8,128)(2,1)S(1)}, bf16[256,768]{1,0:T(8,128)(2,1)S(1)}, u32[]{:S(2)}, u32[]{:S(2)}) %collective-permute-start.22) | collective-permute-done | bytes 393248 | tf_op jit(solution)/shard_map/ppermute | solution.py:934
  126.6 9.5 %mlp_weights.1 = bf16[768,1536]{1,0:T(8,128)(2,1)} custom-call(bf16[512,768]{1,0:T(8,128)(2,1)S(1)} %copy-done.35, bf16[512,768]{1,0:T(8,128)(2,1)} %collective-permute-done.14.nb.refs_1_, bf16[256,768]{1,0:T(8,128)(2,1)S(1)} %copy-done.37, bf16[256,768]{1,0:T(8,128)(2,1)S(1)} %collective-permute-done.18.nb.refs_3_, ...), custom_call_target="tpu_custom_call" | custom-call | flops 10000000000 | bytes 1024 | tf_op jit(solution)/shard_map/mlp_weights/pallas_call | solution.py:736
  136.1 2.5 %add_convert_fusion.2 = bf16[512,768]{1,0:T(8,128)(2,1)} fusion(bf16[512,768]{1,0:T(8,128)(2,1)} %collective-permute-done.25, bf16[512,768]{1,0:T(8,128)(2,1)} %copy-done.18), kind=kLoop, calls=%fused_computation.2 | loop fusion | flops 1572864 | bytes 2359296 | tf_op jit(solution)/shard_map/convert_element_type | solution.py:943
  138.6 3.3 %middle_back.1 = (f32[512,768]{1,0:T(8,128)S(1)}, bf16[512,768]{1,0:T(8,128)(2,1)}, f32[32,768]{1,0:T(8,128)S(1)}) custom-call(bf16[512,768]{1,0:T(8,128)(2,1)} %refs_0_.4, f32[512,768]{1,0:T(8,128)S(1)} %get-tuple-element.115.refs_1_, bf16[512,768]{1,0:T(8,128)(2,1)S(1)} %copy-done.17, bf16[512,768]{1,0:T(8,128)(2,1)} %collective-permute-done.26.refs_3_, ...), custom_call_target="tpu_custom_call" | custom-call | flops 10000000 | bytes 1024 | tf_op jit(solution)/shard_map/middle_back/pallas_call | solution.py:498
  143.8 2.6 %collective-permute-done.28.other = bf16[512,768]{1,0:T(8,128)(2,1)} collective-permute-done((bf16[512,768]{1,0:T(8,128)(2,1)}, bf16[512,768]{1,0:T(8,128)(2,1)}, u32[]{:S(2)}, u32[]{:S(2)}) %collective-permute-start.28) | collective-permute-done | bytes 786464 | tf_op jit(solution)/shard_map/ppermute | solution.py:931
  147.4 4.1 %out_back.1 = (bf16[192,1024]{1,0:T(8,128)(2,1)S(1)}, bf16[192,1024]{1,0:T(8,128)(2,1)}, f32[192,768]{1,0:T(8,128)S(1)}, bf16[192,768]{1,0:T(8,128)(2,1)}) custom-call(bf16[512,768]{1,0:T(8,128)(2,1)} %get-tuple-element.148.own, bf16[512,768]{1,0:T(8,128)(2,1)} %collective-permute-done.28.other, bf16[192,768]{1,0:T(8,128)(2,1)S(1)} %copy-done.13, ...), custom_call_target="tpu_custom_call" | custom-call | flops 10000000 | bytes 1024 | tf_op jit(solution)/shard_map/out_back/pallas_call | solution.py:818
  155.7 13.3 %attention_back.1 = (bf16[192,1024]{1,0:T(8,128)(2,1)}, f32[192,2048]{1,0:T(8,128)}, f32[192,2048]{1,0:T(8,128)}) custom-call(s32[24]{0:T(128)} %concatenate.21.sc, bf16[576,2048]{1,0:T(8,128)(2,1)} %get-tuple-element.105.qt.vt.kt, bf16[2048,192]{1,0:T(8,128)(2,1)} %get-tuple-element.106.kn, bf16[576,2048]{1,0:T(8,128)(2,1)} %get-tuple-element.105.qt.vt.kt, ...), custom_call_target="tpu_custom_call" | custom-call | flops 20000000000 | bytes 1024 | tf_op jit(solution)/shard_map/attention_back/pallas_call | solution.py:375
  168.9 2.8 %collective-permute-done.31.gox = bf16[192,768]{1,0:T(8,128)(2,1)} collective-permute-done((bf16[192,768]{1,0:T(8,128)(2,1)}, bf16[192,768]{1,0:T(8,128)(2,1)}, u32[]{:S(2)}, u32[]{:S(2)}) %collective-permute-start.31) | collective-permute-done | bytes 294944 | tf_op jit(solution)/shard_map/ppermute | solution.py:934
  172.7 13.0 %attention_back_end.1 = (bf16[512,768]{1,0:T(8,128)(2,1)S(1)}, bf16[512,768]{1,0:T(8,128)(2,1)S(1)}, bf16[192,1024]{1,0:T(8,128)(2,1)S(1)}, bf16[192,1024]{1,0:T...) custom-call(s32[24]{0:T(128)S(1)} %copy-done.31, ...), custom_call_target="tpu_custom_call" | custom-call | flops 10000000 | bytes 1024 | tf_op jit(solution)/shard_map/attention_back_end/pallas_call | solution.py:401
  187.7 12.5 %collective-permute-start.35 = (bf16[104,768]{1,0:T(8,128)(2,1)S(1)}, bf16[104,768]{1,0:T(8,128)(2,1)S(1)}, u32[]{:S(2)}, u32[]{:S(2)}) collective-permute-start(bf16[104,768]{1,0:T(8,128)(2,1)S(1)} %get-tuple-element.175), channel_id=1, source_target_pairs={{0,4},{4,0},{8,12},{12,8},{16,20},{20,16},{24,28},{28,24},{1,5},{5... | collective-permute-start | bytes 479240 | tf_op jit(solution)/shard_map/ppermute | solution.py:937
  200.3 4.8 %collective-permute-done.35 = bf16[104,768]{1,0:T(8,128)(2,1)S(1)} collective-permute-done((bf16[104,768]{1,0:T(8,128)(2,1)S(1)}, bf16[104,768]{1,0:T(8,128)(2,1)S(1)}, u32[]{:S(2)}, u32[]{:S(2)}) %collective-permute-start.35) | collective-permute-done | bytes 159776 | tf_op jit(solution)/shard_map/ppermute | solution.py:937
  208.5 1.9 collective-permute-start.38
  212.3 2.8 %collective-permute-done.38 = bf16[104,768]{1,0:T(8,128)(2,1)S(1)} collective-permute-done((bf16[104,768]{1,0:T(8,128)(2,1)S(1)}, bf16[104,768]{1,0:T(8,128)(2,1)S(1)}, u32[]{:S(2)}, u32[]{:S(2)}) %collective-permute-start.38) | collective-permute-done | bytes 159776 | tf_op jit(solution)/shard_map/ppermute | solution.py:937
  218.6 3.3 %collective-permute-start.41 = (bf16[104,768]{1,0:T(8,128)(2,1)S(1)}, bf16[104,768]{1,0:T(8,128)(2,1)S(1)}, u32[]{:S(2)}, u32[]{:S(2)}) collective-permute-start(bf16[104,768]{1,0:T(8,128)(2,1)S(1)} %pad_maximum_fusion.3), channel_id=1, source_target_pairs={{0,24},{4,28},{8,16},{12,20},{16,8},{20,12},{24,0},{28,4},{1,25},{... | collective-permute-start | bytes 479240 | tf_op jit(solution)/shard_map/ppermute | solution.py:937
  222.0 2.8 %add_convert_fusion = bf16[512,768]{1,0:T(8,128)(2,1)} fusion(f32[512,768]{1,0:T(8,128)S(1)} %get-tuple-element.115.refs_1_, bf16[512,768]{1,0:T(8,128)(2,1)} %collective-permute-done.29, bf16[512,768]{1,0:T(8,128)(2,1)} %collective-permute-done.24, bf16[512,768]{1,0:T(8,128)(2,1)S(1)} %copy-done.44), kind=kLoop, calls=%fused_computation | loop fusion | flops 2752512 | bytes 4718592 | tf_op jit(solution)/shard_map/convert_element_type | solution.py:1047
  224.8 4.5 %collective-permute-done.34.refs_4_ = bf16[512,768]{1,0:T(8,128)(2,1)S(1)} collective-permute-done((bf16[512,768]{1,0:T(8,128)(2,1)S(1)}, bf16[512,768]{1,0:T(8,128)(2,1)S(1)}, u32[]{:S(2)}, u32[]{:S(2)}) %collective-permute-start.34) | collective-permute-done | bytes 786464 | tf_op jit(solution)/shard_map/ppermute | solution.py:934
  229.3 3.4 %last.1 = bf16[512,768]{1,0:T(8,128)(2,1)} custom-call(bf16[512,768]{1,0:T(8,128)(2,1)S(1)} %copy-done.2, f32[512,768]{1,0:T(8,128)S(1)} %copy-done.6, bf16[512,768]{1,0:T(8,128)(2,1)S(1)} %get-tuple-element.171.refs_2_, bf16[512,768]{1,0:T(8,128)(2,1)S(1)} %collective-permute-done.33.refs_3_, bf16[512,768]{1,0:T(8,128)(2,1)S(1)} %collective-permute-done.34.refs_4_, ...), custom_call_target="tpu_custom_call" | custom-call | flops 10000000 | bytes 1024 | tf_op jit(solution)/shard_map/last/pallas_call | solution.py:498
  238.0 2.1 collective-permute-done.43
  (232 shorter events, 69.6 us)
Async XLA Ops:
  7.2 80.7 %all-gather.2.cloned.1.call-start = ((), (), s32[]{:S(2)}) async-start(), calls=%async_computation.1 | async-start | bytes 2654208 | tf_op jit(solution)/shard_map/all_gather | solution.py:971
  8.3 17.0 %collective-permute-start.7 = (bf16[96,768]{1,0:T(8,128)(2,1)S(1)}, bf16[96,768]{1,0:T(8,128)(2,1)S(1)}, u32[]{:S(2)}, u32[]{:S(2)}) collective-permute-start(bf16[96,768]{1,0:T(8,128)(2,1)S(1)} %pad_maximum_fusion.4.rest_0_), channel_id=1, source_target_pairs={{0,24},{4,28},{8,16},{12,20},{16,8},{20,12},{24,0},{28,4},{1,25},{... | collective-permute-start | bytes 442376 | tf_op jit(solution)/shard_map/ppermute | solution.py:937
  13.4 12.5 %collective-permute-start.5 = (bf16[96,768]{1,0:T(8,128)(2,1)S(1)}, bf16[96,768]{1,0:T(8,128)(2,1)S(1)}, u32[]{:S(2)}, u32[]{:S(2)}) collective-permute-start(bf16[96,768]{1,0:T(8,128)(2,1)S(1)} %pad_maximum_fusion.4.rest_0_), channel_id=1, source_target_pairs={{0,16},{4,20},{8,24},{12,28},{16,0},{20,4},{24,8},{28,12},{1,17},{... | collective-permute-start | bytes 442376 | tf_op jit(solution)/shard_map/ppermute | solution.py:937
  13.4 11.5 %collective-permute-start.3 = (bf16[96,768]{1,0:T(8,128)(2,1)S(1)}, bf16[96,768]{1,0:T(8,128)(2,1)S(1)}, u32[]{:S(2)}, u32[]{:S(2)}) collective-permute-start(bf16[96,768]{1,0:T(8,128)(2,1)S(1)} %pad_maximum_fusion.4.rest_0_), channel_id=1, source_target_pairs={{0,8},{4,12},{8,0},{12,4},{16,24},{20,28},{24,16},{28,20},{1,9},{5... | collective-permute-start | bytes 442376 | tf_op jit(solution)/shard_map/ppermute | solution.py:937
  14.1 13.9 %collective-permute-start = (bf16[96,768]{1,0:T(8,128)(2,1)S(1)}, bf16[96,768]{1,0:T(8,128)(2,1)S(1)}, u32[]{:S(2)}, u32[]{:S(2)}) collective-permute-start(bf16[96,768]{1,0:T(8,128)(2,1)S(1)} %pad_maximum_fusion.4.rest_0_), channel_id=1, source_target_pairs={{0,4},{4,0},{8,12},{12,8},{16,20},{20,16},{24,28},{28,24},{1,5},{5... | collective-permute-start | bytes 442376 | tf_op jit(solution)/shard_map/ppermute | solution.py:937
  15.7 20.3 %collective-permute-start.2 = (bf16[512,768]{1,0:T(8,128)(2,1)}, bf16[512,768]{1,0:T(8,128)(2,1)}, u32[]{:S(2)}, u32[]{:S(2)}) collective-permute-start(bf16[512,768]{1,0:T(8,128)(2,1)} %refs_0_.5), channel_id=1, source_target_pairs={{0,2},{1,3},{2,0},{3,1},{4,6},{5,7},{6,4},{7,5},{8,10},{9,11},{10,... | collective-permute-start | bytes 2359304 | tf_op jit(solution)/shard_map/ppermute | solution.py:934
  25.9 8.6 %collective-permute-start.6 = (bf16[96,768]{1,0:T(8,128)(2,1)S(1)}, bf16[96,768]{1,0:T(8,128)(2,1)S(1)}, u32[]{:S(2)}, u32[]{:S(2)}) collective-permute-start(bf16[96,768]{1,0:T(8,128)(2,1)S(1)} %collective-permute-done.5.rest_4_), channel_id=1, source_target_pairs={{0,4},{4,0},{8,12},{12,8},{16,20},{20,16},{24,28},{28,24},{1,5},{5... | collective-permute-start | bytes 442376 | tf_op jit(solution)/shard_map/ppermute | solution.py:937
  27.4 8.6 %collective-permute-start.4 = (bf16[96,768]{1,0:T(8,128)(2,1)S(1)}, bf16[96,768]{1,0:T(8,128)(2,1)S(1)}, u32[]{:S(2)}, u32[]{:S(2)}) collective-permute-start(bf16[96,768]{1,0:T(8,128)(2,1)S(1)} %collective-permute-done.3.rest_2_), channel_id=1, source_target_pairs={{0,4},{4,0},{8,12},{12,8},{16,20},{20,16},{24,28},{28,24},{1,5},{5... | collective-permute-start | bytes 442376 | tf_op jit(solution)/shard_map/ppermute | solution.py:937
  28.0 10.3 %collective-permute-start.1 = (bf16[512,768]{1,0:T(8,128)(2,1)S(1)}, bf16[512,768]{1,0:T(8,128)(2,1)}, u32[]{:S(2)}, u32[]{:S(2)}) collective-permute-start(bf16[512,768]{1,0:T(8,128)(2,1)S(1)} %copy-done.1), channel_id=1, source_target_pairs={{0,1},{1,0},{2,3},{3,2},{4,5},{5,4},{6,7},{7,6},{8,9},{9,8},{10,11... | collective-permute-start | bytes 2359304 | tf_op jit(solution)/shard_map/ppermute | solution.py:931
  36.1 196.6 %reduce-scatter.2.cloned.1.call-start = ((), (), s32[]{:S(2)}) async-start(), calls=%async_computation.2 | async-start | bytes 2654208 | tf_op jit(solution)/shard_map/reduce_scatter | solution.py:1008
  37.3 20.6 %collective-permute-start.10 = (bf16[512,768]{1,0:T(8,128)(2,1)}, bf16[512,768]{1,0:T(8,128)(2,1)S(1)}, u32[]{:S(2)}, u32[]{:S(2)}) collective-permute-start(bf16[512,768]{1,0:T(8,128)(2,1)} %refs_0_.4), channel_id=1, source_target_pairs={{0,2},{1,3},{2,0},{3,1},{4,6},{5,7},{6,4},{7,5},{8,10},{9,11},{10,... | collective-permute-start | bytes 2359304 | tf_op jit(solution)/shard_map/ppermute | solution.py:934
  48.2 15.1 %collective-permute-start.11 = (bf16[192,768]{1,0:T(8,128)(2,1)}, bf16[192,768]{1,0:T(8,128)(2,1)S(1)}, u32[]{:S(2)}, u32[]{:S(2)}) collective-permute-start(bf16[192,768]{1,0:T(8,128)(2,1)} %get-tuple-element.111.wm), channel_id=1, source_target_pairs={{0,2},{1,3},{2,0},{3,1},{4,6},{5,7},{6,4},{7,5},{8,10},{9,11},{10,... | collective-permute-start | bytes 884744 | tf_op jit(solution)/shard_map/ppermute | solution.py:934
  63.3 10.2 %collective-permute-start.12 = (bf16[192,1024]{1,0:T(8,128)(2,1)S(1)}, bf16[192,1024]{1,0:T(8,128)(2,1)S(1)}, u32[]{:S(2)}, u32[]{:S(2)}) collective-permute-start(bf16[192,1024]{1,0:T(8,128)(2,1)S(1)} %get-tuple-element.112.ot), channel_id=1, source_target_pairs={{0,2},{1,3},{2,0},{3,1},{4,6},{5,7},{6,4},{7,5},{8,10},{9,11},{10,... | collective-permute-start | bytes 1179656 | tf_op jit(solution)/shard_map/ppermute | solution.py:934
  82.2 17.6 %collective-permute-start.19 = (bf16[512,768]{1,0:T(8,128)(2,1)S(1)}, bf16[512,768]{1,0:T(8,128)(2,1)}, u32[]{:S(2)}, u32[]{:S(2)}) collective-permute-start(bf16[512,768]{1,0:T(8,128)(2,1)S(1)} %collective-permute-done.10.ya.refs_8_), channel_id=1, source_target_pairs={{0,1},{1,0},{2,3},{3,2},{4,5},{5,4},{6,7},{7,6},{8,9},{9,8},{10,11... | collective-permute-start | bytes 2359304 | tf_op jit(solution)/shard_map/ppermute | solution.py:931
  82.6 15.5 %collective-permute-start.17 = (bf16[256,768]{1,0:T(8,128)(2,1)}, bf16[256,768]{1,0:T(8,128)(2,1)S(1)}, u32[]{:S(2)}, u32[]{:S(2)}) collective-permute-start(bf16[256,768]{1,0:T(8,128)(2,1)} %get-tuple-element.121), channel_id=1, source_target_pairs={{0,2},{1,3},{2,0},{3,1},{4,6},{5,7},{6,4},{7,5},{8,10},{9,11},{10,... | collective-permute-start | bytes 1179656 | tf_op jit(solution)/shard_map/ppermute | solution.py:934
  98.2 11.5 %collective-permute-start.16 = (bf16[256,768]{1,0:T(8,128)(2,1)S(1)}, bf16[256,768]{1,0:T(8,128)(2,1)S(1)}, u32[]{:S(2)}, u32[]{:S(2)}) collective-permute-start(bf16[256,768]{1,0:T(8,128)(2,1)S(1)} %copy-done.39), channel_id=1, source_target_pairs={{0,2},{1,3},{2,0},{3,1},{4,6},{5,7},{6,4},{7,5},{8,10},{9,11},{10,... | collective-permute-start | bytes 1179656 | tf_op jit(solution)/shard_map/ppermute | solution.py:934
  109.8 11.6 %collective-permute-start.22 = (bf16[256,768]{1,0:T(8,128)(2,1)S(1)}, bf16[256,768]{1,0:T(8,128)(2,1)S(1)}, u32[]{:S(2)}, u32[]{:S(2)}) collective-permute-start(bf16[256,768]{1,0:T(8,128)(2,1)S(1)} %add_convert_fusion.4), channel_id=1, source_target_pairs={{0,2},{1,3},{2,0},{3,1},{4,6},{5,7},{6,4},{7,5},{8,10},{9,11},{10,... | collective-permute-start | bytes 1179656 | tf_op jit(solution)/shard_map/ppermute | solution.py:934
  121.4 14.7 %collective-permute-start.25 = (bf16[512,768]{1,0:T(8,128)(2,1)}, bf16[512,768]{1,0:T(8,128)(2,1)}, u32[]{:S(2)}, u32[]{:S(2)}) collective-permute-start(bf16[512,768]{1,0:T(8,128)(2,1)} %get-tuple-element.137), channel_id=1, source_target_pairs={{0,1},{1,0},{2,3},{3,2},{4,5},{5,4},{6,7},{7,6},{8,9},{9,8},{10,11... | collective-permute-start | bytes 2359304 | tf_op jit(solution)/shard_map/ppermute | solution.py:931
  124.6 14.1 %collective-permute-start.27 = (bf16[256,768]{1,0:T(8,128)(2,1)}, bf16[256,768]{1,0:T(8,128)(2,1)}, u32[]{:S(2)}, u32[]{:S(2)}) collective-permute-start(bf16[256,768]{1,0:T(8,128)(2,1)} %add_convert_fusion.3), channel_id=1, source_target_pairs={{0,2},{1,3},{2,0},{3,1},{4,6},{5,7},{6,4},{7,5},{8,10},{9,11},{10,... | collective-permute-start | bytes 1179656 | tf_op jit(solution)/shard_map/ppermute | solution.py:934
  126.1 12.5 %collective-permute-start.24 = (bf16[512,768]{1,0:T(8,128)(2,1)}, bf16[512,768]{1,0:T(8,128)(2,1)}, u32[]{:S(2)}, u32[]{:S(2)}) collective-permute-start(bf16[512,768]{1,0:T(8,128)(2,1)} %get-tuple-element.134), channel_id=1, source_target_pairs={{0,1},{1,0},{2,3},{3,2},{4,5},{5,4},{6,7},{7,6},{8,9},{9,8},{10,11... | collective-permute-start | bytes 2359304 | tf_op jit(solution)/shard_map/ppermute | solution.py:931
  126.1 12.5 %collective-permute-start.26 = (bf16[512,768]{1,0:T(8,128)(2,1)}, bf16[512,768]{1,0:T(8,128)(2,1)}, u32[]{:S(2)}, u32[]{:S(2)}) collective-permute-start(bf16[512,768]{1,0:T(8,128)(2,1)} %get-tuple-element.139), channel_id=1, source_target_pairs={{0,1},{1,0},{2,3},{3,2},{4,5},{5,4},{6,7},{7,6},{8,9},{9,8},{10,11... | collective-permute-start | bytes 2359304 | tf_op jit(solution)/shard_map/ppermute | solution.py:931
  153.1 18.6 %collective-permute-start.30 = (bf16[192,1024]{1,0:T(8,128)(2,1)}, bf16[192,1024]{1,0:T(8,128)(2,1)}, u32[]{:S(2)}, u32[]{:S(2)}) collective-permute-start(bf16[192,1024]{1,0:T(8,128)(2,1)} %get-tuple-element.149), channel_id=1, source_target_pairs={{0,2},{1,3},{2,0},{3,1},{4,6},{5,7},{6,4},{7,5},{8,10},{9,11},{10,... | collective-permute-start | bytes 1179656 | tf_op jit(solution)/shard_map/ppermute | solution.py:934
  153.6 18.1 %collective-permute-start.31 = (bf16[192,768]{1,0:T(8,128)(2,1)}, bf16[192,768]{1,0:T(8,128)(2,1)}, u32[]{:S(2)}, u32[]{:S(2)}) collective-permute-start(bf16[192,768]{1,0:T(8,128)(2,1)} %get-tuple-element.159), channel_id=1, source_target_pairs={{0,2},{1,3},{2,0},{3,1},{4,6},{5,7},{6,4},{7,5},{8,10},{9,11},{10,... | collective-permute-start | bytes 884744 | tf_op jit(solution)/shard_map/ppermute | solution.py:934
  155.1 32.6 %collective-permute-start.29 = (bf16[512,768]{1,0:T(8,128)(2,1)}, bf16[512,768]{1,0:T(8,128)(2,1)}, u32[]{:S(2)}, u32[]{:S(2)}) collective-permute-start(bf16[512,768]{1,0:T(8,128)(2,1)} %add_convert_fusion.2), channel_id=1, source_target_pairs={{0,2},{1,3},{2,0},{3,1},{4,6},{5,7},{6,4},{7,5},{8,10},{9,11},{10,... | collective-permute-start | bytes 2359304 | tf_op jit(solution)/shard_map/ppermute | solution.py:934
  187.7 22.8 %collective-permute-start.32 = (bf16[512,768]{1,0:T(8,128)(2,1)S(1)}, bf16[512,768]{1,0:T(8,128)(2,1)S(1)}, u32[]{:S(2)}, u32[]{:S(2)}) collective-permute-start(bf16[512,768]{1,0:T(8,128)(2,1)S(1)} %get-tuple-element.165), channel_id=1, source_target_pairs={{0,1},{1,0},{2,3},{3,2},{4,5},{5,4},{6,7},{7,6},{8,9},{9,8},{10,11... | collective-permute-start | bytes 2359304 | tf_op jit(solution)/shard_map/ppermute | solution.py:931
  187.7 17.4 %collective-permute-start.35 = (bf16[104,768]{1,0:T(8,128)(2,1)S(1)}, bf16[104,768]{1,0:T(8,128)(2,1)S(1)}, u32[]{:S(2)}, u32[]{:S(2)}) collective-permute-start(bf16[104,768]{1,0:T(8,128)(2,1)S(1)} %get-tuple-element.175), channel_id=1, source_target_pairs={{0,4},{4,0},{8,12},{12,8},{16,20},{20,16},{24,28},{28,24},{1,5},{5... | collective-permute-start | bytes 479240 | tf_op jit(solution)/shard_map/ppermute | solution.py:937
  200.2 8.4 %collective-permute-start.37 = (bf16[104,768]{1,0:T(8,128)(2,1)S(1)}, bf16[104,768]{1,0:T(8,128)(2,1)S(1)}, u32[]{:S(2)}, u32[]{:S(2)}) collective-permute-start(bf16[104,768]{1,0:T(8,128)(2,1)S(1)} %get-tuple-element.181), channel_id=1, source_target_pairs={{0,4},{4,0},{8,12},{12,8},{16,20},{20,16},{24,28},{28,24},{1,5},{5... | collective-permute-start | bytes 479240 | tf_op jit(solution)/shard_map/ppermute | solution.py:937
  205.1 10.0 %collective-permute-start.36 = (bf16[104,768]{1,0:T(8,128)(2,1)S(1)}, bf16[104,768]{1,0:T(8,128)(2,1)S(1)}, u32[]{:S(2)}, u32[]{:S(2)}) collective-permute-start(bf16[104,768]{1,0:T(8,128)(2,1)S(1)} %get-tuple-element.176), channel_id=1, source_target_pairs={{0,4},{4,0},{8,12},{12,8},{16,20},{20,16},{24,28},{28,24},{1,5},{5... | collective-permute-start | bytes 479240 | tf_op jit(solution)/shard_map/ppermute | solution.py:937
  210.7 18.5 %collective-permute-start.34 = (bf16[512,768]{1,0:T(8,128)(2,1)S(1)}, bf16[512,768]{1,0:T(8,128)(2,1)S(1)}, u32[]{:S(2)}, u32[]{:S(2)}) collective-permute-start(bf16[512,768]{1,0:T(8,128)(2,1)S(1)} %add_convert_fusion.1), channel_id=1, source_target_pairs={{0,2},{1,3},{2,0},{3,1},{4,6},{5,7},{6,4},{7,5},{8,10},{9,11},{10,... | collective-permute-start | bytes 2359304 | tf_op jit(solution)/shard_map/ppermute | solution.py:934
  215.2 19.3 %collective-permute-start.39 = (bf16[104,768]{1,0:T(8,128)(2,1)S(1)}, bf16[104,768]{1,0:T(8,128)(2,1)S(1)}, u32[]{:S(2)}, u32[]{:S(2)}) collective-permute-start(bf16[104,768]{1,0:T(8,128)(2,1)S(1)} %pad_maximum_fusion.1), channel_id=1, source_target_pairs={{0,8},{4,12},{8,0},{12,4},{16,24},{20,28},{24,16},{28,20},{1,9},{5... | collective-permute-start | bytes 479240 | tf_op jit(solution)/shard_map/ppermute | solution.py:937
  216.5 18.0 %collective-permute-start.40 = (bf16[104,768]{1,0:T(8,128)(2,1)S(1)}, bf16[104,768]{1,0:T(8,128)(2,1)S(1)}, u32[]{:S(2)}, u32[]{:S(2)}) collective-permute-start(bf16[104,768]{1,0:T(8,128)(2,1)S(1)} %pad_maximum_fusion.2), channel_id=1, source_target_pairs={{0,16},{4,20},{8,24},{12,28},{16,0},{20,4},{24,8},{28,12},{1,17},{... | collective-permute-start | bytes 479240 | tf_op jit(solution)/shard_map/ppermute | solution.py:937
  218.6 15.9 %collective-permute-start.41 = (bf16[104,768]{1,0:T(8,128)(2,1)S(1)}, bf16[104,768]{1,0:T(8,128)(2,1)S(1)}, u32[]{:S(2)}, u32[]{:S(2)}) collective-permute-start(bf16[104,768]{1,0:T(8,128)(2,1)S(1)} %pad_maximum_fusion.3), channel_id=1, source_target_pairs={{0,24},{4,28},{8,16},{12,20},{16,8},{20,12},{24,0},{28,4},{1,25},{... | collective-permute-start | bytes 479240 | tf_op jit(solution)/shard_map/ppermute | solution.py:937
  (70 other events, 615.2 us)
Sparse Core Ops, SparseCore 0:
  36.2 51.6 all-gather.1
  143.9 69.8 reduce-scatter.1
where the time goes:
time: 248 us
  Pallas kernels  96.5 us (39%)
  waiting for transfers between devices  54.3 us (22%)
  starting transfers between devices  49.4 us (20%)
  local copies, waits for them, and re-layouts  19.3 us (8%)
  between operations  15.5 us (6%)
  other arithmetic  12.6 us (5%)
    ppermute x14, starting transfers between devices, far(): return lax.ppermute(v, 'dp', [(i, i ^ k) for i in range(dp)])  31 us
    ppermute x13, waiting for transfers between devices, across(): return lax.ppermute(v, 'mp', [(i, i ^ 2) for i in range(mp)])  24.8 us
    pallas_call x3, Pallas kernels, mlp_both(): pl.pallas_call(functools.partial(mlp_kernel, at, len(into)), in_specs=[AN...  22.7 us
    ppermute x14, waiting for transfers between devices, far(): return lax.ppermute(v, 'dp', [(i, i ^ k) for i in range(dp)])  17.1 us
    unnamed x117, local copies, waits for them, and re-layouts  16.2 us
    ppermute x13, starting transfers between devices, across(): return lax.ppermute(v, 'mp', [(i, i ^ 2) for i in range(mp)])  15.8 us
    pallas_call x1, Pallas kernels, first_back(): pl.pallas_call(functools.partial(first_back_kernel, total // 4 // BLK), g...  13.3 us
    pallas_call x1, Pallas kernels, second_back(): pl.pallas_call(functools.partial(second_back_kernel, total // 4 // BLK, p...  13 us
  transfers between devices with their start and end apart: 46, of which 23 were waited for; matrix products, arithmetic and copies ran while one was open for 7% of the time, Pallas kernels for 37%

commit v1 on v0

--- a/solution.py
+++ b/solution.py
@@ -933,6 +933,9 @@
     def across(v):
         return lax.ppermute(v, "mp", [(i, i ^ 2) for i in range(mp)])
 
+    def core_across(v):
+        return lax.ppermute(v, "mp", [(i, i ^ 3) for i in range(mp)])
+
     def far(v, k):
         return lax.ppermute(v, "dp", [(i, i ^ k) for i in range(dp)])
 
@@ -962,7 +965,8 @@
     w_mlp = jnp.concatenate([w_gate, w_up, w_down], axis=1)
     if direct:
         near = [w_attn] + [far(w_attn, k) for k in range(2, dp, 2)]
-        near[1] = after(near[1], sc, gkv, w_mlp)
+        middle_way = len(near) // 2
+        near[middle_way] = after(near[middle_way], sc, gkv, w_mlp)
         w_pieces = [p for v in near for p in (v, far(v, 1))]
         tok1 = core(after(tokens, w_pieces[1]))
     else:
@@ -1006,20 +1010,20 @@
         (after(hid_o, d_sum), hid_a, hid_b),
     )
     mlp_grads = lax.psum_scatter(mlp_all, "dp", scatter_dimension=0, tiled=True)
-    m_sum, m_core = summed(after(m2, d_sum), core(m3)), core(after(m1, d_sum))
+    m_other, m_core = core(m3), core(after(m1, d_sum))
     dh1, da, gain_m_part = middle_back(
         dy0,
         h1,
         d0,
         core(after(d1, d_sum)),
-        (dx_a, after(dx_b, mlp_all, m_sum, m_core)),
+        (dx_a, after(dx_b, mlp_all, m_other, m_core)),
         gain_m,
     )
 
     do_own, do_send, go, go_send = out_back(da, core(da), wo, wo_x, o_own, o_x)
     do_far = across(do_send)
     go_x = across(go_send)
-    m_x = across(after(m_sum, do_send))
+    m_x = across(after(summed(after(m2, da), m_other), do_send))
     dq_own, dk, dv = first_back(sc, qkvt, kn, vn, do_own, o_own, lse_own, gq, gkv)
     r2, r3, dk_own, dv_own, *grads = second_back(
         dp if direct else 1,
@@ -1031,15 +1035,15 @@
     depth = w_query.shape[0]
     parts = []
     if direct:
-        others = {}
         for k in range(dp - 2, -1, -2):
             sent = grads[k + 1]
-            others[k] = far(after(sent, others[k + dp // 2]) if k + dp // 2 in others else sent, 1)
-        for k in range(0, dp, 2):
-            near, other = grads[k], after(others[k], r_sum)
+            if k < dp // 2 and parts:
+                sent = after(sent, parts[k // 2 - dp // 4])
+            near, other = grads[k], after(far(sent, 1), r_sum)
             both = summed(near[:depth], other[:depth])
             part = jnp.concatenate([both, near[depth : depth + 4], other[depth : depth + 4]], axis=0)
-            parts.append(part if k == 0 else far(part, k))
+            parts.insert(0, part)
+        parts = [part if k == 0 else far(part, 2 * k) for k, part in enumerate(parts)]
     r0, r1 = rows_back(after(dk_own, r_sum), dq_own, dv_own, wt)
     grad_tokens = last(tokens, dh1, r0, core(r1), r_x, gain_a)
     output = (
@@ -1052,8 +1056,7 @@
     if direct:
         parts[0] = after(parts[0], grad_tokens, output, grad_gate)
         grad_k, grad_q, grad_v, grad_o, gains = grads_sum(parts)
-        gains = gains + core(gains)
-        gains = gains + across(gains)
+        gains = gains + core(gains) + across(gains) + core_across(gains)
     else:
         width = tokens.shape[1]
         attn_grads = lax.psum_scatter(

time: 248 us -> 246 us (level)
  Pallas kernels: 96.5 us -> 108 us
  waiting for transfers between devices: 54.3 us -> 43.5 us
    ppermute x13, waiting for transfers between devices: 24.8 us -> 13.8 us  [across(): return lax.ppermute(v, 'mp', [(i, i ^ 2) for i in range(mp)])]
    ppermute x17, waiting for transfers between devices: 8.85 us -> 4.29 us  [core(): return lax.ppermute(v, 'mp', [(i, i ^ 1) for i in range(mp)])]
    pallas_call x2, Pallas kernels: 10.5 us -> 14.7 us  [attention(): pl.pallas_call(functools.partial(forward_kernel, half, per), grid=(blocks...]
    pallas_call x1, Pallas kernels: 13 us -> 17.1 us  [second_back(): pl.pallas_call(functools.partial(second_back_kernel, total // 4 // BLK, p...]
    ppermute x14, starting transfers between devices: 31 us -> 27.4 us  [far(): return lax.ppermute(v, 'dp', [(i, i ^ k) for i in range(dp)])]
    ppermute x14, waiting for transfers between devices: 17.1 us -> 20.2 us  [far(): return lax.ppermute(v, 'dp', [(i, i ^ k) for i in range(dp)])]
    pallas_call x1, Pallas kernels: 13.3 us -> 16 us  [first_back(): pl.pallas_call(functools.partial(first_back_kernel, total // 4 // BLK), g...]
  transfers between devices with their start and end apart: 46 -> 47, of which waited for: 23 -> 20; matrix products, arithmetic and copies ran while one was open for 7% -> 7% of each run, Pallas kernels for 37% -> 42%
where the time goes in v1:
time: 246 us; the launch traced here: 245 us
  Pallas kernels  108 us (44%)
  starting transfers between devices  47.9 us (19%)
  waiting for transfers between devices  43.5 us (18%)
  local copies, waits for them, and re-layouts  18.1 us (7%)
  between operations  15.6 us (6%)
  other arithmetic  12.2 us (5%)
    ppermute x14, starting transfers between devices, far(): return lax.ppermute(v, 'dp', [(i, i ^ k) for i in range(dp)])  27.4 us
    pallas_call x3, Pallas kernels, mlp_both(): pl.pallas_call(functools.partial(mlp_kernel, at, len(into)), in_specs=[AN...  22.8 us
    ppermute x14, waiting for transfers between devices, far(): return lax.ppermute(v, 'dp', [(i, i ^ k) for i in range(dp)])  20.2 us
    pallas_call x1, Pallas kernels, second_back(): pl.pallas_call(functools.partial(second_back_kernel, total // 4 // BLK, p...  17.1 us
    ppermute x13, starting transfers between devices, across(): return lax.ppermute(v, 'mp', [(i, i ^ 2) for i in range(mp)])  16.8 us
    pallas_call x1, Pallas kernels, first_back(): pl.pallas_call(functools.partial(first_back_kernel, total // 4 // BLK), g...  16 us
    unnamed x117, local copies, waits for them, and re-layouts  14.9 us
    pallas_call x2, Pallas kernels, attention(): pl.pallas_call(functools.partial(forward_kernel, half, per), grid=(blocks...  14.7 us
  transfers between devices with their start and end apart: 47, of which 20 were waited for; matrix products, arithmetic and copies ran while one was open for 7% of the time, Pallas kernels for 42%

profile of v1, /device:TPU:0, one launch (start us, length us, event | category | flops | bytes accessed | tf_op | source)
XLA Modules:
  0.0 245.0 jit_solution(8694869177882833623)
XLA Ops:
  8.3 5.1 %collective-permute-start.7 = (bf16[96,768]{1,0:T(8,128)(2,1)S(1)}, bf16[96,768]{1,0:T(8,128)(2,1)S(1)}, u32[]{:S(2)}, u32[]{:S(2)}) collective-permute-start(bf16[96,768]{1,0:T(8,128)(2,1)S(1)} %pad_maximum_fusion.4.rest_0_), channel_id=1, source_target_pairs={{0,24},{4,28},{8,16},{12,20},{16,8},{20,12},{24,0},{28,4},{1,25},{... | collective-permute-start | bytes 442376 | tf_op jit(solution)/shard_map/ppermute | solution.py:940
  30.0 3.1 %collective-permute-done.8.rest_7_ = bf16[96,768]{1,0:T(8,128)(2,1)S(1)} collective-permute-done((bf16[96,768]{1,0:T(8,128)(2,1)S(1)}, bf16[96,768]{1,0:T(8,128)(2,1)S(1)}, u32[]{:S(2)}, u32[]{:S(2)}) %collective-permute-start.8) | collective-permute-done | bytes 147488 | tf_op jit(solution)/shard_map/ppermute | solution.py:940
  33.1 2.9 %collective-permute-done.4.rest_3_ = bf16[96,768]{1,0:T(8,128)(2,1)S(1)} collective-permute-done((bf16[96,768]{1,0:T(8,128)(2,1)S(1)}, bf16[96,768]{1,0:T(8,128)(2,1)S(1)}, u32[]{:S(2)}, u32[]{:S(2)}) %collective-permute-start.4) | collective-permute-done | bytes 147488 | tf_op jit(solution)/shard_map/ppermute | solution.py:940
  40.3 9.5 %qkv.1 = (bf16[2048,768]{1,0:T(8,128)(2,1)}, bf16[576,2048]{1,0:T(8,128)(2,1)}, bf16[2048,192]{1,0:T(8,128)(2,1)}, bf16[2048,192]{1,0:T(8,128)(2,1)}, bf16[576,7...) custom-call(s32[24]{0:T(128)} %concatenate.21.sc, bf16[512,768]{1,0:T(8,128)(2,1)} %refs_0_.5, ...), custom_call_target="tpu_custom_call" | custom-call | flops 10000000 | bytes 1024 | tf_op jit(solution)/shard_map/qkv/pallas_call | solution.py:88
  51.2 1.7 copy-done
  54.1 7.0 %attention.2 = (bf16[192,1024]{1,0:T(8,128)(2,1)S(1)}, f32[8,1024]{1,0:T(8,128)S(1)}) custom-call(s32[24]{0:T(128)S(1)} %copy-done.29, bf16[576,2048]{1,0:T(8,128)(2,1)S(1)} %copy-done, bf16[2048,192]{1,0:T(8,128)(2,1)S(1)} %copy-done.16, bf16[576,2048]{1,0:T(8,128)(2,1)S(1)} %copy-done, s32[1,2048]{1,0:T(1,128)S(1)} %copy-done.22, ...), custom_call_target="tpu_custom_call" | custom-call | flops 12000000000 | bytes 1024 | tf_op jit(solution)/shard_map/attention/pallas_call | solution.py:207
  61.1 3.6 %collective-permute-done.11.wx = bf16[192,768]{1,0:T(8,128)(2,1)S(1)} collective-permute-done((bf16[192,768]{1,0:T(8,128)(2,1)}, bf16[192,768]{1,0:T(8,128)(2,1)S(1)}, u32[]{:S(2)}, u32[]{:S(2)}) %collective-permute-start.11) | collective-permute-done | bytes 294944 | tf_op jit(solution)/shard_map/ppermute | solution.py:934
  66.3 7.8 %attention.3 = (bf16[192,1024]{1,0:T(8,128)(2,1)S(1)}, f32[8,1024]{1,0:T(8,128)S(1)}) custom-call(s32[24]{0:T(128)S(1)} %copy-done.29, bf16[576,2048]{1,0:T(8,128)(2,1)S(1)} %copy-done, bf16[2048,192]{1,0:T(8,128)(2,1)S(1)} %copy-done.16, bf16[576,2048]{1,0:T(8,128)(2,1)S(1)} %copy-done, s32[1,2048]{1,0:T(1,128)S(1)} %copy-done.22, ...), custom_call_target="tpu_custom_call" | custom-call | flops 12000000000 | bytes 1024 | tf_op jit(solution)/shard_map/attention/pallas_call | solution.py:207
  74.9 2.1 out_projection.1
  77.6 1.9 collective-permute-done.13.refs_2_
  79.5 2.4 middle.1
  86.0 3.9 %all-gather.2.cloned.1.call-done.w = bf16[768,1536]{1,0:T(8,128)(2,1)} async-done(((bf16[96,1536]{1,0:T(8,128)(2,1)}), bf16[768,1536]{1,0:T(8,128)(2,1)}) %all-gather.2.cloned.1.call-update) | async-done | bytes 2359312 | tf_op jit(solution)/shard_map/all_gather | solution.py:975
  89.9 10.2 %mlp.3 = (bf16[512,768]{1,0:T(8,128)(2,1)}, bf16[512,768]{1,0:T(8,128)(2,1)}, bf16[512,768]{1,0:T(8,128)(2,1)}, bf16[512,768]{1,0:T(8,128)(2,1)}, bf16[1024,512]{1,0:T(8,128)(2,1)}, /*index=5*/bf16[1024,1024]{1,0:T(8,128)(2,1)}) custom-call(bf16[512,768]{1,0:T(8,128)(2,1)} %copy-done.34, bf16[512,768]{1,0:T(8,128)(2,1)} %collective-permute-done.14.nb.refs_1_, ...), custom_call_target="tpu_custom_call" | custom-call | flops 8000000000 | bytes 1024 | tf_op jit(solution)/shard_map/mlp/pallas_call | solution.py:649
  103.7 6.3 %mlp.4 = (bf16[512,768]{1,0:T(8,128)(2,1)S(1)}, bf16[512,768]{1,0:T(8,128)(2,1)}, bf16[256,768]{1,0:T(8,128)(2,1)S(1)}, bf16[256,768]{1,0:T(8,128)(2,1)S(1)}, bf...) custom-call(bf16[256,768]{1,0:T(8,128)(2,1)S(1)} %collective-permute-done.17.na.refs_2_, ...), custom_call_target="tpu_custom_call" | custom-call | flops 8000000000 | bytes 1024 | tf_op jit(solution)/shard_map/mlp/pallas_call | solution.py:649
  113.5 6.3 %mlp.5 = (bf16[512,768]{1,0:T(8,128)(2,1)S(1)}, bf16[512,768]{1,0:T(8,128)(2,1)}, bf16[256,768]{1,0:T(8,128)(2,1)S(1)}, bf16[256,768]{1,0:T(8,128)(2,1)S(1)}, bf...) custom-call(bf16[256,768]{1,0:T(8,128)(2,1)S(1)} %collective-permute-done., ...), custom_call_target="tpu_custom_call", output_to_operand_aliasing={{0}: (5, {}), {1}: (6, {})} | custom-call | flops 8000000000 | bytes 1024 | tf_op jit(solution)/shard_map/mlp/pallas_call | solution.py:649
  120.8 2.7 %collective-permute-done.22.refs_4_ = bf16[256,768]{1,0:T(8,128)(2,1)S(1)} collective-permute-done((bf16[256,768]{1,0:T(8,128)(2,1)S(1)}, bf16[256,768]{1,0:T(8,128)(2,1)S(1)}, u32[]{:S(2)}, u32[]{:S(2)}) %collective-permute-start.22) | collective-permute-done | bytes 393248 | tf_op jit(solution)/shard_map/ppermute | solution.py:934
  124.0 1.7 collective-permute-done.23
  128.6 9.6 %mlp_weights.1 = bf16[768,1536]{1,0:T(8,128)(2,1)} custom-call(bf16[512,768]{1,0:T(8,128)(2,1)S(1)} %copy-done.35, bf16[512,768]{1,0:T(8,128)(2,1)} %collective-permute-done.14.nb.refs_1_, bf16[256,768]{1,0:T(8,128)(2,1)S(1)} %copy-done.37, bf16[256,768]{1,0:T(8,128)(2,1)S(1)} %collective-permute-done.18.nb.refs_3_, ...), custom_call_target="tpu_custom_call" | custom-call | flops 10000000000 | bytes 1024 | tf_op jit(solution)/shard_map/mlp_weights/pallas_call | solution.py:736
  138.3 3.3 %middle_back.1 = (f32[512,768]{1,0:T(8,128)S(1)}, bf16[512,768]{1,0:T(8,128)(2,1)}, f32[32,768]{1,0:T(8,128)S(1)}) custom-call(bf16[512,768]{1,0:T(8,128)(2,1)} %refs_0_.4, f32[512,768]{1,0:T(8,128)S(1)} %get-tuple-element.115.refs_1_, bf16[512,768]{1,0:T(8,128)(2,1)S(1)} %copy-done.17, bf16[512,768]{1,0:T(8,128)(2,1)} %collective-permute-done.25.refs_3_, ...), custom_call_target="tpu_custom_call" | custom-call | flops 10000000 | bytes 1024 | tf_op jit(solution)/shard_map/middle_back/pallas_call | solution.py:498
  144.5 2.2 add_convert_fusion.2
  146.8 4.1 %out_back.1 = (bf16[192,1024]{1,0:T(8,128)(2,1)S(1)}, bf16[192,1024]{1,0:T(8,128)(2,1)}, f32[192,768]{1,0:T(8,128)S(1)}, bf16[192,768]{1,0:T(8,128)(2,1)}) custom-call(bf16[512,768]{1,0:T(8,128)(2,1)} %get-tuple-element.147.own, bf16[512,768]{1,0:T(8,128)(2,1)} %collective-permute-done.28.other, bf16[192,768]{1,0:T(8,128)(2,1)S(1)} %copy-done.13, ...), custom_call_target="tpu_custom_call" | custom-call | flops 10000000 | bytes 1024 | tf_op jit(solution)/shard_map/out_back/pallas_call | solution.py:818
  155.0 16.0 %attention_back.1 = (bf16[192,1024]{1,0:T(8,128)(2,1)}, f32[192,2048]{1,0:T(8,128)}, f32[192,2048]{1,0:T(8,128)}) custom-call(s32[24]{0:T(128)} %concatenate.21.sc, bf16[576,2048]{1,0:T(8,128)(2,1)} %get-tuple-element.105.qt.vt.kt, bf16[2048,192]{1,0:T(8,128)(2,1)} %get-tuple-element.106.kn, bf16[576,2048]{1,0:T(8,128)(2,1)} %get-tuple-element.105.qt.vt.kt, ...), custom_call_target="tpu_custom_call" | custom-call | flops 20000000000 | bytes 1024 | tf_op jit(solution)/shard_map/attention_back/pallas_call | solution.py:375
  172.1 17.1 %attention_back_end.1 = (bf16[512,768]{1,0:T(8,128)(2,1)S(1)}, bf16[512,768]{1,0:T(8,128)(2,1)S(1)}, bf16[192,1024]{1,0:T(8,128)(2,1)S(1)}, bf16[192,1024]{1,0:T...) custom-call(s32[24]{0:T(128)S(1)} %copy-done.30, ...), custom_call_target="tpu_custom_call" | custom-call | flops 10000000 | bytes 1024 | tf_op jit(solution)/shard_map/attention_back_end/pallas_call | solution.py:401
  189.4 7.5 %collective-permute-start.35 = (bf16[104,768]{1,0:T(8,128)(2,1)S(1)}, bf16[104,768]{1,0:T(8,128)(2,1)S(1)}, u32[]{:S(2)}, u32[]{:S(2)}) collective-permute-start(bf16[104,768]{1,0:T(8,128)(2,1)S(1)} %get-tuple-element.176), channel_id=1, source_target_pairs={{0,4},{4,0},{8,12},{12,8},{16,20},{20,16},{24,28},{28,24},{1,5},{5... | collective-permute-start | bytes 479240 | tf_op jit(solution)/shard_map/ppermute | solution.py:940
  197.1 11.1 %collective-permute-done.37 = bf16[104,768]{1,0:T(8,128)(2,1)S(1)} collective-permute-done((bf16[104,768]{1,0:T(8,128)(2,1)S(1)}, bf16[104,768]{1,0:T(8,128)(2,1)S(1)}, u32[]{:S(2)}, u32[]{:S(2)}) %collective-permute-start.37) | collective-permute-done | bytes 159776 | tf_op jit(solution)/shard_map/ppermute | solution.py:940
  209.1 3.5 %collective-permute-start.40 = (bf16[104,768]{1,0:T(8,128)(2,1)S(1)}, bf16[104,768]{1,0:T(8,128)(2,1)S(1)}, u32[]{:S(2)}, u32[]{:S(2)}) collective-permute-start(bf16[104,768]{1,0:T(8,128)(2,1)S(1)} %pad_maximum_fusion), channel_id=1, source_target_pairs={{0,16},{4,20},{8,24},{12,28},{16,0},{20,4},{24,8},{28,12},{1,17},{... | collective-permute-start | bytes 479240 | tf_op jit(solution)/shard_map/ppermute | solution.py:940
  214.6 1.9 rows_back.1
  216.6 2.8 %add_convert_fusion = bf16[512,768]{1,0:T(8,128)(2,1)} fusion(f32[512,768]{1,0:T(8,128)S(1)} %get-tuple-element.115.refs_1_, bf16[512,768]{1,0:T(8,128)(2,1)} %collective-permute-done.29, bf16[512,768]{1,0:T(8,128)(2,1)} %collective-permute-done.24, bf16[512,768]{1,0:T(8,128)(2,1)S(1)} %copy-done.44), kind=kLoop, calls=%fused_computation | loop fusion | flops 2752512 | bytes 4718592 | tf_op jit(solution)/shard_map/convert_element_type | solution.py:1051
  221.5 1.8 collective-permute-start.39
  223.4 4.4 %collective-permute-done.34.refs_4_ = bf16[512,768]{1,0:T(8,128)(2,1)S(1)} collective-permute-done((bf16[512,768]{1,0:T(8,128)(2,1)S(1)}, bf16[512,768]{1,0:T(8,128)(2,1)S(1)}, u32[]{:S(2)}, u32[]{:S(2)}) %collective-permute-start.34) | collective-permute-done | bytes 786464 | tf_op jit(solution)/shard_map/ppermute | solution.py:934
  227.8 3.4 %last.1 = bf16[512,768]{1,0:T(8,128)(2,1)} custom-call(bf16[512,768]{1,0:T(8,128)(2,1)S(1)} %copy-done.2, f32[512,768]{1,0:T(8,128)S(1)} %copy-done.6, bf16[512,768]{1,0:T(8,128)(2,1)S(1)} %get-tuple-element.171.refs_2_, bf16[512,768]{1,0:T(8,128)(2,1)S(1)} %collective-permute-done.33.refs_3_, bf16[512,768]{1,0:T(8,128)(2,1)S(1)} %collective-permute-done.34.refs_4_, ...), custom_call_target="tpu_custom_call" | custom-call | flops 10000000 | bytes 1024 | tf_op jit(solution)/shard_map/last/pallas_call | solution.py:498
  231.2 1.8 slice_convert_fusion
  (233 shorter events, 60.8 us)
Async XLA Ops:
  7.2 82.7 %all-gather.2.cloned.1.call-start = ((), (), s32[]{:S(2)}) async-start(), calls=%async_computation.1 | async-start | bytes 2654208 | tf_op jit(solution)/shard_map/all_gather | solution.py:975
  8.3 17.9 %collective-permute-start.7 = (bf16[96,768]{1,0:T(8,128)(2,1)S(1)}, bf16[96,768]{1,0:T(8,128)(2,1)S(1)}, u32[]{:S(2)}, u32[]{:S(2)}) collective-permute-start(bf16[96,768]{1,0:T(8,128)(2,1)S(1)} %pad_maximum_fusion.4.rest_0_), channel_id=1, source_target_pairs={{0,24},{4,28},{8,16},{12,20},{16,8},{20,12},{24,0},{28,4},{1,25},{... | collective-permute-start | bytes 442376 | tf_op jit(solution)/shard_map/ppermute | solution.py:940
  13.4 12.5 %collective-permute-start.5 = (bf16[96,768]{1,0:T(8,128)(2,1)S(1)}, bf16[96,768]{1,0:T(8,128)(2,1)S(1)}, u32[]{:S(2)}, u32[]{:S(2)}) collective-permute-start(bf16[96,768]{1,0:T(8,128)(2,1)S(1)} %pad_maximum_fusion.4.rest_0_), channel_id=1, source_target_pairs={{0,16},{4,20},{8,24},{12,28},{16,0},{20,4},{24,8},{28,12},{1,17},{... | collective-permute-start | bytes 442376 | tf_op jit(solution)/shard_map/ppermute | solution.py:940
  13.4 14.4 %collective-permute-start.3 = (bf16[96,768]{1,0:T(8,128)(2,1)S(1)}, bf16[96,768]{1,0:T(8,128)(2,1)S(1)}, u32[]{:S(2)}, u32[]{:S(2)}) collective-permute-start(bf16[96,768]{1,0:T(8,128)(2,1)S(1)} %pad_maximum_fusion.4.rest_0_), channel_id=1, source_target_pairs={{0,8},{4,12},{8,0},{12,4},{16,24},{20,28},{24,16},{28,20},{1,9},{5... | collective-permute-start | bytes 442376 | tf_op jit(solution)/shard_map/ppermute | solution.py:940
  14.1 15.8 %collective-permute-start = (bf16[96,768]{1,0:T(8,128)(2,1)S(1)}, bf16[96,768]{1,0:T(8,128)(2,1)S(1)}, u32[]{:S(2)}, u32[]{:S(2)}) collective-permute-start(bf16[96,768]{1,0:T(8,128)(2,1)S(1)} %pad_maximum_fusion.4.rest_0_), channel_id=1, source_target_pairs={{0,4},{4,0},{8,12},{12,8},{16,20},{20,16},{24,28},{28,24},{1,5},{5... | collective-permute-start | bytes 442376 | tf_op jit(solution)/shard_map/ppermute | solution.py:940
  15.7 21.8 %collective-permute-start.2 = (bf16[512,768]{1,0:T(8,128)(2,1)}, bf16[512,768]{1,0:T(8,128)(2,1)}, u32[]{:S(2)}, u32[]{:S(2)}) collective-permute-start(bf16[512,768]{1,0:T(8,128)(2,1)} %refs_0_.5), channel_id=1, source_target_pairs={{0,2},{1,3},{2,0},{3,1},{4,6},{5,7},{6,4},{7,5},{8,10},{9,11},{10,... | collective-permute-start | bytes 2359304 | tf_op jit(solution)/shard_map/ppermute | solution.py:934
  27.8 8.1 %collective-permute-start.4 = (bf16[96,768]{1,0:T(8,128)(2,1)S(1)}, bf16[96,768]{1,0:T(8,128)(2,1)S(1)}, u32[]{:S(2)}, u32[]{:S(2)}) collective-permute-start(bf16[96,768]{1,0:T(8,128)(2,1)S(1)} %collective-permute-done.3.rest_2_), channel_id=1, source_target_pairs={{0,4},{4,0},{8,12},{12,8},{16,20},{20,16},{24,28},{28,24},{1,5},{5... | collective-permute-start | bytes 442376 | tf_op jit(solution)/shard_map/ppermute | solution.py:940
  28.4 9.2 %collective-permute-start.6 = (bf16[96,768]{1,0:T(8,128)(2,1)S(1)}, bf16[96,768]{1,0:T(8,128)(2,1)S(1)}, u32[]{:S(2)}, u32[]{:S(2)}) collective-permute-start(bf16[96,768]{1,0:T(8,128)(2,1)S(1)} %collective-permute-done.5.rest_4_), channel_id=1, source_target_pairs={{0,4},{4,0},{8,12},{12,8},{16,20},{20,16},{24,28},{28,24},{1,5},{5... | collective-permute-start | bytes 442376 | tf_op jit(solution)/shard_map/ppermute | solution.py:940
  29.9 10.4 %collective-permute-start.1 = (bf16[512,768]{1,0:T(8,128)(2,1)S(1)}, bf16[512,768]{1,0:T(8,128)(2,1)}, u32[]{:S(2)}, u32[]{:S(2)}) collective-permute-start(bf16[512,768]{1,0:T(8,128)(2,1)S(1)} %copy-done.1), channel_id=1, source_target_pairs={{0,1},{1,0},{2,3},{3,2},{4,5},{5,4},{6,7},{7,6},{8,9},{9,8},{10,11... | collective-permute-start | bytes 2359304 | tf_op jit(solution)/shard_map/ppermute | solution.py:931
  37.6 193.6 %reduce-scatter.2.cloned.1.call-start = ((), (), s32[]{:S(2)}) async-start(), calls=%async_computation.2 | async-start | bytes 2654208 | tf_op jit(solution)/shard_map/reduce_scatter | solution.py:1012
  38.8 22.3 %collective-permute-start.10 = (bf16[512,768]{1,0:T(8,128)(2,1)}, bf16[512,768]{1,0:T(8,128)(2,1)S(1)}, u32[]{:S(2)}, u32[]{:S(2)}) collective-permute-start(bf16[512,768]{1,0:T(8,128)(2,1)} %refs_0_.4), channel_id=1, source_target_pairs={{0,2},{1,3},{2,0},{3,1},{4,6},{5,7},{6,4},{7,5},{8,10},{9,11},{10,... | collective-permute-start | bytes 2359304 | tf_op jit(solution)/shard_map/ppermute | solution.py:934
  49.8 15.0 %collective-permute-start.11 = (bf16[192,768]{1,0:T(8,128)(2,1)}, bf16[192,768]{1,0:T(8,128)(2,1)S(1)}, u32[]{:S(2)}, u32[]{:S(2)}) collective-permute-start(bf16[192,768]{1,0:T(8,128)(2,1)} %get-tuple-element.111.wm), channel_id=1, source_target_pairs={{0,2},{1,3},{2,0},{3,1},{4,6},{5,7},{6,4},{7,5},{8,10},{9,11},{10,... | collective-permute-start | bytes 884744 | tf_op jit(solution)/shard_map/ppermute | solution.py:934
  64.8 10.2 %collective-permute-start.12 = (bf16[192,1024]{1,0:T(8,128)(2,1)S(1)}, bf16[192,1024]{1,0:T(8,128)(2,1)S(1)}, u32[]{:S(2)}, u32[]{:S(2)}) collective-permute-start(bf16[192,1024]{1,0:T(8,128)(2,1)S(1)} %get-tuple-element.112.ot), channel_id=1, source_target_pairs={{0,2},{1,3},{2,0},{3,1},{4,6},{5,7},{6,4},{7,5},{8,10},{9,11},{10,... | collective-permute-start | bytes 1179656 | tf_op jit(solution)/shard_map/ppermute | solution.py:934
  77.1 8.5 %collective-permute-start.15 = (bf16[512,768]{1,0:T(8,128)(2,1)}, bf16[512,768]{1,0:T(8,128)(2,1)}, u32[]{:S(2)}, u32[]{:S(2)}) collective-permute-start(bf16[512,768]{1,0:T(8,128)(2,1)} %refs_0_.4), channel_id=1, source_target_pairs={{0,1},{1,0},{2,3},{3,2},{4,5},{5,4},{6,7},{7,6},{8,9},{9,8},{10,11... | collective-permute-start | bytes 2359304 | tf_op jit(solution)/shard_map/ppermute | solution.py:931
  83.7 18.1 %collective-permute-start.19 = (bf16[512,768]{1,0:T(8,128)(2,1)S(1)}, bf16[512,768]{1,0:T(8,128)(2,1)}, u32[]{:S(2)}, u32[]{:S(2)}) collective-permute-start(bf16[512,768]{1,0:T(8,128)(2,1)S(1)} %copy-done.33), channel_id=1, source_target_pairs={{0,1},{1,0},{2,3},{3,2},{4,5},{5,4},{6,7},{7,6},{8,9},{9,8},{10,11... | collective-permute-start | bytes 2359304 | tf_op jit(solution)/shard_map/ppermute | solution.py:931
  84.1 16.1 %collective-permute-start.17 = (bf16[256,768]{1,0:T(8,128)(2,1)}, bf16[256,768]{1,0:T(8,128)(2,1)S(1)}, u32[]{:S(2)}, u32[]{:S(2)}) collective-permute-start(bf16[256,768]{1,0:T(8,128)(2,1)} %get-tuple-element.121), channel_id=1, source_target_pairs={{0,2},{1,3},{2,0},{3,1},{4,6},{5,7},{6,4},{7,5},{8,10},{9,11},{10,... | collective-permute-start | bytes 1179656 | tf_op jit(solution)/shard_map/ppermute | solution.py:934
  100.3 11.5 %collective-permute-start.16 = (bf16[256,768]{1,0:T(8,128)(2,1)S(1)}, bf16[256,768]{1,0:T(8,128)(2,1)S(1)}, u32[]{:S(2)}, u32[]{:S(2)}) collective-permute-start(bf16[256,768]{1,0:T(8,128)(2,1)S(1)} %copy-done.39), channel_id=1, source_target_pairs={{0,2},{1,3},{2,0},{3,1},{4,6},{5,7},{6,4},{7,5},{8,10},{9,11},{10,... | collective-permute-start | bytes 1179656 | tf_op jit(solution)/shard_map/ppermute | solution.py:934
  111.9 11.6 %collective-permute-start.22 = (bf16[256,768]{1,0:T(8,128)(2,1)S(1)}, bf16[256,768]{1,0:T(8,128)(2,1)S(1)}, u32[]{:S(2)}, u32[]{:S(2)}) collective-permute-start(bf16[256,768]{1,0:T(8,128)(2,1)S(1)} %add_convert_fusion.4), channel_id=1, source_target_pairs={{0,2},{1,3},{2,0},{3,1},{4,6},{5,7},{6,4},{7,5},{8,10},{9,11},{10,... | collective-permute-start | bytes 1179656 | tf_op jit(solution)/shard_map/ppermute | solution.py:934
  123.5 14.7 %collective-permute-start.27 = (bf16[512,768]{1,0:T(8,128)(2,1)}, bf16[512,768]{1,0:T(8,128)(2,1)}, u32[]{:S(2)}, u32[]{:S(2)}) collective-permute-start(bf16[512,768]{1,0:T(8,128)(2,1)} %get-tuple-element.145), channel_id=1, source_target_pairs={{0,1},{1,0},{2,3},{3,2},{4,5},{5,4},{6,7},{7,6},{8,9},{9,8},{10,11... | collective-permute-start | bytes 2359304 | tf_op jit(solution)/shard_map/ppermute | solution.py:931
  126.6 11.6 %collective-permute-start.26 = (bf16[256,768]{1,0:T(8,128)(2,1)}, bf16[256,768]{1,0:T(8,128)(2,1)}, u32[]{:S(2)}, u32[]{:S(2)}) collective-permute-start(bf16[256,768]{1,0:T(8,128)(2,1)} %add_convert_fusion.3), channel_id=1, source_target_pairs={{0,2},{1,3},{2,0},{3,1},{4,6},{5,7},{6,4},{7,5},{8,10},{9,11},{10,... | collective-permute-start | bytes 1179656 | tf_op jit(solution)/shard_map/ppermute | solution.py:934
  128.1 10.1 %collective-permute-start.24 = (bf16[512,768]{1,0:T(8,128)(2,1)}, bf16[512,768]{1,0:T(8,128)(2,1)}, u32[]{:S(2)}, u32[]{:S(2)}) collective-permute-start(bf16[512,768]{1,0:T(8,128)(2,1)} %get-tuple-element.134), channel_id=1, source_target_pairs={{0,1},{1,0},{2,3},{3,2},{4,5},{5,4},{6,7},{7,6},{8,9},{9,8},{10,11... | collective-permute-start | bytes 2359304 | tf_op jit(solution)/shard_map/ppermute | solution.py:931
  128.1 10.1 %collective-permute-start.25 = (bf16[512,768]{1,0:T(8,128)(2,1)}, bf16[512,768]{1,0:T(8,128)(2,1)}, u32[]{:S(2)}, u32[]{:S(2)}) collective-permute-start(bf16[512,768]{1,0:T(8,128)(2,1)} %get-tuple-element.137), channel_id=1, source_target_pairs={{0,1},{1,0},{2,3},{3,2},{4,5},{5,4},{6,7},{7,6},{8,9},{9,8},{10,11... | collective-permute-start | bytes 2359304 | tf_op jit(solution)/shard_map/ppermute | solution.py:931
  151.6 19.4 %collective-permute-start.30 = (bf16[192,1024]{1,0:T(8,128)(2,1)}, bf16[192,1024]{1,0:T(8,128)(2,1)}, u32[]{:S(2)}, u32[]{:S(2)}) collective-permute-start(bf16[192,1024]{1,0:T(8,128)(2,1)} %get-tuple-element.149), channel_id=1, source_target_pairs={{0,2},{1,3},{2,0},{3,1},{4,6},{5,7},{6,4},{7,5},{8,10},{9,11},{10,... | collective-permute-start | bytes 1179656 | tf_op jit(solution)/shard_map/ppermute | solution.py:934
  153.0 18.0 %collective-permute-start.31 = (bf16[192,768]{1,0:T(8,128)(2,1)}, bf16[192,768]{1,0:T(8,128)(2,1)}, u32[]{:S(2)}, u32[]{:S(2)}) collective-permute-start(bf16[192,768]{1,0:T(8,128)(2,1)} %get-tuple-element.159), channel_id=1, source_target_pairs={{0,2},{1,3},{2,0},{3,1},{4,6},{5,7},{6,4},{7,5},{8,10},{9,11},{10,... | collective-permute-start | bytes 884744 | tf_op jit(solution)/shard_map/ppermute | solution.py:934
  153.7 35.6 %collective-permute-start.29 = (bf16[512,768]{1,0:T(8,128)(2,1)}, bf16[512,768]{1,0:T(8,128)(2,1)}, u32[]{:S(2)}, u32[]{:S(2)}) collective-permute-start(bf16[512,768]{1,0:T(8,128)(2,1)} %add_convert_fusion.2), channel_id=1, source_target_pairs={{0,2},{1,3},{2,0},{3,1},{4,6},{5,7},{6,4},{7,5},{8,10},{9,11},{10,... | collective-permute-start | bytes 2359304 | tf_op jit(solution)/shard_map/ppermute | solution.py:934
  189.4 19.7 %collective-permute-start.35 = (bf16[104,768]{1,0:T(8,128)(2,1)S(1)}, bf16[104,768]{1,0:T(8,128)(2,1)S(1)}, u32[]{:S(2)}, u32[]{:S(2)}) collective-permute-start(bf16[104,768]{1,0:T(8,128)(2,1)S(1)} %get-tuple-element.176), channel_id=1, source_target_pairs={{0,4},{4,0},{8,12},{12,8},{16,20},{20,16},{24,28},{28,24},{1,5},{5... | collective-permute-start | bytes 479240 | tf_op jit(solution)/shard_map/ppermute | solution.py:940
  196.9 11.3 %collective-permute-start.37 = (bf16[104,768]{1,0:T(8,128)(2,1)S(1)}, bf16[104,768]{1,0:T(8,128)(2,1)S(1)}, u32[]{:S(2)}, u32[]{:S(2)}) collective-permute-start(bf16[104,768]{1,0:T(8,128)(2,1)S(1)} %get-tuple-element.184), channel_id=1, source_target_pairs={{0,4},{4,0},{8,12},{12,8},{16,20},{20,16},{24,28},{28,24},{1,5},{5... | collective-permute-start | bytes 479240 | tf_op jit(solution)/shard_map/ppermute | solution.py:940
  208.3 19.5 %collective-permute-start.34 = (bf16[512,768]{1,0:T(8,128)(2,1)S(1)}, bf16[512,768]{1,0:T(8,128)(2,1)S(1)}, u32[]{:S(2)}, u32[]{:S(2)}) collective-permute-start(bf16[512,768]{1,0:T(8,128)(2,1)S(1)} %add_convert_fusion.1), channel_id=1, source_target_pairs={{0,2},{1,3},{2,0},{3,1},{4,6},{5,7},{6,4},{7,5},{8,10},{9,11},{10,... | collective-permute-start | bytes 2359304 | tf_op jit(solution)/shard_map/ppermute | solution.py:934
  209.1 23.9 %collective-permute-start.40 = (bf16[104,768]{1,0:T(8,128)(2,1)S(1)}, bf16[104,768]{1,0:T(8,128)(2,1)S(1)}, u32[]{:S(2)}, u32[]{:S(2)}) collective-permute-start(bf16[104,768]{1,0:T(8,128)(2,1)S(1)} %pad_maximum_fusion), channel_id=1, source_target_pairs={{0,16},{4,20},{8,24},{12,28},{16,0},{20,4},{24,8},{28,12},{1,17},{... | collective-permute-start | bytes 479240 | tf_op jit(solution)/shard_map/ppermute | solution.py:940
  213.2 8.3 %collective-permute-start.38 = (bf16[104,768]{1,0:T(8,128)(2,1)S(1)}, bf16[104,768]{1,0:T(8,128)(2,1)S(1)}, u32[]{:S(2)}, u32[]{:S(2)}) collective-permute-start(bf16[104,768]{1,0:T(8,128)(2,1)S(1)} %get-tuple-element.186), channel_id=1, source_target_pairs={{0,4},{4,0},{8,12},{12,8},{16,20},{20,16},{24,28},{28,24},{1,5},{5... | collective-permute-start | bytes 479240 | tf_op jit(solution)/shard_map/ppermute | solution.py:940
  219.7 13.4 %collective-permute-start.41 = (bf16[104,768]{1,0:T(8,128)(2,1)S(1)}, bf16[104,768]{1,0:T(8,128)(2,1)S(1)}, u32[]{:S(2)}, u32[]{:S(2)}) collective-permute-start(bf16[104,768]{1,0:T(8,128)(2,1)S(1)} %pad_maximum_fusion.2), channel_id=1, source_target_pairs={{0,24},{4,28},{8,16},{12,20},{16,8},{20,12},{24,0},{28,4},{1,25},{... | collective-permute-start | bytes 479240 | tf_op jit(solution)/shard_map/ppermute | solution.py:940
  221.5 11.5 %collective-permute-start.39 = (bf16[104,768]{1,0:T(8,128)(2,1)S(1)}, bf16[104,768]{1,0:T(8,128)(2,1)S(1)}, u32[]{:S(2)}, u32[]{:S(2)}) collective-permute-start(bf16[104,768]{1,0:T(8,128)(2,1)S(1)} %pad_maximum_fusion.3), channel_id=1, source_target_pairs={{0,8},{4,12},{8,0},{12,4},{16,24},{20,28},{24,16},{28,20},{1,9},{5... | collective-permute-start | bytes 479240 | tf_op jit(solution)/shard_map/ppermute | solution.py:940
  (71 other events, 615.9 us)
Sparse Core Ops, SparseCore 0:
  37.7 52.1 all-gather.1
  143.6 70.1 reduce-scatter.1

commit v2 on v1

--- a/solution.py
+++ b/solution.py
@@ -1035,15 +1035,17 @@
     depth = w_query.shape[0]
     parts = []
     if direct:
-        for k in range(dp - 2, -1, -2):
+        for k in range(dp - 2, 0, -2):
             sent = grads[k + 1]
             if k < dp // 2 and parts:
-                sent = after(sent, parts[k // 2 - dp // 4])
+                sent = after(sent, parts[-1])
             near, other = grads[k], after(far(sent, 1), r_sum)
             both = summed(near[:depth], other[:depth])
             part = jnp.concatenate([both, near[depth : depth + 4], other[depth : depth + 4]], axis=0)
             parts.insert(0, part)
-        parts = [part if k == 0 else far(part, 2 * k) for k, part in enumerate(parts)]
+        last_sent = after(grads[1], parts[0]) if parts else grads[1]
+        parts = [far(part, 2 * k + 2) for k, part in enumerate(parts)]
+        parts = [grads[0], far(last_sent, 1)] + parts
     r0, r1 = rows_back(after(dk_own, r_sum), dq_own, dv_own, wt)
     grad_tokens = last(tokens, dh1, r0, core(r1), r_x, gain_a)
     output = (

time: 246 us -> 241 us (0.980)
  Pallas kernels: 108 us -> 104 us
  waiting for transfers between devices: 43.5 us -> 40.1 us
  transfers between devices with their start and end apart: 47 -> 47, of which waited for: 20 -> 19; matrix products, arithmetic and copies ran while one was open for 7% -> 7% of each run, Pallas kernels for 42% -> 41%
where the time goes in v2:
time: 241 us; the launch traced here: 240 us
  Pallas kernels  104 us (43%)
  starting transfers between devices  49.6 us (21%)
  waiting for transfers between devices  40.1 us (17%)
  local copies, waits for them, and re-layouts  19 us (8%)
  between operations  15.5 us (6%)
  other arithmetic  12.2 us (5%)
    ppermute x14, starting transfers between devices, far(): return lax.ppermute(v, 'dp', [(i, i ^ k) for i in range(dp)])  27.6 us
    pallas_call x3, Pallas kernels, mlp_both(): pl.pallas_call(functools.partial(mlp_kernel, at, len(into)), in_specs=[AN...  22.8 us
    ppermute x14, waiting for transfers between devices, far(): return lax.ppermute(v, 'dp', [(i, i ^ k) for i in range(dp)])  18.8 us
    ppermute x13, starting transfers between devices, across(): return lax.ppermute(v, 'mp', [(i, i ^ 2) for i in range(mp)])  18.7 us
    pallas_call x1, Pallas kernels, second_back(): pl.pallas_call(functools.partial(second_back_kernel, total // 4 // BLK, p...  16.4 us
    unnamed x117, local copies, waits for them, and re-layouts  15.8 us
    pallas_call x1, Pallas kernels, first_back(): pl.pallas_call(functools.partial(first_back_kernel, total // 4 // BLK), g...  14.6 us
    pallas_call x2, Pallas kernels, attention(): pl.pallas_call(functools.partial(forward_kernel, half, per), grid=(blocks...  13 us
  transfers between devices with their start and end apart: 47, of which 19 were waited for; matrix products, arithmetic and copies ran while one was open for 7% of the time, Pallas kernels for 41%

profile of v2, /device:TPU:0, one launch (start us, length us, event | category | flops | bytes accessed | tf_op | source)
XLA Modules:
  0.0 240.2 jit_solution(13595986528081971403)
XLA Ops:
  8.3 5.1 %collective-permute-start.7 = (bf16[96,768]{1,0:T(8,128)(2,1)S(1)}, bf16[96,768]{1,0:T(8,128)(2,1)S(1)}, u32[]{:S(2)}, u32[]{:S(2)}) collective-permute-start(bf16[96,768]{1,0:T(8,128)(2,1)S(1)} %pad_maximum_fusion.3.rest_0_), channel_id=1, source_target_pairs={{0,24},{4,28},{8,16},{12,20},{16,8},{20,12},{24,0},{28,4},{1,25},{... | collective-permute-start | bytes 442376 | tf_op jit(solution)/shard_map/ppermute | solution.py:940
  30.0 3.1 %collective-permute-done.8.rest_7_ = bf16[96,768]{1,0:T(8,128)(2,1)S(1)} collective-permute-done((bf16[96,768]{1,0:T(8,128)(2,1)S(1)}, bf16[96,768]{1,0:T(8,128)(2,1)S(1)}, u32[]{:S(2)}, u32[]{:S(2)}) %collective-permute-start.8) | collective-permute-done | bytes 147488 | tf_op jit(solution)/shard_map/ppermute | solution.py:940
  33.1 2.9 %collective-permute-done.4.rest_3_ = bf16[96,768]{1,0:T(8,128)(2,1)S(1)} collective-permute-done((bf16[96,768]{1,0:T(8,128)(2,1)S(1)}, bf16[96,768]{1,0:T(8,128)(2,1)S(1)}, u32[]{:S(2)}, u32[]{:S(2)}) %collective-permute-start.4) | collective-permute-done | bytes 147488 | tf_op jit(solution)/shard_map/ppermute | solution.py:940
  40.3 9.5 %qkv.1 = (bf16[2048,768]{1,0:T(8,128)(2,1)}, bf16[576,2048]{1,0:T(8,128)(2,1)}, bf16[2048,192]{1,0:T(8,128)(2,1)}, bf16[2048,192]{1,0:T(8,128)(2,1)}, bf16[576,7...) custom-call(s32[24]{0:T(128)} %concatenate.18.sc, bf16[512,768]{1,0:T(8,128)(2,1)} %refs_0_.5, ...), custom_call_target="tpu_custom_call" | custom-call | flops 10000000 | bytes 1024 | tf_op jit(solution)/shard_map/qkv/pallas_call | solution.py:88
  54.1 6.1 %attention.2 = (bf16[192,1024]{1,0:T(8,128)(2,1)S(1)}, f32[8,1024]{1,0:T(8,128)S(1)}) custom-call(s32[24]{0:T(128)S(1)} %copy-done.29, bf16[576,2048]{1,0:T(8,128)(2,1)S(1)} %copy-done, bf16[2048,192]{1,0:T(8,128)(2,1)S(1)} %copy-done.16, bf16[576,2048]{1,0:T(8,128)(2,1)S(1)} %copy-done, s32[1,2048]{1,0:T(1,128)S(1)} %copy-done.22, ...), custom_call_target="tpu_custom_call" | custom-call | flops 12000000000 | bytes 1024 | tf_op jit(solution)/shard_map/attention/pallas_call | solution.py:207
  60.3 4.5 %collective-permute-done.11.wx = bf16[192,768]{1,0:T(8,128)(2,1)S(1)} collective-permute-done((bf16[192,768]{1,0:T(8,128)(2,1)}, bf16[192,768]{1,0:T(8,128)(2,1)S(1)}, u32[]{:S(2)}, u32[]{:S(2)}) %collective-permute-start.11) | collective-permute-done | bytes 294944 | tf_op jit(solution)/shard_map/ppermute | solution.py:934
  66.2 6.9 %attention.3 = (bf16[192,1024]{1,0:T(8,128)(2,1)S(1)}, f32[8,1024]{1,0:T(8,128)S(1)}) custom-call(s32[24]{0:T(128)S(1)} %copy-done.29, bf16[576,2048]{1,0:T(8,128)(2,1)S(1)} %copy-done, bf16[2048,192]{1,0:T(8,128)(2,1)S(1)} %copy-done.16, bf16[576,2048]{1,0:T(8,128)(2,1)S(1)} %copy-done, s32[1,2048]{1,0:T(1,128)S(1)} %copy-done.22, ...), custom_call_target="tpu_custom_call" | custom-call | flops 12000000000 | bytes 1024 | tf_op jit(solution)/shard_map/attention/pallas_call | solution.py:207
  74.9 2.1 out_projection.1
  77.6 1.9 collective-permute-done.13.refs_2_
  79.5 2.4 %middle.1 = (f32[512,768]{1,0:T(8,128)S(1)}, bf16[512,768]{1,0:T(8,128)(2,1)S(1)}, bf16[256,768]{1,0:T(8,128)(2,1)}, bf16[256,768]{1,0:T(8,128)(2,1)S(1)}) custom-call(bf16[512,768]{1,0:T(8,128)(2,1)S(1)} %copy-done.2, bf16[512,768]{1,0:T(8,128)(2,1)S(1)} %get-tuple-element.112.refs_1_, bf16[512,768]{1,0:T(8,128)(2,1)S(1)} %collective-permute-done.13.refs_2_, ...), custom_call_target="tpu_custom_call" | custom-call | flops 10000000 | bytes 1024 | tf_op jit(solution)/shard_map/middle/pallas_call | solution.py:498
  86.0 3.8 %all-gather.2.cloned.1.call-done.w = bf16[768,1536]{1,0:T(8,128)(2,1)} async-done(((bf16[96,1536]{1,0:T(8,128)(2,1)}), bf16[768,1536]{1,0:T(8,128)(2,1)}) %all-gather.2.cloned.1.call-update) | async-done | bytes 2359312 | tf_op jit(solution)/shard_map/all_gather | solution.py:975
  89.8 10.2 %mlp.3 = (bf16[512,768]{1,0:T(8,128)(2,1)}, bf16[512,768]{1,0:T(8,128)(2,1)}, bf16[512,768]{1,0:T(8,128)(2,1)}, bf16[512,768]{1,0:T(8,128)(2,1)}, bf16[1024,512]{1,0:T(8,128)(2,1)}, /*index=5*/bf16[1024,1024]{1,0:T(8,128)(2,1)}) custom-call(bf16[512,768]{1,0:T(8,128)(2,1)} %copy-done.34, bf16[512,768]{1,0:T(8,128)(2,1)} %collective-permute-done.14.nb.refs_1_, ...), custom_call_target="tpu_custom_call" | custom-call | flops 8000000000 | bytes 1024 | tf_op jit(solution)/shard_map/mlp/pallas_call | solution.py:649
  103.5 6.3 %mlp.4 = (bf16[512,768]{1,0:T(8,128)(2,1)S(1)}, bf16[512,768]{1,0:T(8,128)(2,1)}, bf16[256,768]{1,0:T(8,128)(2,1)S(1)}, bf16[256,768]{1,0:T(8,128)(2,1)S(1)}, bf...) custom-call(bf16[256,768]{1,0:T(8,128)(2,1)S(1)} %collective-permute-done.17.na.refs_2_, ...), custom_call_target="tpu_custom_call" | custom-call | flops 8000000000 | bytes 1024 | tf_op jit(solution)/shard_map/mlp/pallas_call | solution.py:649
  113.4 6.3 %mlp.5 = (bf16[512,768]{1,0:T(8,128)(2,1)S(1)}, bf16[512,768]{1,0:T(8,128)(2,1)}, bf16[256,768]{1,0:T(8,128)(2,1)S(1)}, bf16[256,768]{1,0:T(8,128)(2,1)S(1)}, bf...) custom-call(bf16[256,768]{1,0:T(8,128)(2,1)S(1)} %collective-permute-done., ...), custom_call_target="tpu_custom_call", output_to_operand_aliasing={{0}: (5, {}), {1}: (6, {})} | custom-call | flops 8000000000 | bytes 1024 | tf_op jit(solution)/shard_map/mlp/pallas_call | solution.py:649
  120.7 2.7 %collective-permute-done.22.refs_4_ = bf16[256,768]{1,0:T(8,128)(2,1)S(1)} collective-permute-done((bf16[256,768]{1,0:T(8,128)(2,1)S(1)}, bf16[256,768]{1,0:T(8,128)(2,1)S(1)}, u32[]{:S(2)}, u32[]{:S(2)}) %collective-permute-start.22) | collective-permute-done | bytes 393248 | tf_op jit(solution)/shard_map/ppermute | solution.py:934
  128.5 9.6 %mlp_weights.1 = bf16[768,1536]{1,0:T(8,128)(2,1)} custom-call(bf16[512,768]{1,0:T(8,128)(2,1)S(1)} %copy-done.35, bf16[512,768]{1,0:T(8,128)(2,1)} %collective-permute-done.14.nb.refs_1_, bf16[256,768]{1,0:T(8,128)(2,1)S(1)} %copy-done.37, bf16[256,768]{1,0:T(8,128)(2,1)S(1)} %collective-permute-done.18.nb.refs_3_, ...), custom_call_target="tpu_custom_call" | custom-call | flops 10000000000 | bytes 1024 | tf_op jit(solution)/shard_map/mlp_weights/pallas_call | solution.py:736
  138.1 3.3 %middle_back.1 = (f32[512,768]{1,0:T(8,128)S(1)}, bf16[512,768]{1,0:T(8,128)(2,1)}, f32[32,768]{1,0:T(8,128)S(1)}) custom-call(bf16[512,768]{1,0:T(8,128)(2,1)} %refs_0_.4, f32[512,768]{1,0:T(8,128)S(1)} %get-tuple-element.114.refs_1_, bf16[512,768]{1,0:T(8,128)(2,1)S(1)} %copy-done.17, bf16[512,768]{1,0:T(8,128)(2,1)} %collective-permute-done.25.refs_3_, ...), custom_call_target="tpu_custom_call" | custom-call | flops 10000000 | bytes 1024 | tf_op jit(solution)/shard_map/middle_back/pallas_call | solution.py:498
  144.4 2.2 add_convert_fusion.2
  146.6 4.1 %out_back.1 = (bf16[192,1024]{1,0:T(8,128)(2,1)S(1)}, bf16[192,1024]{1,0:T(8,128)(2,1)}, f32[192,768]{1,0:T(8,128)S(1)}, bf16[192,768]{1,0:T(8,128)(2,1)}) custom-call(bf16[512,768]{1,0:T(8,128)(2,1)} %get-tuple-element.146.own, bf16[512,768]{1,0:T(8,128)(2,1)} %collective-permute-done.28.other, bf16[192,768]{1,0:T(8,128)(2,1)S(1)} %copy-done.13, ...), custom_call_target="tpu_custom_call" | custom-call | flops 10000000 | bytes 1024 | tf_op jit(solution)/shard_map/out_back/pallas_call | solution.py:818
  154.9 14.6 %attention_back.1 = (bf16[192,1024]{1,0:T(8,128)(2,1)}, f32[192,2048]{1,0:T(8,128)}, f32[192,2048]{1,0:T(8,128)}) custom-call(s32[24]{0:T(128)} %concatenate.18.sc, bf16[576,2048]{1,0:T(8,128)(2,1)} %get-tuple-element.104.qt.vt.kt, bf16[2048,192]{1,0:T(8,128)(2,1)} %get-tuple-element.105.kn, bf16[576,2048]{1,0:T(8,128)(2,1)} %get-tuple-element.104.qt.vt.kt, ...), custom_call_target="tpu_custom_call" | custom-call | flops 20000000000 | bytes 1024 | tf_op jit(solution)/shard_map/attention_back/pallas_call | solution.py:375
  172.1 16.4 %attention_back_end.1 = (bf16[512,768]{1,0:T(8,128)(2,1)S(1)}, bf16[512,768]{1,0:T(8,128)(2,1)S(1)}, bf16[192,1024]{1,0:T(8,128)(2,1)S(1)}, bf16[192,1024]{1,0:T...) custom-call(s32[24]{0:T(128)S(1)} %copy-done.30, ...), custom_call_target="tpu_custom_call" | custom-call | flops 10000000 | bytes 1024 | tf_op jit(solution)/shard_map/attention_back_end/pallas_call | solution.py:401
  188.6 2.8 %collective-permute-start.35 = (bf16[104,768]{1,0:T(8,128)(2,1)S(1)}, bf16[104,768]{1,0:T(8,128)(2,1)S(1)}, u32[]{:S(2)}, u32[]{:S(2)}) collective-permute-start(bf16[104,768]{1,0:T(8,128)(2,1)S(1)} %get-tuple-element.178), channel_id=1, source_target_pairs={{0,4},{4,0},{8,12},{12,8},{16,20},{20,16},{24,28},{28,24},{1,5},{5... | collective-permute-start | bytes 479240 | tf_op jit(solution)/shard_map/ppermute | solution.py:940
  191.7 2.2 collective-permute-start.34
  193.9 7.9 %collective-permute-done.39 = bf16[104,768]{1,0:T(8,128)(2,1)S(1)} collective-permute-done((bf16[104,768]{1,0:T(8,128)(2,1)S(1)}, bf16[104,768]{1,0:T(8,128)(2,1)S(1)}, u32[]{:S(2)}, u32[]{:S(2)}) %collective-permute-start.39) | collective-permute-done | bytes 159776 | tf_op jit(solution)/shard_map/ppermute | solution.py:940
  201.9 4.9 %collective-permute-start.41 = (bf16[104,768]{1,0:T(8,128)(2,1)S(1)}, bf16[104,768]{1,0:T(8,128)(2,1)S(1)}, u32[]{:S(2)}, u32[]{:S(2)}) collective-permute-start(bf16[104,768]{1,0:T(8,128)(2,1)S(1)} %pad_maximum_fusion), channel_id=1, source_target_pairs={{0,24},{4,28},{8,16},{12,20},{16,8},{20,12},{24,0},{28,4},{1,25},{... | collective-permute-start | bytes 479240 | tf_op jit(solution)/shard_map/ppermute | solution.py:940
  206.8 1.9 rows_back.1
  208.8 7.0 %collective-permute-start.40 = (bf16[104,768]{1,0:T(8,128)(2,1)S(1)}, bf16[104,768]{1,0:T(8,128)(2,1)S(1)}, u32[]{:S(2)}, u32[]{:S(2)}) collective-permute-start(bf16[104,768]{1,0:T(8,128)(2,1)S(1)} %pad_maximum_fusion.2), channel_id=1, source_target_pairs={{0,16},{4,20},{8,24},{12,28},{16,0},{20,4},{24,8},{28,12},{1,17},{... | collective-permute-start | bytes 479240 | tf_op jit(solution)/shard_map/ppermute | solution.py:940
  215.8 2.8 %add_convert_fusion = bf16[512,768]{1,0:T(8,128)(2,1)} fusion(f32[512,768]{1,0:T(8,128)S(1)} %get-tuple-element.114.refs_1_, bf16[512,768]{1,0:T(8,128)(2,1)} %collective-permute-done.29, bf16[512,768]{1,0:T(8,128)(2,1)} %collective-permute-done.24, bf16[512,768]{1,0:T(8,128)(2,1)S(1)} %copy-done.44), kind=kLoop, calls=%fused_computation | loop fusion | flops 2752512 | bytes 4718592 | tf_op jit(solution)/shard_map/convert_element_type | solution.py:1053
  218.7 1.8 collective-permute-start.37
  220.5 3.4 %last.1 = bf16[512,768]{1,0:T(8,128)(2,1)} custom-call(bf16[512,768]{1,0:T(8,128)(2,1)S(1)} %copy-done.2, f32[512,768]{1,0:T(8,128)S(1)} %copy-done.6, bf16[512,768]{1,0:T(8,128)(2,1)S(1)} %get-tuple-element.170.refs_2_, bf16[512,768]{1,0:T(8,128)(2,1)S(1)} %collective-permute-done.33.refs_3_, bf16[512,768]{1,0:T(8,128)(2,1)S(1)} %collective-permute-done.34.refs_4_, ...), custom_call_target="tpu_custom_call" | custom-call | flops 10000000 | bytes 1024 | tf_op jit(solution)/shard_map/last/pallas_call | solution.py:498
  223.9 1.8 slice_convert_fusion
  225.7 2.3 collective-permute-done.38.refs_2_
  (229 shorter events, 62.0 us)
Async XLA Ops:
  7.2 82.6 %all-gather.2.cloned.1.call-start = ((), (), s32[]{:S(2)}) async-start(), calls=%async_computation.1 | async-start | bytes 2654208 | tf_op jit(solution)/shard_map/all_gather | solution.py:975
  8.3 17.9 %collective-permute-start.7 = (bf16[96,768]{1,0:T(8,128)(2,1)S(1)}, bf16[96,768]{1,0:T(8,128)(2,1)S(1)}, u32[]{:S(2)}, u32[]{:S(2)}) collective-permute-start(bf16[96,768]{1,0:T(8,128)(2,1)S(1)} %pad_maximum_fusion.3.rest_0_), channel_id=1, source_target_pairs={{0,24},{4,28},{8,16},{12,20},{16,8},{20,12},{24,0},{28,4},{1,25},{... | collective-permute-start | bytes 442376 | tf_op jit(solution)/shard_map/ppermute | solution.py:940
  13.4 12.5 %collective-permute-start.5 = (bf16[96,768]{1,0:T(8,128)(2,1)S(1)}, bf16[96,768]{1,0:T(8,128)(2,1)S(1)}, u32[]{:S(2)}, u32[]{:S(2)}) collective-permute-start(bf16[96,768]{1,0:T(8,128)(2,1)S(1)} %pad_maximum_fusion.3.rest_0_), channel_id=1, source_target_pairs={{0,16},{4,20},{8,24},{12,28},{16,0},{20,4},{24,8},{28,12},{1,17},{... | collective-permute-start | bytes 442376 | tf_op jit(solution)/shard_map/ppermute | solution.py:940
  13.4 14.4 %collective-permute-start.3 = (bf16[96,768]{1,0:T(8,128)(2,1)S(1)}, bf16[96,768]{1,0:T(8,128)(2,1)S(1)}, u32[]{:S(2)}, u32[]{:S(2)}) collective-permute-start(bf16[96,768]{1,0:T(8,128)(2,1)S(1)} %pad_maximum_fusion.3.rest_0_), channel_id=1, source_target_pairs={{0,8},{4,12},{8,0},{12,4},{16,24},{20,28},{24,16},{28,20},{1,9},{5... | collective-permute-start | bytes 442376 | tf_op jit(solution)/shard_map/ppermute | solution.py:940
  14.1 15.8 %collective-permute-start = (bf16[96,768]{1,0:T(8,128)(2,1)S(1)}, bf16[96,768]{1,0:T(8,128)(2,1)S(1)}, u32[]{:S(2)}, u32[]{:S(2)}) collective-permute-start(bf16[96,768]{1,0:T(8,128)(2,1)S(1)} %pad_maximum_fusion.3.rest_0_), channel_id=1, source_target_pairs={{0,4},{4,0},{8,12},{12,8},{16,20},{20,16},{24,28},{28,24},{1,5},{5... | collective-permute-start | bytes 442376 | tf_op jit(solution)/shard_map/ppermute | solution.py:940
  15.7 21.8 %collective-permute-start.2 = (bf16[512,768]{1,0:T(8,128)(2,1)}, bf16[512,768]{1,0:T(8,128)(2,1)}, u32[]{:S(2)}, u32[]{:S(2)}) collective-permute-start(bf16[512,768]{1,0:T(8,128)(2,1)} %refs_0_.5), channel_id=1, source_target_pairs={{0,2},{1,3},{2,0},{3,1},{4,6},{5,7},{6,4},{7,5},{8,10},{9,11},{10,... | collective-permute-start | bytes 2359304 | tf_op jit(solution)/shard_map/ppermute | solution.py:934
  28.4 9.2 %collective-permute-start.6 = (bf16[96,768]{1,0:T(8,128)(2,1)S(1)}, bf16[96,768]{1,0:T(8,128)(2,1)S(1)}, u32[]{:S(2)}, u32[]{:S(2)}) collective-permute-start(bf16[96,768]{1,0:T(8,128)(2,1)S(1)} %collective-permute-done.5.rest_4_), channel_id=1, source_target_pairs={{0,4},{4,0},{8,12},{12,8},{16,20},{20,16},{24,28},{28,24},{1,5},{5... | collective-permute-start | bytes 442376 | tf_op jit(solution)/shard_map/ppermute | solution.py:940
  29.9 10.4 %collective-permute-start.1 = (bf16[512,768]{1,0:T(8,128)(2,1)S(1)}, bf16[512,768]{1,0:T(8,128)(2,1)}, u32[]{:S(2)}, u32[]{:S(2)}) collective-permute-start(bf16[512,768]{1,0:T(8,128)(2,1)S(1)} %copy-done.1), channel_id=1, source_target_pairs={{0,1},{1,0},{2,3},{3,2},{4,5},{5,4},{6,7},{7,6},{8,9},{9,8},{10,11... | collective-permute-start | bytes 2359304 | tf_op jit(solution)/shard_map/ppermute | solution.py:931
  37.6 186.3 %reduce-scatter.2.cloned.1.call-start = ((), (), s32[]{:S(2)}) async-start(), calls=%async_computation.2 | async-start | bytes 2654208 | tf_op jit(solution)/shard_map/reduce_scatter | solution.py:1012
  38.8 21.5 %collective-permute-start.10 = (bf16[512,768]{1,0:T(8,128)(2,1)}, bf16[512,768]{1,0:T(8,128)(2,1)S(1)}, u32[]{:S(2)}, u32[]{:S(2)}) collective-permute-start(bf16[512,768]{1,0:T(8,128)(2,1)} %refs_0_.4), channel_id=1, source_target_pairs={{0,2},{1,3},{2,0},{3,1},{4,6},{5,7},{6,4},{7,5},{8,10},{9,11},{10,... | collective-permute-start | bytes 2359304 | tf_op jit(solution)/shard_map/ppermute | solution.py:934
  49.8 15.0 %collective-permute-start.11 = (bf16[192,768]{1,0:T(8,128)(2,1)}, bf16[192,768]{1,0:T(8,128)(2,1)S(1)}, u32[]{:S(2)}, u32[]{:S(2)}) collective-permute-start(bf16[192,768]{1,0:T(8,128)(2,1)} %get-tuple-element.110.wm), channel_id=1, source_target_pairs={{0,2},{1,3},{2,0},{3,1},{4,6},{5,7},{6,4},{7,5},{8,10},{9,11},{10,... | collective-permute-start | bytes 884744 | tf_op jit(solution)/shard_map/ppermute | solution.py:934
  64.8 10.2 %collective-permute-start.12 = (bf16[192,1024]{1,0:T(8,128)(2,1)S(1)}, bf16[192,1024]{1,0:T(8,128)(2,1)S(1)}, u32[]{:S(2)}, u32[]{:S(2)}) collective-permute-start(bf16[192,1024]{1,0:T(8,128)(2,1)S(1)} %get-tuple-element.111.ot), channel_id=1, source_target_pairs={{0,2},{1,3},{2,0},{3,1},{4,6},{5,7},{6,4},{7,5},{8,10},{9,11},{10,... | collective-permute-start | bytes 1179656 | tf_op jit(solution)/shard_map/ppermute | solution.py:934
  77.1 8.5 %collective-permute-start.15 = (bf16[512,768]{1,0:T(8,128)(2,1)}, bf16[512,768]{1,0:T(8,128)(2,1)}, u32[]{:S(2)}, u32[]{:S(2)}) collective-permute-start(bf16[512,768]{1,0:T(8,128)(2,1)} %refs_0_.4), channel_id=1, source_target_pairs={{0,1},{1,0},{2,3},{3,2},{4,5},{5,4},{6,7},{7,6},{8,9},{9,8},{10,11... | collective-permute-start | bytes 2359304 | tf_op jit(solution)/shard_map/ppermute | solution.py:931
  83.7 18.0 %collective-permute-start.19 = (bf16[512,768]{1,0:T(8,128)(2,1)S(1)}, bf16[512,768]{1,0:T(8,128)(2,1)}, u32[]{:S(2)}, u32[]{:S(2)}) collective-permute-start(bf16[512,768]{1,0:T(8,128)(2,1)S(1)} %copy-done.33), channel_id=1, source_target_pairs={{0,1},{1,0},{2,3},{3,2},{4,5},{5,4},{6,7},{7,6},{8,9},{9,8},{10,11... | collective-permute-start | bytes 2359304 | tf_op jit(solution)/shard_map/ppermute | solution.py:931
  84.1 16.0 %collective-permute-start.17 = (bf16[256,768]{1,0:T(8,128)(2,1)}, bf16[256,768]{1,0:T(8,128)(2,1)S(1)}, u32[]{:S(2)}, u32[]{:S(2)}) collective-permute-start(bf16[256,768]{1,0:T(8,128)(2,1)} %get-tuple-element.120), channel_id=1, source_target_pairs={{0,2},{1,3},{2,0},{3,1},{4,6},{5,7},{6,4},{7,5},{8,10},{9,11},{10,... | collective-permute-start | bytes 1179656 | tf_op jit(solution)/shard_map/ppermute | solution.py:934
  100.2 11.5 %collective-permute-start.16 = (bf16[256,768]{1,0:T(8,128)(2,1)S(1)}, bf16[256,768]{1,0:T(8,128)(2,1)S(1)}, u32[]{:S(2)}, u32[]{:S(2)}) collective-permute-start(bf16[256,768]{1,0:T(8,128)(2,1)S(1)} %copy-done.39), channel_id=1, source_target_pairs={{0,2},{1,3},{2,0},{3,1},{4,6},{5,7},{6,4},{7,5},{8,10},{9,11},{10,... | collective-permute-start | bytes 1179656 | tf_op jit(solution)/shard_map/ppermute | solution.py:934
  111.8 11.6 %collective-permute-start.22 = (bf16[256,768]{1,0:T(8,128)(2,1)S(1)}, bf16[256,768]{1,0:T(8,128)(2,1)S(1)}, u32[]{:S(2)}, u32[]{:S(2)}) collective-permute-start(bf16[256,768]{1,0:T(8,128)(2,1)S(1)} %add_convert_fusion.4), channel_id=1, source_target_pairs={{0,2},{1,3},{2,0},{3,1},{4,6},{5,7},{6,4},{7,5},{8,10},{9,11},{10,... | collective-permute-start | bytes 1179656 | tf_op jit(solution)/shard_map/ppermute | solution.py:934
  123.4 14.7 %collective-permute-start.27 = (bf16[512,768]{1,0:T(8,128)(2,1)}, bf16[512,768]{1,0:T(8,128)(2,1)}, u32[]{:S(2)}, u32[]{:S(2)}) collective-permute-start(bf16[512,768]{1,0:T(8,128)(2,1)} %get-tuple-element.144), channel_id=1, source_target_pairs={{0,1},{1,0},{2,3},{3,2},{4,5},{5,4},{6,7},{7,6},{8,9},{9,8},{10,11... | collective-permute-start | bytes 2359304 | tf_op jit(solution)/shard_map/ppermute | solution.py:931
  126.5 11.6 %collective-permute-start.26 = (bf16[256,768]{1,0:T(8,128)(2,1)}, bf16[256,768]{1,0:T(8,128)(2,1)}, u32[]{:S(2)}, u32[]{:S(2)}) collective-permute-start(bf16[256,768]{1,0:T(8,128)(2,1)} %add_convert_fusion.3), channel_id=1, source_target_pairs={{0,2},{1,3},{2,0},{3,1},{4,6},{5,7},{6,4},{7,5},{8,10},{9,11},{10,... | collective-permute-start | bytes 1179656 | tf_op jit(solution)/shard_map/ppermute | solution.py:934
  128.0 10.1 %collective-permute-start.24 = (bf16[512,768]{1,0:T(8,128)(2,1)}, bf16[512,768]{1,0:T(8,128)(2,1)}, u32[]{:S(2)}, u32[]{:S(2)}) collective-permute-start(bf16[512,768]{1,0:T(8,128)(2,1)} %get-tuple-element.133), channel_id=1, source_target_pairs={{0,1},{1,0},{2,3},{3,2},{4,5},{5,4},{6,7},{7,6},{8,9},{9,8},{10,11... | collective-permute-start | bytes 2359304 | tf_op jit(solution)/shard_map/ppermute | solution.py:931
  128.0 10.1 %collective-permute-start.25 = (bf16[512,768]{1,0:T(8,128)(2,1)}, bf16[512,768]{1,0:T(8,128)(2,1)}, u32[]{:S(2)}, u32[]{:S(2)}) collective-permute-start(bf16[512,768]{1,0:T(8,128)(2,1)} %get-tuple-element.136), channel_id=1, source_target_pairs={{0,1},{1,0},{2,3},{3,2},{4,5},{5,4},{6,7},{7,6},{8,9},{9,8},{10,11... | collective-permute-start | bytes 2359304 | tf_op jit(solution)/shard_map/ppermute | solution.py:931
  151.5 18.6 %collective-permute-start.30 = (bf16[192,1024]{1,0:T(8,128)(2,1)}, bf16[192,1024]{1,0:T(8,128)(2,1)}, u32[]{:S(2)}, u32[]{:S(2)}) collective-permute-start(bf16[192,1024]{1,0:T(8,128)(2,1)} %get-tuple-element.148), channel_id=1, source_target_pairs={{0,2},{1,3},{2,0},{3,1},{4,6},{5,7},{6,4},{7,5},{8,10},{9,11},{10,... | collective-permute-start | bytes 1179656 | tf_op jit(solution)/shard_map/ppermute | solution.py:934
  152.8 17.3 %collective-permute-start.31 = (bf16[192,768]{1,0:T(8,128)(2,1)}, bf16[192,768]{1,0:T(8,128)(2,1)}, u32[]{:S(2)}, u32[]{:S(2)}) collective-permute-start(bf16[192,768]{1,0:T(8,128)(2,1)} %get-tuple-element.158), channel_id=1, source_target_pairs={{0,2},{1,3},{2,0},{3,1},{4,6},{5,7},{6,4},{7,5},{8,10},{9,11},{10,... | collective-permute-start | bytes 884744 | tf_op jit(solution)/shard_map/ppermute | solution.py:934
  153.5 34.9 %collective-permute-start.29 = (bf16[512,768]{1,0:T(8,128)(2,1)}, bf16[512,768]{1,0:T(8,128)(2,1)}, u32[]{:S(2)}, u32[]{:S(2)}) collective-permute-start(bf16[512,768]{1,0:T(8,128)(2,1)} %add_convert_fusion.2), channel_id=1, source_target_pairs={{0,2},{1,3},{2,0},{3,1},{4,6},{5,7},{6,4},{7,5},{8,10},{9,11},{10,... | collective-permute-start | bytes 2359304 | tf_op jit(solution)/shard_map/ppermute | solution.py:934
  188.6 13.2 %collective-permute-start.35 = (bf16[104,768]{1,0:T(8,128)(2,1)S(1)}, bf16[104,768]{1,0:T(8,128)(2,1)S(1)}, u32[]{:S(2)}, u32[]{:S(2)}) collective-permute-start(bf16[104,768]{1,0:T(8,128)(2,1)S(1)} %get-tuple-element.178), channel_id=1, source_target_pairs={{0,4},{4,0},{8,12},{12,8},{16,20},{20,16},{24,28},{28,24},{1,5},{5... | collective-permute-start | bytes 479240 | tf_op jit(solution)/shard_map/ppermute | solution.py:940
  191.4 10.4 %collective-permute-start.39 = (bf16[104,768]{1,0:T(8,128)(2,1)S(1)}, bf16[104,768]{1,0:T(8,128)(2,1)S(1)}, u32[]{:S(2)}, u32[]{:S(2)}) collective-permute-start(bf16[104,768]{1,0:T(8,128)(2,1)S(1)} %get-tuple-element.184), channel_id=1, source_target_pairs={{0,4},{4,0},{8,12},{12,8},{16,20},{20,16},{24,28},{28,24},{1,5},{5... | collective-permute-start | bytes 479240 | tf_op jit(solution)/shard_map/ppermute | solution.py:940
  191.7 28.8 %collective-permute-start.34 = (bf16[512,768]{1,0:T(8,128)(2,1)S(1)}, bf16[512,768]{1,0:T(8,128)(2,1)S(1)}, u32[]{:S(2)}, u32[]{:S(2)}) collective-permute-start(bf16[512,768]{1,0:T(8,128)(2,1)S(1)} %add_convert_fusion.1), channel_id=1, source_target_pairs={{0,2},{1,3},{2,0},{3,1},{4,6},{5,7},{6,4},{7,5},{8,10},{9,11},{10,... | collective-permute-start | bytes 2359304 | tf_op jit(solution)/shard_map/ppermute | solution.py:934
  201.9 23.8 %collective-permute-start.41 = (bf16[104,768]{1,0:T(8,128)(2,1)S(1)}, bf16[104,768]{1,0:T(8,128)(2,1)S(1)}, u32[]{:S(2)}, u32[]{:S(2)}) collective-permute-start(bf16[104,768]{1,0:T(8,128)(2,1)S(1)} %pad_maximum_fusion), channel_id=1, source_target_pairs={{0,24},{4,28},{8,16},{12,20},{16,8},{20,12},{24,0},{28,4},{1,25},{... | collective-permute-start | bytes 479240 | tf_op jit(solution)/shard_map/ppermute | solution.py:940
  206.8 11.7 %collective-permute-start.36 = (bf16[104,768]{1,0:T(8,128)(2,1)S(1)}, bf16[104,768]{1,0:T(8,128)(2,1)S(1)}, u32[]{:S(2)}, u32[]{:S(2)}) collective-permute-start(bf16[104,768]{1,0:T(8,128)(2,1)S(1)} %get-tuple-element.180), channel_id=1, source_target_pairs={{0,4},{4,0},{8,12},{12,8},{16,20},{20,16},{24,28},{28,24},{1,5},{5... | collective-permute-start | bytes 479240 | tf_op jit(solution)/shard_map/ppermute | solution.py:940
  208.6 10.0 %collective-permute-start.33 = (bf16[512,768]{1,0:T(8,128)(2,1)S(1)}, bf16[512,768]{1,0:T(8,128)(2,1)S(1)}, u32[]{:S(2)}, u32[]{:S(2)}) collective-permute-start(bf16[512,768]{1,0:T(8,128)(2,1)S(1)} %get-tuple-element.171), channel_id=1, source_target_pairs={{0,1},{1,0},{2,3},{3,2},{4,5},{5,4},{6,7},{7,6},{8,9},{9,8},{10,11... | collective-permute-start | bytes 2359304 | tf_op jit(solution)/shard_map/ppermute | solution.py:931
  208.8 16.9 %collective-permute-start.40 = (bf16[104,768]{1,0:T(8,128)(2,1)S(1)}, bf16[104,768]{1,0:T(8,128)(2,1)S(1)}, u32[]{:S(2)}, u32[]{:S(2)}) collective-permute-start(bf16[104,768]{1,0:T(8,128)(2,1)S(1)} %pad_maximum_fusion.2), channel_id=1, source_target_pairs={{0,16},{4,20},{8,24},{12,28},{16,0},{20,4},{24,8},{28,12},{1,17},{... | collective-permute-start | bytes 479240 | tf_op jit(solution)/shard_map/ppermute | solution.py:940
  218.6 9.4 %collective-permute-start.38 = (bf16[104,768]{1,0:T(8,128)(2,1)S(1)}, bf16[104,768]{1,0:T(8,128)(2,1)S(1)}, u32[]{:S(2)}, u32[]{:S(2)}) collective-permute-start(bf16[104,768]{1,0:T(8,128)(2,1)S(1)} %pad_maximum_fusion.1), channel_id=1, source_target_pairs={{0,8},{4,12},{8,0},{12,4},{16,24},{20,28},{24,16},{28,20},{1,9},{5... | collective-permute-start | bytes 479240 | tf_op jit(solution)/shard_map/ppermute | solution.py:940
  (71 other events, 596.5 us)
Sparse Core Ops, SparseCore 0:
  37.7 52.0 all-gather.1
  143.4 71.8 reduce-scatter.1

commit v3 on v2

--- a/solution.py
+++ b/solution.py
@@ -1047,7 +1047,6 @@
         parts = [far(part, 2 * k + 2) for k, part in enumerate(parts)]
         parts = [grads[0], far(last_sent, 1)] + parts
     r0, r1 = rows_back(after(dk_own, r_sum), dq_own, dv_own, wt)
-    grad_tokens = last(tokens, dh1, r0, core(r1), r_x, gain_a)
     output = (
         h1 + (m0.astype(F32) + m_core.astype(F32) + after(m_x, r_sum).astype(F32))
     ).astype(BF16)
@@ -1055,8 +1054,9 @@
     grad_gate, grad_up, grad_down = (
         mlp_grads[:, j * units : (j + 1) * units].astype(F32) for j in range(3)
     )
+    grad_tokens = last(tokens, after(dh1, output, grad_gate), r0, core(r1), r_x, gain_a)
     if direct:
-        parts[0] = after(parts[0], grad_tokens, output, grad_gate)
+        parts[0] = after(parts[0], grad_tokens)
         grad_k, grad_q, grad_v, grad_o, gains = grads_sum(parts)
         gains = gains + core(gains) + across(gains) + core_across(gains)
     else:

time: 241 us -> 244 us (1.012)
  starting transfers between devices: 49.6 us -> 42.8 us
  Pallas kernels: 104 us -> 109 us
  local copies, waits for them, and re-layouts: 19 us -> 22.2 us
  other arithmetic: 12.2 us -> 15 us
    ppermute x14, starting transfers between devices: 27.6 us -> 22.8 us  [far(): return lax.ppermute(v, 'dp', [(i, i ^ k) for i in range(dp)])]
    unnamed x117 -> x125, local copies, waits for them, and re-layouts: 15.8 us -> 19 us
    pallas_call x1, Pallas kernels: 16.4 us -> 19.1 us  [second_back(): pl.pallas_call(functools.partial(second_back_kernel, total // 4 // BLK, p...]
  transfers between devices with their start and end apart: 47 -> 47, of which waited for: 19 -> 19; matrix products, arithmetic and copies ran while one was open for 7% -> 8% of each run, Pallas kernels for 41% -> 43%
where the time goes in v3:
time: 244 us; the launch traced here: 243 us
  Pallas kernels  109 us (45%)
  starting transfers between devices  42.8 us (18%)
  waiting for transfers between devices  38.5 us (16%)
  local copies, waits for them, and re-layouts  22.2 us (9%)
  between operations  15.6 us (6%)
  other arithmetic  15 us (6%)
    ppermute x14, starting transfers between devices, far(): return lax.ppermute(v, 'dp', [(i, i ^ k) for i in range(dp)])  22.8 us
    pallas_call x3, Pallas kernels, mlp_both(): pl.pallas_call(functools.partial(mlp_kernel, at, len(into)), in_specs=[AN...  22.8 us
    pallas_call x1, Pallas kernels, second_back(): pl.pallas_call(functools.partial(second_back_kernel, total // 4 // BLK, p...  19.1 us
    unnamed x125, local copies, waits for them, and re-layouts  19 us
    ppermute x14, waiting for transfers between devices, far(): return lax.ppermute(v, 'dp', [(i, i ^ k) for i in range(dp)])  18.3 us
    ppermute x13, starting transfers between devices, across(): return lax.ppermute(v, 'mp', [(i, i ^ 2) for i in range(mp)])  16.4 us
    pallas_call x2, Pallas kernels, attention(): pl.pallas_call(functools.partial(forward_kernel, half, per), grid=(blocks...  14.7 us
    pallas_call x1, Pallas kernels, first_back(): pl.pallas_call(functools.partial(first_back_kernel, total // 4 // BLK), g...  14.6 us
  transfers between devices with their start and end apart: 47, of which 19 were waited for; matrix products, arithmetic and copies ran while one was open for 8% of the time, Pallas kernels for 43%

profile of v3, /device:TPU:0, one launch (start us, length us, event | category | flops | bytes accessed | tf_op | source)
XLA Modules:
  0.0 243.3 jit_solution(15571687690467767815)
XLA Ops:
  8.3 5.1 %collective-permute-start.7 = (bf16[96,768]{1,0:T(8,128)(2,1)S(1)}, bf16[96,768]{1,0:T(8,128)(2,1)S(1)}, u32[]{:S(2)}, u32[]{:S(2)}) collective-permute-start(bf16[96,768]{1,0:T(8,128)(2,1)S(1)} %pad_maximum_fusion.3.rest_0_), channel_id=1, source_target_pairs={{0,24},{4,28},{8,16},{12,20},{16,8},{20,12},{24,0},{28,4},{1,25},{... | collective-permute-start | bytes 442376 | tf_op jit(solution)/shard_map/ppermute | solution.py:940
  30.0 3.1 %collective-permute-done.8.rest_7_ = bf16[96,768]{1,0:T(8,128)(2,1)S(1)} collective-permute-done((bf16[96,768]{1,0:T(8,128)(2,1)S(1)}, bf16[96,768]{1,0:T(8,128)(2,1)S(1)}, u32[]{:S(2)}, u32[]{:S(2)}) %collective-permute-start.8) | collective-permute-done | bytes 147488 | tf_op jit(solution)/shard_map/ppermute | solution.py:940
  33.1 2.9 %collective-permute-done.4.rest_3_ = bf16[96,768]{1,0:T(8,128)(2,1)S(1)} collective-permute-done((bf16[96,768]{1,0:T(8,128)(2,1)S(1)}, bf16[96,768]{1,0:T(8,128)(2,1)S(1)}, u32[]{:S(2)}, u32[]{:S(2)}) %collective-permute-start.4) | collective-permute-done | bytes 147488 | tf_op jit(solution)/shard_map/ppermute | solution.py:940
  40.3 9.4 %qkv.1 = (bf16[2048,768]{1,0:T(8,128)(2,1)}, bf16[576,2048]{1,0:T(8,128)(2,1)}, bf16[2048,192]{1,0:T(8,128)(2,1)}, bf16[2048,192]{1,0:T(8,128)(2,1)}, bf16[576,7...) custom-call(s32[24]{0:T(128)} %concatenate.18.sc, bf16[512,768]{1,0:T(8,128)(2,1)} %refs_0_.5, ...), custom_call_target="tpu_custom_call" | custom-call | flops 10000000 | bytes 1024 | tf_op jit(solution)/shard_map/qkv/pallas_call | solution.py:88
  51.2 1.7 copy-done
  54.1 7.8 %attention.2 = (bf16[192,1024]{1,0:T(8,128)(2,1)S(1)}, f32[8,1024]{1,0:T(8,128)S(1)}) custom-call(s32[24]{0:T(128)S(1)} %copy-done.33, bf16[576,2048]{1,0:T(8,128)(2,1)S(1)} %copy-done, bf16[2048,192]{1,0:T(8,128)(2,1)S(1)} %copy-done.16, bf16[576,2048]{1,0:T(8,128)(2,1)S(1)} %copy-done, s32[1,2048]{1,0:T(1,128)S(1)} %copy-done.26, ...), custom_call_target="tpu_custom_call" | custom-call | flops 12000000000 | bytes 1024 | tf_op jit(solution)/shard_map/attention/pallas_call | solution.py:207
  62.0 2.8 %collective-permute-done.11.wx = bf16[192,768]{1,0:T(8,128)(2,1)S(1)} collective-permute-done((bf16[192,768]{1,0:T(8,128)(2,1)}, bf16[192,768]{1,0:T(8,128)(2,1)S(1)}, u32[]{:S(2)}, u32[]{:S(2)}) %collective-permute-start.11) | collective-permute-done | bytes 294944 | tf_op jit(solution)/shard_map/ppermute | solution.py:934
  66.2 6.9 %attention.3 = (bf16[192,1024]{1,0:T(8,128)(2,1)S(1)}, f32[8,1024]{1,0:T(8,128)S(1)}) custom-call(s32[24]{0:T(128)S(1)} %copy-done.33, bf16[576,2048]{1,0:T(8,128)(2,1)S(1)} %copy-done, bf16[2048,192]{1,0:T(8,128)(2,1)S(1)} %copy-done.16, bf16[576,2048]{1,0:T(8,128)(2,1)S(1)} %copy-done, s32[1,2048]{1,0:T(1,128)S(1)} %copy-done.26, ...), custom_call_target="tpu_custom_call" | custom-call | flops 12000000000 | bytes 1024 | tf_op jit(solution)/shard_map/attention/pallas_call | solution.py:207
  74.9 2.1 out_projection.1
  77.6 1.9 collective-permute-done.13.refs_2_
  79.5 2.4 %middle.1 = (f32[512,768]{1,0:T(8,128)S(1)}, bf16[512,768]{1,0:T(8,128)(2,1)S(1)}, bf16[256,768]{1,0:T(8,128)(2,1)}, bf16[256,768]{1,0:T(8,128)(2,1)S(1)}) custom-call(bf16[512,768]{1,0:T(8,128)(2,1)S(1)} %copy-done.2, bf16[512,768]{1,0:T(8,128)(2,1)S(1)} %get-tuple-element.113.refs_1_, bf16[512,768]{1,0:T(8,128)(2,1)S(1)} %collective-permute-done.13.refs_2_, ...), custom_call_target="tpu_custom_call" | custom-call | flops 10000000 | bytes 1024 | tf_op jit(solution)/shard_map/middle/pallas_call | solution.py:498
  86.0 3.9 %all-gather.2.cloned.1.call-done.w = bf16[768,1536]{1,0:T(8,128)(2,1)} async-done(((bf16[96,1536]{1,0:T(8,128)(2,1)}), bf16[768,1536]{1,0:T(8,128)(2,1)}) %all-gather.2.cloned.1.call-update) | async-done | bytes 2359312 | tf_op jit(solution)/shard_map/all_gather | solution.py:975
  90.0 10.2 %mlp.3 = (bf16[512,768]{1,0:T(8,128)(2,1)}, bf16[512,768]{1,0:T(8,128)(2,1)}, bf16[512,768]{1,0:T(8,128)(2,1)}, bf16[512,768]{1,0:T(8,128)(2,1)}, bf16[1024,512]{1,0:T(8,128)(2,1)}, /*index=5*/bf16[1024,1024]{1,0:T(8,128)(2,1)}) custom-call(bf16[512,768]{1,0:T(8,128)(2,1)} %copy-done.38, bf16[512,768]{1,0:T(8,128)(2,1)} %collective-permute-done.14.nb.refs_1_, ...), custom_call_target="tpu_custom_call" | custom-call | flops 8000000000 | bytes 1024 | tf_op jit(solution)/shard_map/mlp/pallas_call | solution.py:649
  102.0 1.7 copy-done.35
  103.7 6.3 %mlp.4 = (bf16[512,768]{1,0:T(8,128)(2,1)S(1)}, bf16[512,768]{1,0:T(8,128)(2,1)}, bf16[256,768]{1,0:T(8,128)(2,1)S(1)}, bf16[256,768]{1,0:T(8,128)(2,1)S(1)}, bf...) custom-call(bf16[256,768]{1,0:T(8,128)(2,1)S(1)} %collective-permute-done.17.na.refs_2_, ...), custom_call_target="tpu_custom_call" | custom-call | flops 8000000000 | bytes 1024 | tf_op jit(solution)/shard_map/mlp/pallas_call | solution.py:649
  113.5 6.3 %mlp.5 = (bf16[512,768]{1,0:T(8,128)(2,1)S(1)}, bf16[512,768]{1,0:T(8,128)(2,1)}, bf16[256,768]{1,0:T(8,128)(2,1)S(1)}, bf16[256,768]{1,0:T(8,128)(2,1)S(1)}, bf...) custom-call(bf16[256,768]{1,0:T(8,128)(2,1)S(1)} %collective-permute-done., ...), custom_call_target="tpu_custom_call", output_to_operand_aliasing={{0}: (5, {}), {1}: (6, {})} | custom-call | flops 8000000000 | bytes 1024 | tf_op jit(solution)/shard_map/mlp/pallas_call | solution.py:649
  120.8 2.7 %collective-permute-done.22.refs_4_ = bf16[256,768]{1,0:T(8,128)(2,1)S(1)} collective-permute-done((bf16[256,768]{1,0:T(8,128)(2,1)S(1)}, bf16[256,768]{1,0:T(8,128)(2,1)S(1)}, u32[]{:S(2)}, u32[]{:S(2)}) %collective-permute-start.22) | collective-permute-done | bytes 393248 | tf_op jit(solution)/shard_map/ppermute | solution.py:934
  124.0 1.7 collective-permute-done.23
  128.6 9.5 %mlp_weights.1 = bf16[768,1536]{1,0:T(8,128)(2,1)} custom-call(bf16[512,768]{1,0:T(8,128)(2,1)S(1)} %copy-done.39, bf16[512,768]{1,0:T(8,128)(2,1)} %collective-permute-done.14.nb.refs_1_, bf16[256,768]{1,0:T(8,128)(2,1)S(1)} %copy-done.41, bf16[256,768]{1,0:T(8,128)(2,1)S(1)} %collective-permute-done.18.nb.refs_3_, ...), custom_call_target="tpu_custom_call" | custom-call | flops 10000000000 | bytes 1024 | tf_op jit(solution)/shard_map/mlp_weights/pallas_call | solution.py:736
  138.2 3.3 %middle_back.1 = (f32[512,768]{1,0:T(8,128)S(1)}, bf16[512,768]{1,0:T(8,128)(2,1)}, f32[32,768]{1,0:T(8,128)S(1)}) custom-call(bf16[512,768]{1,0:T(8,128)(2,1)} %refs_0_.4, f32[512,768]{1,0:T(8,128)S(1)} %get-tuple-element.115.refs_1_, bf16[512,768]{1,0:T(8,128)(2,1)S(1)} %copy-done.17, bf16[512,768]{1,0:T(8,128)(2,1)} %collective-permute-done.25.refs_3_, ...), custom_call_target="tpu_custom_call" | custom-call | flops 10000000 | bytes 1024 | tf_op jit(solution)/shard_map/middle_back/pallas_call | solution.py:498
  144.5 2.2 add_convert_fusion.2
  146.7 4.1 %out_back.1 = (bf16[192,1024]{1,0:T(8,128)(2,1)S(1)}, bf16[192,1024]{1,0:T(8,128)(2,1)}, f32[192,768]{1,0:T(8,128)S(1)}, bf16[192,768]{1,0:T(8,128)(2,1)}) custom-call(bf16[512,768]{1,0:T(8,128)(2,1)} %get-tuple-element.147.own, bf16[512,768]{1,0:T(8,128)(2,1)} %collective-permute-done.28.other, bf16[192,768]{1,0:T(8,128)(2,1)S(1)} %copy-done.13, ...), custom_call_target="tpu_custom_call" | custom-call | flops 10000000 | bytes 1024 | tf_op jit(solution)/shard_map/out_back/pallas_call | solution.py:818
  155.0 14.6 %attention_back.1 = (bf16[192,1024]{1,0:T(8,128)(2,1)}, f32[192,2048]{1,0:T(8,128)}, f32[192,2048]{1,0:T(8,128)}) custom-call(s32[24]{0:T(128)} %concatenate.18.sc, bf16[576,2048]{1,0:T(8,128)(2,1)} %get-tuple-element.105.qt.vt.kt, bf16[2048,192]{1,0:T(8,128)(2,1)} %get-tuple-element.106.kn, bf16[576,2048]{1,0:T(8,128)(2,1)} %get-tuple-element.105.qt.vt.kt, ...), custom_call_target="tpu_custom_call" | custom-call | flops 20000000000 | bytes 1024 | tf_op jit(solution)/shard_map/attention_back/pallas_call | solution.py:375
  172.1 19.1 %attention_back_end.1 = (bf16[512,768]{1,0:T(8,128)(2,1)S(1)}, bf16[512,768]{1,0:T(8,128)(2,1)S(1)}, bf16[192,1024]{1,0:T(8,128)(2,1)S(1)}, bf16[192,1024]{1,0:T...) custom-call(s32[24]{0:T(128)S(1)} %copy-done.34, ...), custom_call_target="tpu_custom_call" | custom-call | flops 10000000 | bytes 1024 | tf_op jit(solution)/shard_map/attention_back_end/pallas_call | solution.py:401
  191.5 2.0 collective-permute-start.39
  194.8 9.7 %collective-permute-done.39 = bf16[104,768]{1,0:T(8,128)(2,1)S(1)} collective-permute-done((bf16[104,768]{1,0:T(8,128)(2,1)S(1)}, bf16[104,768]{1,0:T(8,128)(2,1)S(1)}, u32[]{:S(2)}, u32[]{:S(2)}) %collective-permute-start.39) | collective-permute-done | bytes 159776 | tf_op jit(solution)/shard_map/ppermute | solution.py:940
  205.3 7.1 %collective-permute-start.41 = (bf16[104,768]{1,0:T(8,128)(2,1)}, bf16[104,768]{1,0:T(8,128)(2,1)S(1)}, u32[]{:S(2)}, u32[]{:S(2)}) collective-permute-start(bf16[104,768]{1,0:T(8,128)(2,1)} %pad_maximum_fusion), channel_id=1, source_target_pairs={{0,24},{4,28},{8,16},{12,20},{16,8},{20,12},{24,0},{28,4},{1,25},{... | collective-permute-start | bytes 479240 | tf_op jit(solution)/shard_map/ppermute | solution.py:940
  213.0 1.9 rows_back.1
  215.8 2.7 %add_convert_fusion = bf16[512,768]{1,0:T(8,128)(2,1)} fusion(f32[512,768]{1,0:T(8,128)S(1)} %get-tuple-element.115.refs_1_, bf16[512,768]{1,0:T(8,128)(2,1)} %collective-permute-done.29, bf16[512,768]{1,0:T(8,128)(2,1)} %collective-permute-done.24, bf16[512,768]{1,0:T(8,128)(2,1)S(1)} %copy-done.48), kind=kLoop, calls=%fused_computation | loop fusion | flops 2752512 | bytes 4718592 | tf_op jit(solution)/shard_map/convert_element_type | solution.py:1052
  222.1 1.8 slice_convert_fusion
  226.2 3.4 %last.1 = bf16[512,768]{1,0:T(8,128)(2,1)} custom-call(bf16[512,768]{1,0:T(8,128)(2,1)S(1)} %copy-done.2, f32[512,768]{1,0:T(8,128)S(1)} %copy-done.6, bf16[512,768]{1,0:T(8,128)(2,1)S(1)} %copy-done.21, bf16[512,768]{1,0:T(8,128)(2,1)S(1)} %copy-done.23, bf16[512,768]{1,0:T(8,128)(2,1)S(1)} %collective-permute-done.34.refs_4_, f32[1,768]{1,0:T(1,128)S(1)} %copy-done.30), custom_call_target="tpu_custom_call" | custom-call | flops 10000000 | bytes 1024 | tf_op jit(solution)/shard_map/last/pallas_call | solution.py:498
  229.6 1.9 grads_sum.1
  (237 shorter events, 65.5 us)
Async XLA Ops:
  7.2 82.8 %all-gather.2.cloned.1.call-start = ((), (), s32[]{:S(2)}) async-start(), calls=%async_computation.1 | async-start | bytes 2654208 | tf_op jit(solution)/shard_map/all_gather | solution.py:975
  8.3 17.9 %collective-permute-start.7 = (bf16[96,768]{1,0:T(8,128)(2,1)S(1)}, bf16[96,768]{1,0:T(8,128)(2,1)S(1)}, u32[]{:S(2)}, u32[]{:S(2)}) collective-permute-start(bf16[96,768]{1,0:T(8,128)(2,1)S(1)} %pad_maximum_fusion.3.rest_0_), channel_id=1, source_target_pairs={{0,24},{4,28},{8,16},{12,20},{16,8},{20,12},{24,0},{28,4},{1,25},{... | collective-permute-start | bytes 442376 | tf_op jit(solution)/shard_map/ppermute | solution.py:940
  13.4 12.5 %collective-permute-start.5 = (bf16[96,768]{1,0:T(8,128)(2,1)S(1)}, bf16[96,768]{1,0:T(8,128)(2,1)S(1)}, u32[]{:S(2)}, u32[]{:S(2)}) collective-permute-start(bf16[96,768]{1,0:T(8,128)(2,1)S(1)} %pad_maximum_fusion.3.rest_0_), channel_id=1, source_target_pairs={{0,16},{4,20},{8,24},{12,28},{16,0},{20,4},{24,8},{28,12},{1,17},{... | collective-permute-start | bytes 442376 | tf_op jit(solution)/shard_map/ppermute | solution.py:940
  13.4 14.4 %collective-permute-start.3 = (bf16[96,768]{1,0:T(8,128)(2,1)S(1)}, bf16[96,768]{1,0:T(8,128)(2,1)S(1)}, u32[]{:S(2)}, u32[]{:S(2)}) collective-permute-start(bf16[96,768]{1,0:T(8,128)(2,1)S(1)} %pad_maximum_fusion.3.rest_0_), channel_id=1, source_target_pairs={{0,8},{4,12},{8,0},{12,4},{16,24},{20,28},{24,16},{28,20},{1,9},{5... | collective-permute-start | bytes 442376 | tf_op jit(solution)/shard_map/ppermute | solution.py:940
  14.1 15.8 %collective-permute-start = (bf16[96,768]{1,0:T(8,128)(2,1)S(1)}, bf16[96,768]{1,0:T(8,128)(2,1)S(1)}, u32[]{:S(2)}, u32[]{:S(2)}) collective-permute-start(bf16[96,768]{1,0:T(8,128)(2,1)S(1)} %pad_maximum_fusion.3.rest_0_), channel_id=1, source_target_pairs={{0,4},{4,0},{8,12},{12,8},{16,20},{20,16},{24,28},{28,24},{1,5},{5... | collective-permute-start | bytes 442376 | tf_op jit(solution)/shard_map/ppermute | solution.py:940
  15.7 21.8 %collective-permute-start.2 = (bf16[512,768]{1,0:T(8,128)(2,1)}, bf16[512,768]{1,0:T(8,128)(2,1)}, u32[]{:S(2)}, u32[]{:S(2)}) collective-permute-start(bf16[512,768]{1,0:T(8,128)(2,1)} %refs_0_.5), channel_id=1, source_target_pairs={{0,2},{1,3},{2,0},{3,1},{4,6},{5,7},{6,4},{7,5},{8,10},{9,11},{10,... | collective-permute-start | bytes 2359304 | tf_op jit(solution)/shard_map/ppermute | solution.py:934
  27.8 8.1 %collective-permute-start.4 = (bf16[96,768]{1,0:T(8,128)(2,1)S(1)}, bf16[96,768]{1,0:T(8,128)(2,1)S(1)}, u32[]{:S(2)}, u32[]{:S(2)}) collective-permute-start(bf16[96,768]{1,0:T(8,128)(2,1)S(1)} %collective-permute-done.3.rest_2_), channel_id=1, source_target_pairs={{0,4},{4,0},{8,12},{12,8},{16,20},{20,16},{24,28},{28,24},{1,5},{5... | collective-permute-start | bytes 442376 | tf_op jit(solution)/shard_map/ppermute | solution.py:940
  28.4 9.2 %collective-permute-start.6 = (bf16[96,768]{1,0:T(8,128)(2,1)S(1)}, bf16[96,768]{1,0:T(8,128)(2,1)S(1)}, u32[]{:S(2)}, u32[]{:S(2)}) collective-permute-start(bf16[96,768]{1,0:T(8,128)(2,1)S(1)} %collective-permute-done.5.rest_4_), channel_id=1, source_target_pairs={{0,4},{4,0},{8,12},{12,8},{16,20},{20,16},{24,28},{28,24},{1,5},{5... | collective-permute-start | bytes 442376 | tf_op jit(solution)/shard_map/ppermute | solution.py:940
  29.9 10.4 %collective-permute-start.1 = (bf16[512,768]{1,0:T(8,128)(2,1)S(1)}, bf16[512,768]{1,0:T(8,128)(2,1)}, u32[]{:S(2)}, u32[]{:S(2)}) collective-permute-start(bf16[512,768]{1,0:T(8,128)(2,1)S(1)} %copy-done.1), channel_id=1, source_target_pairs={{0,1},{1,0},{2,3},{3,2},{4,5},{5,4},{6,7},{7,6},{8,9},{9,8},{10,11... | collective-permute-start | bytes 2359304 | tf_op jit(solution)/shard_map/ppermute | solution.py:931
  37.6 184.5 %reduce-scatter.2.cloned.1.call-start = ((), (), s32[]{:S(2)}) async-start(), calls=%async_computation.2 | async-start | bytes 2654208 | tf_op jit(solution)/shard_map/reduce_scatter | solution.py:1012
  38.8 23.2 %collective-permute-start.10 = (bf16[512,768]{1,0:T(8,128)(2,1)}, bf16[512,768]{1,0:T(8,128)(2,1)S(1)}, u32[]{:S(2)}, u32[]{:S(2)}) collective-permute-start(bf16[512,768]{1,0:T(8,128)(2,1)} %refs_0_.4), channel_id=1, source_target_pairs={{0,2},{1,3},{2,0},{3,1},{4,6},{5,7},{6,4},{7,5},{8,10},{9,11},{10,... | collective-permute-start | bytes 2359304 | tf_op jit(solution)/shard_map/ppermute | solution.py:934
  49.8 15.0 %collective-permute-start.11 = (bf16[192,768]{1,0:T(8,128)(2,1)}, bf16[192,768]{1,0:T(8,128)(2,1)S(1)}, u32[]{:S(2)}, u32[]{:S(2)}) collective-permute-start(bf16[192,768]{1,0:T(8,128)(2,1)} %get-tuple-element.111.wm), channel_id=1, source_target_pairs={{0,2},{1,3},{2,0},{3,1},{4,6},{5,7},{6,4},{7,5},{8,10},{9,11},{10,... | collective-permute-start | bytes 884744 | tf_op jit(solution)/shard_map/ppermute | solution.py:934
  64.8 10.2 %collective-permute-start.12 = (bf16[192,1024]{1,0:T(8,128)(2,1)S(1)}, bf16[192,1024]{1,0:T(8,128)(2,1)S(1)}, u32[]{:S(2)}, u32[]{:S(2)}) collective-permute-start(bf16[192,1024]{1,0:T(8,128)(2,1)S(1)} %get-tuple-element.112.ot), channel_id=1, source_target_pairs={{0,2},{1,3},{2,0},{3,1},{4,6},{5,7},{6,4},{7,5},{8,10},{9,11},{10,... | collective-permute-start | bytes 1179656 | tf_op jit(solution)/shard_map/ppermute | solution.py:934
  77.1 8.5 %collective-permute-start.15 = (bf16[512,768]{1,0:T(8,128)(2,1)}, bf16[512,768]{1,0:T(8,128)(2,1)}, u32[]{:S(2)}, u32[]{:S(2)}) collective-permute-start(bf16[512,768]{1,0:T(8,128)(2,1)} %refs_0_.4), channel_id=1, source_target_pairs={{0,1},{1,0},{2,3},{3,2},{4,5},{5,4},{6,7},{7,6},{8,9},{9,8},{10,11... | collective-permute-start | bytes 2359304 | tf_op jit(solution)/shard_map/ppermute | solution.py:931
  83.7 18.1 %collective-permute-start.19 = (bf16[512,768]{1,0:T(8,128)(2,1)S(1)}, bf16[512,768]{1,0:T(8,128)(2,1)}, u32[]{:S(2)}, u32[]{:S(2)}) collective-permute-start(bf16[512,768]{1,0:T(8,128)(2,1)S(1)} %copy-done.37), channel_id=1, source_target_pairs={{0,1},{1,0},{2,3},{3,2},{4,5},{5,4},{6,7},{7,6},{8,9},{9,8},{10,11... | collective-permute-start | bytes 2359304 | tf_op jit(solution)/shard_map/ppermute | solution.py:931
  84.1 16.1 %collective-permute-start.17 = (bf16[256,768]{1,0:T(8,128)(2,1)}, bf16[256,768]{1,0:T(8,128)(2,1)S(1)}, u32[]{:S(2)}, u32[]{:S(2)}) collective-permute-start(bf16[256,768]{1,0:T(8,128)(2,1)} %get-tuple-element.121), channel_id=1, source_target_pairs={{0,2},{1,3},{2,0},{3,1},{4,6},{5,7},{6,4},{7,5},{8,10},{9,11},{10,... | collective-permute-start | bytes 1179656 | tf_op jit(solution)/shard_map/ppermute | solution.py:934
  100.3 11.5 %collective-permute-start.16 = (bf16[256,768]{1,0:T(8,128)(2,1)S(1)}, bf16[256,768]{1,0:T(8,128)(2,1)S(1)}, u32[]{:S(2)}, u32[]{:S(2)}) collective-permute-start(bf16[256,768]{1,0:T(8,128)(2,1)S(1)} %copy-done.43), channel_id=1, source_target_pairs={{0,2},{1,3},{2,0},{3,1},{4,6},{5,7},{6,4},{7,5},{8,10},{9,11},{10,... | collective-permute-start | bytes 1179656 | tf_op jit(solution)/shard_map/ppermute | solution.py:934
  111.9 11.6 %collective-permute-start.22 = (bf16[256,768]{1,0:T(8,128)(2,1)S(1)}, bf16[256,768]{1,0:T(8,128)(2,1)S(1)}, u32[]{:S(2)}, u32[]{:S(2)}) collective-permute-start(bf16[256,768]{1,0:T(8,128)(2,1)S(1)} %add_convert_fusion.4), channel_id=1, source_target_pairs={{0,2},{1,3},{2,0},{3,1},{4,6},{5,7},{6,4},{7,5},{8,10},{9,11},{10,... | collective-permute-start | bytes 1179656 | tf_op jit(solution)/shard_map/ppermute | solution.py:934
  123.5 14.6 %collective-permute-start.27 = (bf16[512,768]{1,0:T(8,128)(2,1)}, bf16[512,768]{1,0:T(8,128)(2,1)}, u32[]{:S(2)}, u32[]{:S(2)}) collective-permute-start(bf16[512,768]{1,0:T(8,128)(2,1)} %get-tuple-element.145), channel_id=1, source_target_pairs={{0,1},{1,0},{2,3},{3,2},{4,5},{5,4},{6,7},{7,6},{8,9},{9,8},{10,11... | collective-permute-start | bytes 2359304 | tf_op jit(solution)/shard_map/ppermute | solution.py:931
  126.6 11.6 %collective-permute-start.26 = (bf16[256,768]{1,0:T(8,128)(2,1)}, bf16[256,768]{1,0:T(8,128)(2,1)}, u32[]{:S(2)}, u32[]{:S(2)}) collective-permute-start(bf16[256,768]{1,0:T(8,128)(2,1)} %add_convert_fusion.3), channel_id=1, source_target_pairs={{0,2},{1,3},{2,0},{3,1},{4,6},{5,7},{6,4},{7,5},{8,10},{9,11},{10,... | collective-permute-start | bytes 1179656 | tf_op jit(solution)/shard_map/ppermute | solution.py:934
  128.1 10.1 %collective-permute-start.24 = (bf16[512,768]{1,0:T(8,128)(2,1)}, bf16[512,768]{1,0:T(8,128)(2,1)}, u32[]{:S(2)}, u32[]{:S(2)}) collective-permute-start(bf16[512,768]{1,0:T(8,128)(2,1)} %get-tuple-element.134), channel_id=1, source_target_pairs={{0,1},{1,0},{2,3},{3,2},{4,5},{5,4},{6,7},{7,6},{8,9},{9,8},{10,11... | collective-permute-start | bytes 2359304 | tf_op jit(solution)/shard_map/ppermute | solution.py:931
  128.1 10.1 %collective-permute-start.25 = (bf16[512,768]{1,0:T(8,128)(2,1)}, bf16[512,768]{1,0:T(8,128)(2,1)}, u32[]{:S(2)}, u32[]{:S(2)}) collective-permute-start(bf16[512,768]{1,0:T(8,128)(2,1)} %get-tuple-element.137), channel_id=1, source_target_pairs={{0,1},{1,0},{2,3},{3,2},{4,5},{5,4},{6,7},{7,6},{8,9},{9,8},{10,11... | collective-permute-start | bytes 2359304 | tf_op jit(solution)/shard_map/ppermute | solution.py:931
  151.6 18.6 %collective-permute-start.30 = (bf16[192,1024]{1,0:T(8,128)(2,1)}, bf16[192,1024]{1,0:T(8,128)(2,1)}, u32[]{:S(2)}, u32[]{:S(2)}) collective-permute-start(bf16[192,1024]{1,0:T(8,128)(2,1)} %get-tuple-element.149), channel_id=1, source_target_pairs={{0,2},{1,3},{2,0},{3,1},{4,6},{5,7},{6,4},{7,5},{8,10},{9,11},{10,... | collective-permute-start | bytes 1179656 | tf_op jit(solution)/shard_map/ppermute | solution.py:934
  152.9 17.2 %collective-permute-start.31 = (bf16[192,768]{1,0:T(8,128)(2,1)}, bf16[192,768]{1,0:T(8,128)(2,1)}, u32[]{:S(2)}, u32[]{:S(2)}) collective-permute-start(bf16[192,768]{1,0:T(8,128)(2,1)} %get-tuple-element.159), channel_id=1, source_target_pairs={{0,2},{1,3},{2,0},{3,1},{4,6},{5,7},{6,4},{7,5},{8,10},{9,11},{10,... | collective-permute-start | bytes 884744 | tf_op jit(solution)/shard_map/ppermute | solution.py:934
  153.6 37.6 %collective-permute-start.29 = (bf16[512,768]{1,0:T(8,128)(2,1)}, bf16[512,768]{1,0:T(8,128)(2,1)}, u32[]{:S(2)}, u32[]{:S(2)}) collective-permute-start(bf16[512,768]{1,0:T(8,128)(2,1)} %add_convert_fusion.2), channel_id=1, source_target_pairs={{0,2},{1,3},{2,0},{3,1},{4,6},{5,7},{6,4},{7,5},{8,10},{9,11},{10,... | collective-permute-start | bytes 2359304 | tf_op jit(solution)/shard_map/ppermute | solution.py:934
  191.4 13.2 %collective-permute-start.35 = (bf16[104,768]{1,0:T(8,128)(2,1)S(1)}, bf16[104,768]{1,0:T(8,128)(2,1)S(1)}, u32[]{:S(2)}, u32[]{:S(2)}) collective-permute-start(bf16[104,768]{1,0:T(8,128)(2,1)S(1)} %get-tuple-element.180), channel_id=1, source_target_pairs={{0,4},{4,0},{8,12},{12,8},{16,20},{20,16},{24,28},{28,24},{1,5},{5... | collective-permute-start | bytes 479240 | tf_op jit(solution)/shard_map/ppermute | solution.py:940
  191.5 13.1 %collective-permute-start.39 = (bf16[104,768]{1,0:T(8,128)(2,1)S(1)}, bf16[104,768]{1,0:T(8,128)(2,1)S(1)}, u32[]{:S(2)}, u32[]{:S(2)}) collective-permute-start(bf16[104,768]{1,0:T(8,128)(2,1)S(1)} %get-tuple-element.186), channel_id=1, source_target_pairs={{0,4},{4,0},{8,12},{12,8},{16,20},{20,16},{24,28},{28,24},{1,5},{5... | collective-permute-start | bytes 479240 | tf_op jit(solution)/shard_map/ppermute | solution.py:940
  194.7 29.2 %collective-permute-start.34 = (bf16[512,768]{1,0:T(8,128)(2,1)}, bf16[512,768]{1,0:T(8,128)(2,1)S(1)}, u32[]{:S(2)}, u32[]{:S(2)}) collective-permute-start(bf16[512,768]{1,0:T(8,128)(2,1)} %add_convert_fusion.1), channel_id=1, source_target_pairs={{0,2},{1,3},{2,0},{3,1},{4,6},{5,7},{6,4},{7,5},{8,10},{9,11},{10,... | collective-permute-start | bytes 2359304 | tf_op jit(solution)/shard_map/ppermute | solution.py:934
  205.3 24.3 %collective-permute-start.41 = (bf16[104,768]{1,0:T(8,128)(2,1)}, bf16[104,768]{1,0:T(8,128)(2,1)S(1)}, u32[]{:S(2)}, u32[]{:S(2)}) collective-permute-start(bf16[104,768]{1,0:T(8,128)(2,1)} %pad_maximum_fusion), channel_id=1, source_target_pairs={{0,24},{4,28},{8,16},{12,20},{16,8},{20,12},{24,0},{28,4},{1,25},{... | collective-permute-start | bytes 479240 | tf_op jit(solution)/shard_map/ppermute | solution.py:940
  215.8 13.8 %collective-permute-start.40 = (bf16[104,768]{1,0:T(8,128)(2,1)}, bf16[104,768]{1,0:T(8,128)(2,1)}, u32[]{:S(2)}, u32[]{:S(2)}) collective-permute-start(bf16[104,768]{1,0:T(8,128)(2,1)} %pad_maximum_fusion.2), channel_id=1, source_target_pairs={{0,16},{4,20},{8,24},{12,28},{16,0},{20,4},{24,8},{28,12},{1,17},{... | collective-permute-start | bytes 479240 | tf_op jit(solution)/shard_map/ppermute | solution.py:940
  219.2 10.4 %collective-permute-start.38 = (bf16[104,768]{1,0:T(8,128)(2,1)}, bf16[104,768]{1,0:T(8,128)(2,1)}, u32[]{:S(2)}, u32[]{:S(2)}) collective-permute-start(bf16[104,768]{1,0:T(8,128)(2,1)} %pad_maximum_fusion.1), channel_id=1, source_target_pairs={{0,8},{4,12},{8,0},{12,4},{16,24},{20,28},{24,16},{28,20},{1,9},{5... | collective-permute-start | bytes 479240 | tf_op jit(solution)/shard_map/ppermute | solution.py:940
  220.7 9.0 %collective-permute-start.37 = (bf16[104,768]{1,0:T(8,128)(2,1)}, bf16[104,768]{1,0:T(8,128)(2,1)}, u32[]{:S(2)}, u32[]{:S(2)}) collective-permute-start(bf16[104,768]{1,0:T(8,128)(2,1)} %get-tuple-element.184), channel_id=1, source_target_pairs={{0,4},{4,0},{8,12},{12,8},{16,20},{20,16},{24,28},{28,24},{1,5},{5... | collective-permute-start | bytes 479240 | tf_op jit(solution)/shard_map/ppermute | solution.py:940
  (75 other events, 592.1 us)
Sparse Core Ops, SparseCore 0:
  37.7 52.1 all-gather.1
  143.5 69.9 reduce-scatter.1
